TPU v7x, 32 devices: a whole 2x2x4 slice. The times are simulated.
32 devices in a mesh: group: 2 (over y), gx: 4 (over x, core), gy: 4 (over z).
Axes of the slice: x: 2, y: 2, z: 4, core: 2. Of those that a mesh axis runs over, the one named last changes fastest.
Arguments:
- pressure: float32 [192, 64, 768], P(('group', 'gx'), 'gy'), parts along dimension 0, may hold values from -6 to 6
- pressure_prev: float32 [192, 64, 768], P(('group', 'gx'), 'gy'), parts along dimension 0, may hold values from -6 to 6
- courant: float32 [192, 64, 768], P(('group', 'gx'), 'gy'), parts along dimension 0, may hold values from 0.05 to 0.3
- nonlinearity: float32 [192, 64, 768], P(('group', 'gx'), 'gy'), parts along dimension 0, may hold values from 0.03 to 0.3
- absorption: float32 [192, 64, 768], P(('group', 'gx'), 'gy'), parts along dimension 0, may hold values from 0.2 to 2
- own_map: int32 [96, 32], P(('group', 'gx'), 'gy'), parts along dimension 0, may hold values from 0 to 16, as said below
- slot_table: int32 [96, 32], P(('group', 'gx'), 'gy'), parts along dimension 0, may hold values from 0 to 511
- displacement: float32 [128, 128, 384], P(('group', 'gx'), 'gy'), parts along dimension 0, may hold values from -6 to 6
- displacement_prev: float32 [128, 128, 384], P(('group', 'gx'), 'gy'), parts along dimension 0, may hold values from -6 to 6
- layer_labels: int32 [128, 128, 384], P(('group', 'gx'), 'gy'), parts along dimension 0, may hold values from 0 to 3
- shear_table: float32 [8], P('group'), parts along dimension 0, may hold values from 0.05 to 0.15
- viscosity_table: float32 [8], P('group'), parts along dimension 0, may hold values from 0.01 to 0.06
Outputs:
- pressure_mid: float32 [192, 64, 768], P(('group', 'gx'), 'gy'), parts along dimension 0
- pressure_new: float32 [192, 64, 768], P(('group', 'gx'), 'gy'), parts along dimension 0
- tissue_force: float32 [128, 128, 384], P(('group', 'gx'), 'gy'), parts along dimension 0
- displacement_mid: float32 [128, 128, 384], P(('group', 'gx'), 'gy'), parts along dimension 0
- displacement_new: float32 [128, 128, 384], P(('group', 'gx'), 'gy'), parts along dimension 0
There are 2 independent parts, one for each index of `group`. A program takes and returns all parts, laid end to end along the dimension named above; each array names one. Nothing has to cross between parts.
Inputs may be any that keep to these rules, and one draw needn't show every extreme that they name: `own_map`: A value below 16 names tissue block (v // 4, v % 4); 16 marks a line outside the focal zone. Among the lines of one device's block of the map, at most 6 name any one tissue block, and exactly 6 do for some block in every draw.
All inputs are finite; a program needn't handle non-finite values.
Results may differ from a plain program's by a relative error of at most 0.0003.
Values sent between devices are 32-bit elements; how exact they have to be, the bound alone decides.
No kernel may reach another device: no remote copies, remote signals or barrier semaphores. Data moves between devices by JAX's collectives and lax.ppermute only.
A program may use at most 64 MiB of HBM per device.

v0:
```python
import jax
import jax.numpy as jnp
from jax import lax
from jax.sharding import PartitionSpec as P


def extended(x, sides, width):
    for axis, dim in sides:
        size, length = (lax.axis_size(axis), x.shape[dim])
        up = [(i, (i + 1) % size) for i in range(size - 1)]
        down = [(j, i) for i, j in up]
        last = lax.slice_in_dim(x, length - width, length, axis=dim)
        first = lax.slice_in_dim(x, 0, width, axis=dim)
        before = lax.ppermute(last, axis, up)
        after = lax.ppermute(first, axis, down)
        x = jnp.concatenate([before, x, after], axis=dim)
    return x


def laplace_ext(ext):
    centre = ext[1:-1, 1:-1]
    zeros = jnp.zeros(centre.shape[:2] + (1,), centre.dtype)
    upper = jnp.concatenate([centre[:, :, 1:], zeros], axis=2)
    lower = jnp.concatenate([zeros, centre[:, :, :-1]], axis=2)
    total = ext[2:, 1:-1] + ext[:-2, 1:-1] + ext[1:-1, 2:] + ext[1:-1, :-2]
    return total + upper + lower - 6.0 * centre


def wave_update(now_ext, before, courant, nonlinearity, absorption):
    now = now_ext[1:-1, 1:-1]
    return (
        2.0 * now
        - before
        + courant * laplace_ext(now_ext)
        + nonlinearity * (now * now - before * before)
        - 0.1 * absorption * (now - before)
    )


def faces_step(now, before, courant, nonlinearity, absorption):
    now_ext = extended(now, (("gx", 0), ("gy", 1)), 1)
    return wave_update(now_ext, before, courant, nonlinearity, absorption)


def layer_lookup(labels, table):
    result = jnp.zeros(labels.shape, jnp.float32)
    for kind in range(table.shape[0]):
        result = result + jnp.where(labels == kind, table[kind], 0.0)
    return result


def elastic_step(now, before, shear, viscosity, force):
    ext = extended(jnp.stack([now, now - before]), (("gx", 1), ("gy", 2)), 1)
    return (
        2.0 * now
        - before
        + shear * laplace_ext(ext[0])
        + viscosity * laplace_ext(ext[1])
        + 0.25 * force
    )


def local(
    pressure,
    pressure_prev,
    courant,
    nonlinearity,
    absorption,
    own_map,
    slot_table,
    displacement,
    displacement_prev,
    layer_labels,
    shear_table,
    viscosity_table,
):
    depth, across, lateral = pressure.shape
    pressure_mid = faces_step(pressure, pressure_prev, courant, nonlinearity, absorption)
    pressure_new = faces_step(pressure_mid, pressure, courant, nonlinearity, absorption)
    force = (
        0.1
        * absorption
        * (pressure_mid * pressure_mid + pressure_new * pressure_new)
        * lax.rsqrt(courant)
    )
    line_count = depth // 2 * (across // 2)
    paired = force.reshape(depth // 2, 2, across // 2, 2, lateral).sum(axis=(1, 3))
    pairing = (
        jnp.arange(lateral, dtype=jnp.int32)[:, None] // 2
        == jnp.arange(lateral // 2, dtype=jnp.int32)[None, :]
    ).astype(jnp.float32)
    lines = (
        jnp.dot(paired.reshape(line_count, lateral), pairing, precision=lax.Precision.HIGHEST)
        * 0.125
    )
    owners = own_map.reshape(line_count)
    places = slot_table.reshape(line_count)
    rows_grid = lax.axis_size("gx")
    cols_grid = lax.axis_size("gy")
    blocks = rows_grid * cols_grid
    capacity = max(2, line_count // blocks)
    order = jnp.arange(line_count, dtype=jnp.int32)
    same_owner = owners[:, None] == owners[None, :]
    rank = jnp.sum(same_owner & (order[None, :] < order[:, None]), axis=1)
    send_index = owners * capacity + rank
    match = jnp.arange(blocks * capacity, dtype=jnp.int32)[:, None] == send_index[None, :]
    send_lines = jnp.dot(match.astype(jnp.float32), lines, precision=lax.Precision.HIGHEST)
    send_places = jnp.sum(jnp.where(match, places[None, :] + 1, 0), axis=1)
    got_lines, got_places = (
        lax.all_to_all(
            send_lines.reshape(blocks, capacity, lateral // 2),
            ("gx", "gy"),
            split_axis=0,
            concat_axis=0,
            tiled=True,
        ),
        lax.all_to_all(
            send_places.reshape(blocks, capacity),
            ("gx", "gy"),
            split_axis=0,
            concat_axis=0,
            tiled=True,
        ),
    )
    tile_rows, tile_cols, tile_depth = displacement.shape
    got_lines = got_lines.reshape(blocks * capacity, tile_depth)
    got_places = got_places.reshape(blocks * capacity)
    landing = jnp.arange(tile_rows * tile_cols, dtype=jnp.int32)[:, None] == got_places[None, :] - 1
    tissue_force = jnp.dot(
        landing.astype(jnp.float32), got_lines, precision=lax.Precision.HIGHEST
    ).reshape(tile_rows, tile_cols, tile_depth)
    shear = layer_lookup(layer_labels, shear_table)
    viscosity = layer_lookup(layer_labels, viscosity_table)
    displacement_mid = elastic_step(displacement, displacement_prev, shear, viscosity, tissue_force)
    displacement_new = elastic_step(displacement_mid, displacement, shear, viscosity, tissue_force)
    return (pressure_mid, pressure_new, tissue_force, displacement_mid, displacement_new)


def solution(mesh):
    return jax.shard_map(
        local,
        mesh=mesh,
        in_specs=(
            P(("group", "gx"), "gy", None),
            P(("group", "gx"), "gy", None),
            P(("group", "gx"), "gy", None),
            P(("group", "gx"), "gy", None),
            P(("group", "gx"), "gy", None),
            P(("group", "gx"), "gy"),
            P(("group", "gx"), "gy"),
            P(("group", "gx"), "gy", None),
            P(("group", "gx"), "gy", None),
            P(("group", "gx"), "gy", None),
            P("group"),
            P("group"),
        ),
        out_specs=(
            P(("group", "gx"), "gy", None),
            P(("group", "gx"), "gy", None),
            P(("group", "gx"), "gy", None),
            P(("group", "gx"), "gy", None),
            P(("group", "gx"), "gy", None),
        ),
        check_vma=False,
    )
```

profile of v0, /device:TPU:0, one launch (start us, length us, event | category | flops | bytes accessed | tf_op | source)
XLA Modules:
  0.0 124.3 jit_solution(6843285488986913172)
XLA Ops:
  3.4 7.4 %all-to-all-start = ((s32[16,1,6]{2,1,0:T(1,128)}), s32[16,1,6]{2,1,0:T(1,128)S(1)}, u32[]{:S(2)}, u32[]{:S(2)}) async-start(s32[16,1,6]{2,1,0:T(1,128)} %bitcast), calls=%async_computation | async-start | bytes 16384 | tf_op jit(solution)/shard_map/all_to_all | solution.py:117
  13.0 3.2 %collective-permute-start.1 = (f32[1,16,768]{2,0,1:T(1,128)S(1)}, f32[1,16,768]{2,0,1:T(1,128)S(1)}, u32[]{:S(2)}, u32[]{:S(2)}) collective-permute-start(f32[1,16,768]{2,0,1:T(1,128)S(1)} %copy.113), channel_id=1, source_target_pairs={{0,4},{4,8},{8,12},{1,5},{5,9},{9,13},{2,6},{6,10},{10,14},{3,7},{... | collective-permute-start | bytes 147464 | tf_op jit(solution)/shard_map/ppermute | solution.py:14
  17.7 3.7 %collective-permute-start.8 = (f32[2,1,32,384]{3,2,1,0:T(8,128)S(1)}, f32[2,1,32,384]{3,2,1,0:T(8,128)S(1)}, u32[]{:S(2)}, u32[]{:S(2)}) collective-permute-start(f32[2,1,32,384]{3,2,1,0:T(8,128)S(1)} %get-tuple-element.43), channel_id=1, source_target_pairs={{0,4},{4,8},{8,12},{1,5},{5,9},{9,13},{2,6},{6,10},{10,14},{3,7},{... | collective-permute-start | bytes 294920 | tf_op jit(solution)/shard_map/ppermute | solution.py:14
  24.7 1.8 %fusion.61 = (f32[24,16,767]{2,0,1:T(8,128)}, f32[24,16,767]{2,0,1:T(8,128)}) fusion(f32[24,16,768]{2,0,1:T(8,128)S(1)} %copy.109), kind=kLoop, calls=%fused_computation.138 | loop fusion | bytes 4712448 | tf_op jit(solution)/shard_map/slice | solution.py:23
  28.1 4.6 %collective-permute-start.3 = (f32[26,1,768]{2,0,1:T(8,128)S(1)}, f32[26,1,768]{2,0,1:T(8,128)S(1)}, u32[]{:S(2)}, u32[]{:S(2)}) collective-permute-start(f32[26,1,768]{2,0,1:T(8,128)S(1)} %get-tuple-element.48), channel_id=1, source_target_pairs={{0,1},{1,2},{2,3},{4,5},{5,6},{6,7},{8,9},{9,10},{10,11},{12,13},{... | collective-permute-start | bytes 239624 | tf_op jit(solution)/shard_map/ppermute | solution.py:14
  32.8 3.5 %collective-permute-start.10 = (f32[2,18,1,384]{3,2,1,0:T(1,128)S(1)}, f32[2,18,1,384]{3,2,1,0:T(1,128)S(1)}, u32[]{:S(2)}, u32[]{:S(2)}) collective-permute-start(f32[2,18,1,384]{3,2,1,0:T(1,128)S(1)} %get-tuple-element.39), channel_id=1, source_target_pairs={{0,1},{1,2},{2,3},{4,5},{5,6},{6,7},{8,9},{9,10},{10,11},{12,13},{... | collective-permute-start | bytes 165896 | tf_op jit(solution)/shard_map/ppermute | solution.py:14
  37.7 6.1 %fusion.17 = f32[24,16,768]{2,0,1:T(8,128)S(1)} fusion(f32[26,1,768]{2,0,1:T(8,128)S(1)} %collective-permute-done.3, f32[1,16,768]{2,0,1:T(1,128)S(1)} %collective-permute-done, f32[24,16,768]{2,0,1:T(8,128)S(1)} %copy.109, f32[1,16,768]{2,0,1:T(1,128)S(1)} %collective-permute-done.1, f32[26,1,768]{2,0,1:T(8,128)S(1)} %collective-permute-done.2, ...), kind=kLoop, calls=%fused_computation.28 | loop fusion | flops 8257536 | bytes 9692160 | tf_op jit(solution)/shard_map/sub | solution.py:32
  44.3 2.2 %collective-permute-start.5 = (f32[1,16,768]{2,0,1:T(1,128)S(1)}, f32[1,16,768]{2,0,1:T(1,128)S(1)}, u32[]{:S(2)}, u32[]{:S(2)}) collective-permute-start(f32[1,16,768]{2,0,1:T(1,128)S(1)} %get-tuple-element.49), channel_id=1, source_target_pairs={{0,4},{4,8},{8,12},{1,5},{5,9},{9,13},{2,6},{6,10},{10,14},{3,7},{... | collective-permute-start | bytes 147464 | tf_op jit(solution)/shard_map/ppermute | solution.py:14
  48.1 3.3 %collective-permute-done.4 = f32[1,16,768]{2,0,1:T(1,128)S(1)} collective-permute-done((f32[1,16,768]{2,0,1:T(1,128)S(1)}, f32[1,16,768]{2,0,1:T(1,128)S(1)}, u32[]{:S(2)}, u32[]{:S(2)}) %collective-permute-start.4) | collective-permute-done | bytes 49184 | tf_op jit(solution)/shard_map/ppermute | solution.py:15
  52.8 5.3 %collective-permute-start.7 = (f32[26,1,768]{2,0,1:T(8,128)S(1)}, f32[26,1,768]{2,0,1:T(8,128)S(1)}, u32[]{:S(2)}, u32[]{:S(2)}) collective-permute-start(f32[26,1,768]{2,0,1:T(8,128)S(1)} %get-tuple-element.46), channel_id=1, source_target_pairs={{0,1},{1,2},{2,3},{4,5},{5,6},{6,7},{8,9},{9,10},{10,11},{12,13},{... | collective-permute-start | bytes 239624 | tf_op jit(solution)/shard_map/ppermute | solution.py:14
  58.6 1.7 %collective-permute-done.7 = f32[26,1,768]{2,0,1:T(8,128)S(1)} collective-permute-done((f32[26,1,768]{2,0,1:T(8,128)S(1)}, f32[26,1,768]{2,0,1:T(8,128)S(1)}, u32[]{:S(2)}, u32[]{:S(2)}) %collective-permute-start.7) | collective-permute-done | bytes 79904 | tf_op jit(solution)/shard_map/ppermute | solution.py:14
  60.3 5.1 %rsqrt_multiply_fusion = (f32[24,16,768]{2,0,1:T(8,128)}, f32[24,16,768]{2,0,1:T(8,128)}) fusion(f32[24,16,768]{2,0,1:T(8,128)S(1)} %fusion.17, f32[24,16,768]{2,1,0:T(8,128)S(1)} %copy-done.9, f32[24,16,768]{2,1,0:T(8,128)S(1)} %copy-done.10, f32[24,16,768]{2,1,0:T(8,128)S(1)} %copy-done.8, f32[24,16,767]{2,0,1:T(8,128)S(1)} %get-tuple-element.52, ...), kind=kLoop, calls=%fused_computation.40 | loop fusion | flops 9437184 | bytes 10871808 | tf_op jit(solution)/shard_map/mul | solution.py:81
  65.4 2.9 %reshape.115 = f32[12,2,8,2,768]{4,1,0,3,2:T(2,128)} reshape(f32[24,16,768]{2,0,1:T(8,128)} %get-tuple-element.31) | data formatting | bytes 2359296 | tf_op jit(solution)/shard_map/reshape | solution.py:87
  68.3 2.9 %reduce_sum.29 = f32[12,8,768]{2,0,1:T(8,128)} reduce(f32[12,2,8,2,768]{4,1,0,3,2:T(2,128)} %reshape.115, f32[]{:T(128)} %constant.14.clone.1), dimensions={1,3}, to_apply=%region_2.3 | reduce | flops 221184 | bytes 1474564 | tf_op jit(solution)/shard_map/reduce_sum | solution.py:87
  71.2 1.7 %fusion.21 = f32[96,384]{1,0:T(8,128)S(1)} fusion(s32[768]{0:T(1024)S(1)} %add_select_fusion, f32[12,8,768]{2,0,1:T(8,128)} %reduce_sum.29), kind=kOutput, calls=%fused_computation.42 | convolution fusion | flops 340070400 | bytes 445440 | tf_op jit(solution)/shard_map/dot_general | solution.py:93
  73.8 8.3 %all-to-all-start.1 = ((f32[16,6,384]{2,1,0:T(8,128)}), f32[16,6,384]{2,1,0:T(8,128)}, u32[]{:S(2)}, u32[]{:S(2)}) async-start(f32[16,6,384]{2,1,0:T(8,128)} %reshape.117), calls=%async_computation.1 | async-start | bytes 393216 | tf_op jit(solution)/shard_map/all_to_all | solution.py:110
  82.1 2.3 %fusion.65 = (f32[16,32,383]{2,1,0:T(8,128)}, f32[16,32,383]{2,1,0:T(8,128)}, f32[16,32,383]{2,1,0:T(8,128)}, f32[16,32,383]{2,1,0:T(8,128)}) fusion(f32[18,34,384]{2,1,0:T(8,128)S(1)} %get-tuple-element.35, f32[18,34,384]{2,1,0:T(8,128)S(1)} %get-tuple-element.36), kind=kLoop, calls=%fused_computation.142 | loop fusion | bytes 6275072 | tf_op jit(solution)/shard_map/slice | solution.py:23
  84.4 5.8 %all-to-all-done.1 = f32[16,6,384]{2,1,0:T(8,128)} async-done(((f32[16,6,384]{2,1,0:T(8,128)}), f32[16,6,384]{2,1,0:T(8,128)}, u32[]{:S(2)}, u32[]{:S(2)}) %all-to-all-start.1) | async-done | bytes 147488 | tf_op jit(solution)/shard_map/all_to_all | solution.py:110
  92.3 8.6 %subtract_bitcast_fusion = (f32[1,16,32,384]{3,2,1,0:T(8,128)S(1)}, f32[16,32,384]{2,1,0:T(8,128)S(1)}, pred[16,32,384]{2,1,0:T(8,128)(4,1)S(1)}, pred[16,32,384...) fusion(f32[16,32,384]{2,1,0:T(8,128)S(1)} %copy-done.1, ...), kind=kLoop, calls=%fused_computation.85 | loop fusion | flops 8060928 | bytes 16506912 | tf_op jit(solution)/shard_map/stack | solution.py:53
  100.9 2.2 %collective-permute-start.12 = (f32[2,1,32,384]{3,2,1,0:T(8,128)S(1)}, f32[2,1,32,384]{3,2,1,0:T(8,128)S(1)}, u32[]{:S(2)}, u32[]{:S(2)}) collective-permute-start(f32[2,1,32,384]{3,2,1,0:T(8,128)S(1)} %get-tuple-element.41), channel_id=1, source_target_pairs={{0,4},{4,8},{8,12},{1,5},{5,9},{9,13},{2,6},{6,10},{10,14},{3,7},{... | collective-permute-start | bytes 294920 | tf_op jit(solution)/shard_map/ppermute | solution.py:14
  104.4 2.5 %collective-permute-done.13 = f32[2,1,32,384]{3,2,1,0:T(8,128)S(1)} collective-permute-done((f32[2,1,32,384]{3,2,1,0:T(8,128)S(1)}, f32[2,1,32,384]{3,2,1,0:T(8,128)S(1)}, u32[]{:S(2)}, u32[]{:S(2)}) %collective-permute-start.13) | collective-permute-done | bytes 98336 | tf_op jit(solution)/shard_map/ppermute | solution.py:15
  107.0 2.8 %collective-permute-start.14 = (f32[2,18,1,384]{3,2,1,0:T(1,128)S(1)}, f32[2,18,1,384]{3,2,1,0:T(1,128)S(1)}, u32[]{:S(2)}, u32[]{:S(2)}) collective-permute-start(f32[2,18,1,384]{3,2,1,0:T(1,128)S(1)} %get-tuple-element.37), channel_id=1, source_target_pairs={{0,1},{1,2},{2,3},{4,5},{5,6},{6,7},{8,9},{9,10},{10,11},{12,13},{... | collective-permute-start | bytes 165896 | tf_op jit(solution)/shard_map/ppermute | solution.py:14
  113.9 2.0 %collective-permute-done.15 = f32[2,18,1,384]{3,2,1,0:T(1,128)S(1)} collective-permute-done((f32[2,18,1,384]{3,2,1,0:T(1,128)S(1)}, f32[2,18,1,384]{3,2,1,0:T(1,128)S(1)}, u32[]{:S(2)}, u32[]{:S(2)}) %collective-permute-start.15) | collective-permute-done | bytes 55328 | tf_op jit(solution)/shard_map/ppermute | solution.py:15
  117.0 7.3 %fusion.25 = f32[16,32,384]{2,1,0:T(8,128)} fusion(f32[18,34,384]{2,1,0:T(8,128)S(1)} %get-tuple-element.34, f32[18,34,384]{2,1,0:T(8,128)S(1)} %get-tuple-element.33, f32[16,32,383]{2,1,0:T(8,128)S(1)} %get-tuple-element.60, f32[16,32,383]{2,1,0:T(8,128)S(1)} %get-tuple-element.59, f32[16,32,383]{2,1,0:T(8,128)S(1)} %get-tuple-element.58, ...), kind=kLoop, calls=%fused_computation.51 | loop fusion | flops 7077888 | bytes 14934048 | tf_op jit(solution)/shard_map/add | solution.py:55
  (89 shorter events, 26.2 us)
Async XLA Ops:
  3.4 23.1 %all-to-all-start = ((s32[16,1,6]{2,1,0:T(1,128)}), s32[16,1,6]{2,1,0:T(1,128)S(1)}, u32[]{:S(2)}, u32[]{:S(2)}) async-start(s32[16,1,6]{2,1,0:T(1,128)} %bitcast), calls=%async_computation | async-start | bytes 16384 | tf_op jit(solution)/shard_map/all_to_all | solution.py:117
  11.6 15.0 %collective-permute-start = (f32[1,16,768]{2,0,1:T(1,128)S(1)}, f32[1,16,768]{2,0,1:T(1,128)S(1)}, u32[]{:S(2)}, u32[]{:S(2)}) collective-permute-start(f32[1,16,768]{2,0,1:T(1,128)S(1)} %copy.111), channel_id=1, source_target_pairs={{4,0},{8,4},{12,8},{5,1},{9,5},{13,9},{6,2},{10,6},{14,10},{7,3},{... | collective-permute-start | bytes 147464 | tf_op jit(solution)/shard_map/ppermute | solution.py:15
  13.0 13.6 %collective-permute-start.1 = (f32[1,16,768]{2,0,1:T(1,128)S(1)}, f32[1,16,768]{2,0,1:T(1,128)S(1)}, u32[]{:S(2)}, u32[]{:S(2)}) collective-permute-start(f32[1,16,768]{2,0,1:T(1,128)S(1)} %copy.113), channel_id=1, source_target_pairs={{0,4},{4,8},{8,12},{1,5},{5,9},{9,13},{2,6},{6,10},{10,14},{3,7},{... | collective-permute-start | bytes 147464 | tf_op jit(solution)/shard_map/ppermute | solution.py:14
  17.7 15.1 %copy-start.3 = (f32[1,16,32,384]{3,2,1,0:T(8,128)}, f32[1,16,32,384]{3,2,1,0:T(8,128)S(1)}, u32[]{:S(2)}) copy-start(f32[1,16,32,384]{3,2,1,0:T(8,128)S(1)} %subtract_bitcast_fusion.1) | copy-start | bytes 2359300
  17.7 15.0 %collective-permute-start.8 = (f32[2,1,32,384]{3,2,1,0:T(8,128)S(1)}, f32[2,1,32,384]{3,2,1,0:T(8,128)S(1)}, u32[]{:S(2)}, u32[]{:S(2)}) collective-permute-start(f32[2,1,32,384]{3,2,1,0:T(8,128)S(1)} %get-tuple-element.43), channel_id=1, source_target_pairs={{0,4},{4,8},{8,12},{1,5},{5,9},{9,13},{2,6},{6,10},{10,14},{3,7},{... | collective-permute-start | bytes 294920 | tf_op jit(solution)/shard_map/ppermute | solution.py:14
  21.4 11.3 %collective-permute-start.9 = (f32[2,1,32,384]{3,2,1,0:T(8,128)S(1)}, f32[2,1,32,384]{3,2,1,0:T(8,128)S(1)}, u32[]{:S(2)}, u32[]{:S(2)}) collective-permute-start(f32[2,1,32,384]{3,2,1,0:T(8,128)S(1)} %get-tuple-element.44), channel_id=1, source_target_pairs={{4,0},{8,4},{12,8},{5,1},{9,5},{13,9},{6,2},{10,6},{14,10},{7,3},{... | collective-permute-start | bytes 294920 | tf_op jit(solution)/shard_map/ppermute | solution.py:15
  26.6 11.0 %copy-start.9 = (f32[24,16,768]{2,1,0:T(8,128)S(1)}, f32[24,16,768]{2,1,0:T(8,128)}, u32[]{:S(2)}) copy-start(f32[24,16,768]{2,1,0:T(8,128)} %param.14) | copy-start | bytes 3538948
  26.7 11.0 %copy-start.8 = (f32[24,16,768]{2,1,0:T(8,128)S(1)}, f32[24,16,768]{2,1,0:T(8,128)}, u32[]{:S(2)}) copy-start(f32[24,16,768]{2,1,0:T(8,128)} %param.15) | copy-start | bytes 3538948
  26.7 11.0 %collective-permute-start.2 = (f32[26,1,768]{2,0,1:T(8,128)S(1)}, f32[26,1,768]{2,0,1:T(8,128)S(1)}, u32[]{:S(2)}, u32[]{:S(2)}) collective-permute-start(f32[26,1,768]{2,0,1:T(8,128)S(1)} %get-tuple-element.47), channel_id=1, source_target_pairs={{1,0},{2,1},{3,2},{5,4},{6,5},{7,6},{9,8},{10,9},{11,10},{13,12},{... | collective-permute-start | bytes 239624 | tf_op jit(solution)/shard_map/ppermute | solution.py:15
  28.1 9.5 %collective-permute-start.3 = (f32[26,1,768]{2,0,1:T(8,128)S(1)}, f32[26,1,768]{2,0,1:T(8,128)S(1)}, u32[]{:S(2)}, u32[]{:S(2)}) collective-permute-start(f32[26,1,768]{2,0,1:T(8,128)S(1)} %get-tuple-element.48), channel_id=1, source_target_pairs={{0,1},{1,2},{2,3},{4,5},{5,6},{6,7},{8,9},{9,10},{10,11},{12,13},{... | collective-permute-start | bytes 239624 | tf_op jit(solution)/shard_map/ppermute | solution.py:14
  32.8 15.0 %collective-permute-start.10 = (f32[2,18,1,384]{3,2,1,0:T(1,128)S(1)}, f32[2,18,1,384]{3,2,1,0:T(1,128)S(1)}, u32[]{:S(2)}, u32[]{:S(2)}) collective-permute-start(f32[2,18,1,384]{3,2,1,0:T(1,128)S(1)} %get-tuple-element.39), channel_id=1, source_target_pairs={{0,1},{1,2},{2,3},{4,5},{5,6},{6,7},{8,9},{9,10},{10,11},{12,13},{... | collective-permute-start | bytes 165896 | tf_op jit(solution)/shard_map/ppermute | solution.py:14
  36.4 11.4 %collective-permute-start.11 = (f32[2,18,1,384]{3,2,1,0:T(1,128)S(1)}, f32[2,18,1,384]{3,2,1,0:T(1,128)S(1)}, u32[]{:S(2)}, u32[]{:S(2)}) collective-permute-start(f32[2,18,1,384]{3,2,1,0:T(1,128)S(1)} %get-tuple-element.40), channel_id=1, source_target_pairs={{1,0},{2,1},{3,2},{5,4},{6,5},{7,6},{9,8},{10,9},{11,10},{13,12},{... | collective-permute-start | bytes 165896 | tf_op jit(solution)/shard_map/ppermute | solution.py:15
  44.3 3.8 %collective-permute-start.5 = (f32[1,16,768]{2,0,1:T(1,128)S(1)}, f32[1,16,768]{2,0,1:T(1,128)S(1)}, u32[]{:S(2)}, u32[]{:S(2)}) collective-permute-start(f32[1,16,768]{2,0,1:T(1,128)S(1)} %get-tuple-element.49), channel_id=1, source_target_pairs={{0,4},{4,8},{8,12},{1,5},{5,9},{9,13},{2,6},{6,10},{10,14},{3,7},{... | collective-permute-start | bytes 147464 | tf_op jit(solution)/shard_map/ppermute | solution.py:14
  46.5 4.9 %collective-permute-start.4 = (f32[1,16,768]{2,0,1:T(1,128)S(1)}, f32[1,16,768]{2,0,1:T(1,128)S(1)}, u32[]{:S(2)}, u32[]{:S(2)}) collective-permute-start(f32[1,16,768]{2,0,1:T(1,128)S(1)} %get-tuple-element.50), channel_id=1, source_target_pairs={{4,0},{8,4},{12,8},{5,1},{9,5},{13,9},{6,2},{10,6},{14,10},{7,3},{... | collective-permute-start | bytes 147464 | tf_op jit(solution)/shard_map/ppermute | solution.py:15
  51.5 7.1 %collective-permute-start.6 = (f32[26,1,768]{2,0,1:T(8,128)S(1)}, f32[26,1,768]{2,0,1:T(8,128)S(1)}, u32[]{:S(2)}, u32[]{:S(2)}) collective-permute-start(f32[26,1,768]{2,0,1:T(8,128)S(1)} %get-tuple-element.45), channel_id=1, source_target_pairs={{1,0},{2,1},{3,2},{5,4},{6,5},{7,6},{9,8},{10,9},{11,10},{13,12},{... | collective-permute-start | bytes 239624 | tf_op jit(solution)/shard_map/ppermute | solution.py:15
  52.8 7.5 %copy-start.7 = (f32[24,16,768]{2,1,0:T(8,128)S(1)}, f32[24,16,768]{2,1,0:T(8,128)}, u32[]{:S(2)}) copy-start(f32[24,16,768]{2,1,0:T(8,128)} %param.12) | copy-start | bytes 3538948
  52.8 7.5 %collective-permute-start.7 = (f32[26,1,768]{2,0,1:T(8,128)S(1)}, f32[26,1,768]{2,0,1:T(8,128)S(1)}, u32[]{:S(2)}, u32[]{:S(2)}) collective-permute-start(f32[26,1,768]{2,0,1:T(8,128)S(1)} %get-tuple-element.46), channel_id=1, source_target_pairs={{0,1},{1,2},{2,3},{4,5},{5,6},{6,7},{8,9},{9,10},{10,11},{12,13},{... | collective-permute-start | bytes 239624 | tf_op jit(solution)/shard_map/ppermute | solution.py:14
  73.8 16.4 %all-to-all-start.1 = ((f32[16,6,384]{2,1,0:T(8,128)}), f32[16,6,384]{2,1,0:T(8,128)}, u32[]{:S(2)}, u32[]{:S(2)}) async-start(f32[16,6,384]{2,1,0:T(8,128)} %reshape.117), calls=%async_computation.1 | async-start | bytes 393216 | tf_op jit(solution)/shard_map/all_to_all | solution.py:110
  91.7 25.4 %copy-start.5 = (f32[16,32,384]{2,1,0:T(8,128)}, f32[16,32,384]{2,1,0:T(8,128)S(1)}, u32[]{:S(2)}) copy-start(f32[16,32,384]{2,1,0:T(8,128)S(1)} %fusion.47) | copy-start | bytes 2359300
  100.9 16.2 %copy-start.2 = (f32[16,32,384]{2,1,0:T(8,128)}, f32[16,32,384]{2,1,0:T(8,128)S(1)}, u32[]{:S(2)}) copy-start(f32[16,32,384]{2,1,0:T(8,128)S(1)} %get-tuple-element.26) | copy-start | bytes 2359300
  100.9 3.5 %collective-permute-start.12 = (f32[2,1,32,384]{3,2,1,0:T(8,128)S(1)}, f32[2,1,32,384]{3,2,1,0:T(8,128)S(1)}, u32[]{:S(2)}, u32[]{:S(2)}) collective-permute-start(f32[2,1,32,384]{3,2,1,0:T(8,128)S(1)} %get-tuple-element.41), channel_id=1, source_target_pairs={{0,4},{4,8},{8,12},{1,5},{5,9},{9,13},{2,6},{6,10},{10,14},{3,7},{... | collective-permute-start | bytes 294920 | tf_op jit(solution)/shard_map/ppermute | solution.py:14
  103.1 3.8 %collective-permute-start.13 = (f32[2,1,32,384]{3,2,1,0:T(8,128)S(1)}, f32[2,1,32,384]{3,2,1,0:T(8,128)S(1)}, u32[]{:S(2)}, u32[]{:S(2)}) collective-permute-start(f32[2,1,32,384]{3,2,1,0:T(8,128)S(1)} %get-tuple-element.42), channel_id=1, source_target_pairs={{4,0},{8,4},{12,8},{5,1},{9,5},{13,9},{6,2},{10,6},{14,10},{7,3},{... | collective-permute-start | bytes 294920 | tf_op jit(solution)/shard_map/ppermute | solution.py:15
  107.0 7.0 %collective-permute-start.14 = (f32[2,18,1,384]{3,2,1,0:T(1,128)S(1)}, f32[2,18,1,384]{3,2,1,0:T(1,128)S(1)}, u32[]{:S(2)}, u32[]{:S(2)}) collective-permute-start(f32[2,18,1,384]{3,2,1,0:T(1,128)S(1)} %get-tuple-element.37), channel_id=1, source_target_pairs={{0,1},{1,2},{2,3},{4,5},{5,6},{6,7},{8,9},{9,10},{10,11},{12,13},{... | collective-permute-start | bytes 165896 | tf_op jit(solution)/shard_map/ppermute | solution.py:14
  109.8 6.2 %collective-permute-start.15 = (f32[2,18,1,384]{3,2,1,0:T(1,128)S(1)}, f32[2,18,1,384]{3,2,1,0:T(1,128)S(1)}, u32[]{:S(2)}, u32[]{:S(2)}) collective-permute-start(f32[2,18,1,384]{3,2,1,0:T(1,128)S(1)} %get-tuple-element.38), channel_id=1, source_target_pairs={{1,0},{2,1},{3,2},{5,4},{6,5},{7,6},{9,8},{10,9},{11,10},{13,12},{... | collective-permute-start | bytes 165896 | tf_op jit(solution)/shard_map/ppermute | solution.py:15
  (8 other events, 27.3 us)
where the time goes:
time: 127 us; the launch traced here: 124 us
  starting transfers between devices  53.6 us (42%)
  other arithmetic  33.3 us (26%)
  local copies, waits for them, and re-layouts  18.1 us (14%)
  waiting for transfers between devices  15.6 us (12%)
  matrix products  2.46 us (2%)
    ppermute x8, starting transfers between devices, extended(): before = lax.ppermute(last, axis, up)  27.4 us
    ppermute x8, starting transfers between devices, extended(): after = lax.ppermute(first, axis, down)  10.6 us
    another operation x2, other arithmetic, elastic_step(): ext = extended(jnp.stack([now, now - before]), (('gx', 1), ('gy', 2)), 1)  10.1 us
    all_to_all x1, starting transfers between devices, local(): lax.all_to_all(send_lines.reshape(blocks, capacity, lateral // 2), ('gx',...  8.29 us
    ppermute x8, waiting for transfers between devices, extended(): after = lax.ppermute(first, axis, down)  8.15 us
    all_to_all x1, starting transfers between devices, local(): lax.all_to_all(send_places.reshape(blocks, capacity), ('gx', 'gy'), split...  7.39 us
    add x1, other arithmetic, elastic_step(): 2.0 * now - before + shear * laplace_ext(ext[0])  7.28 us
    sub x1, other arithmetic, wave_update(): 2.0 * now - before + courant * laplace_ext(now_ext)  6.11 us
  transfers between devices with their start and end apart: 18, of which 6 were waited for; matrix products, arithmetic and copies ran while one was open for 15% of the time, Pallas kernels for 0%

commit v1 on v0

v1 whole, which is shorter than its diff:
```python
import functools

import jax
import jax.numpy as jnp
from jax import lax
from jax.experimental import pallas as pl
from jax.experimental.pallas import tpu as pltpu
from jax.sharding import PartitionSpec as P

VMEM = pl.BlockSpec(memory_space=pltpu.VMEM)
SMEM = pl.BlockSpec(memory_space=pltpu.SMEM)
EXACT = lax.Precision.HIGHEST


def lateral(x):
    dim, size = x.ndim - 1, x.shape[-1]
    lane = lax.broadcasted_iota(jnp.int32, x.shape, dim)
    lower = jnp.where(lane == 0, 0.0, pltpu.roll(x, 1, dim))
    upper = jnp.where(lane == size - 1, 0.0, pltpu.roll(x, size - 1, dim))
    return lower + upper


def beside(x, before, after):
    size = x.shape[0]
    row = lax.broadcasted_iota(jnp.int32, x.shape, 0)
    up = jnp.where(row == 0, before, pltpu.roll(x, 1, 0))
    down = jnp.where(row == size - 1, after, pltpu.roll(x, size - 1, 0))
    return up + down


def at_ends(shape, first, last):
    row = lax.broadcasted_iota(jnp.int32, shape, 0)
    return jnp.where(row == 0, first, jnp.where(row == shape[0] - 1, last, 0.0))


def wave(now, before, lap, courant, nonlinearity, absorption):
    return (
        2.0 * now
        - before
        + courant * lap
        + nonlinearity * (now * now - before * before)
        - 0.1 * absorption * (now - before)
    )


def lookup(kinds, table, first):
    result = jnp.zeros(kinds.shape, jnp.float32)
    for kind in range(table.shape[0]):
        result = jnp.where(kinds == kind + first, table[kind], result)
    return result


def halves(ref, base, x):
    half, depth = x.shape[0] // 2, x.shape[1]
    ref[base : base + half, 0:depth] = x[:half]
    ref[base : base + half, depth : 2 * depth] = x[half:]


def whole(ref, base, half, depth):
    return jnp.concatenate(
        [ref[base : base + half, 0:depth], ref[base : base + half, depth : 2 * depth]], axis=0
    )


def border_rows(*refs):
    fields, (shear, viscosity, first, last), buffers, sems = refs[:8], refs[8:12], refs[12:28], refs[28]
    copies = []
    for k, buffer in enumerate(buffers):
        field, count = fields[k // 2], buffer.shape[0]
        start = 0 if k % 2 == 0 else field.shape[0] - count
        copies.append(
            pltpu.make_async_copy(field.at[pl.ds(start, count)], buffer, sems.at[k])
        )
    for copy in copies:
        copy.start()
    for copy in copies:
        copy.wait()
    p0, p1, q0, q1, c0, c1, n0, n1, a0, a1, d0, d1, e0, e1, l0, l1 = buffers
    sides = (
        (p0, 0, 1, q0, c0, n0, a0, d0, e0, l0, first),
        (p1, 1, 0, q1, c1, n1, a1, d1, e1, l1, last),
    )
    for p_ref, at, inner, q_ref, c_ref, n_ref, a_ref, d_ref, b_ref, l_ref, out in sides:
        p, c = p_ref[at], c_ref[0]
        across, half = p.shape[0], d_ref.shape[1] // 2
        lap = p_ref[inner] + beside(p, 0.0, 0.0) + lateral(p) - 6.0 * p
        out[0:across] = p
        out[across : 2 * across] = c
        out[2 * across : 3 * across] = wave(p, q_ref[0], lap, c, n_ref[0], a_ref[0])
        d = d_ref[at]
        e = d - b_ref[at]
        d_in = d_ref[inner]
        e_in = d_in - b_ref[inner]
        labels = l_ref[0]
        s, v = lookup(labels, shear, 0), lookup(labels, viscosity, 0)
        lap_d = d_in + beside(d, 0.0, 0.0) + lateral(d) - 6.0 * d
        lap_e = e_in + beside(e, 0.0, 0.0) + lateral(e) - 6.0 * e
        base = 3 * across
        halves(out, base, d)
        halves(out, base + half, e)
        halves(out, base + 2 * half, d + e + s * lap_d + v * lap_e)
        halves(out, base + 3 * half, labels.astype(jnp.float32) + 1.0)


def border_columns(
    p_ref, q_ref, c_ref, n_ref, a_ref, d_ref, b_ref, l_ref, shear, viscosity, before, after, left, right
):
    deep, across, _ = p_ref.shape
    rows, cols, depth = d_ref.shape
    half = cols // 2
    row = lambda ref, base, j: ref[base + j : base + j + 1, :]
    base = 3 * across

    def line(ref, offset, j):
        at, lane = (j, 0) if j < half else (j - half, depth)
        return ref[base + offset + at : base + offset + at + 1, lane : lane + depth]

    for j, inner, k, k_in, out in (
        (0, 1, 0, 1, left),
        (across - 1, across - 2, cols - 1, cols - 2, right),
    ):
        p, c = p_ref[:, j, :], c_ref[:, j, :]
        p_up, p_down = row(before, 0, j), row(after, 0, j)
        lap = beside(p, p_up, p_down) + p_ref[:, inner, :] + lateral(p) - 6.0 * p
        out[0:deep] = p
        out[deep : 2 * deep] = c
        out[2 * deep : 3 * deep] = wave(
            p, q_ref[:, j, :], lap, c, n_ref[:, j, :], a_ref[:, j, :]
        )
        d = d_ref[:, k, :]
        e = d - b_ref[:, k, :]
        d_in = d_ref[:, k_in, :]
        e_in = d_in - b_ref[:, k_in, :]
        labels = l_ref[:, k, :]
        s, v = lookup(labels, shear, 0), lookup(labels, viscosity, 0)
        d_up, d_down = line(before, 0, k), line(after, 0, k)
        e_up, e_down = line(before, half, k), line(after, half, k)
        lap_d = beside(d, d_up, d_down) + d_in + lateral(d) - 6.0 * d
        lap_e = beside(e, e_up, e_down) + e_in + lateral(e) - 6.0 * e
        top = 3 * deep
        out[top : top + 1] = p_up
        out[top + 1 : top + 2] = p_down
        out[top + 2 : top + 3, 0:depth] = d_up
        out[top + 2 : top + 3, depth : 2 * depth] = e_up
        out[top + 3 : top + 4, 0:depth] = d_down
        out[top + 3 : top + 4, depth : 2 * depth] = e_down
        out[top + 4 : top + 8] = jnp.zeros((4, p.shape[1]), jnp.float32)
        out[top + 8 : top + 8 + rows, 0:depth] = d
        out[top + 8 : top + 8 + rows, depth : 2 * depth] = e
        out[top + 8 + rows : top + 8 + 2 * rows, 0:depth] = labels.astype(jnp.float32) + 1.0
        out[top + 8 + rows : top + 8 + 2 * rows, depth : 2 * depth] = (
            d + e + s * lap_d + v * lap_e
        )


def first_steps(
    p_ref, q_ref, c_ref, n_ref, a_ref, d_ref, b_ref, l_ref, shear, viscosity, before, after, mid, free
):
    deep, across, _ = p_ref.shape
    rows, cols, depth = d_ref.shape
    half = cols // 2
    base = 3 * across

    def acoustic(i, p_up, p_down):
        p = p_ref[i]
        lap = p_up + p_down + beside(p, 0.0, 0.0) + lateral(p) - 6.0 * p
        mid[i] = wave(p, q_ref[i], lap, c_ref[i], n_ref[i], a_ref[i])

    acoustic(0, before[0:across], p_ref[1])
    acoustic(deep - 1, p_ref[deep - 2], after[0:across])

    def acoustic_body(i, carry):
        acoustic(i, p_ref[i - 1], p_ref[i + 1])
        return carry

    lax.fori_loop(1, deep - 1, acoustic_body, 0)

    def elastic(i, d_up, d_down, e_up, e_down):
        d = d_ref[i]
        e = d - b_ref[i]
        s, v = lookup(l_ref[i], shear, 0), lookup(l_ref[i], viscosity, 0)
        lap_d = d_up + d_down + beside(d, 0.0, 0.0) + lateral(d) - 6.0 * d
        lap_e = e_up + e_down + beside(e, 0.0, 0.0) + lateral(e) - 6.0 * e
        free[i] = d + e + s * lap_d + v * lap_e

    change = lambda i: d_ref[i] - b_ref[i]
    elastic(
        0, whole(before, base, half, depth), d_ref[1], whole(before, base + half, half, depth), change(1)
    )
    elastic(
        rows - 1,
        d_ref[rows - 2],
        whole(after, base, half, depth),
        change(rows - 2),
        whole(after, base + half, half, depth),
    )

    def elastic_body(i, carry):
        elastic(i, d_ref[i - 1], d_ref[i + 1], change(i - 1), change(i + 1))
        return carry

    lax.fori_loop(1, rows - 1, elastic_body, 0)


def dot(x, y, contract=((1,), (0,))):
    return lax.dot_general(
        x, y, (contract, ((), ())), precision=EXACT, preferred_element_type=jnp.float32
    )


def selected(x, y):
    high = y.astype(jnp.bfloat16)
    low = (y - high.astype(jnp.float32)).astype(jnp.bfloat16)
    x = x.astype(jnp.bfloat16)
    product = functools.partial(jnp.dot, preferred_element_type=jnp.float32)
    return product(x, high) + product(x, low)


def iota(shape, dim):
    return lax.broadcasted_iota(jnp.int32, shape, dim)


def second_acoustic(
    blocks,
    capacity,
    chunk,
    mid_ref,
    p_ref,
    c_ref,
    n_ref,
    a_ref,
    own_ref,
    slot_ref,
    before,
    after,
    left,
    right,
    mid,
    new,
    send,
    first_col,
    last_col,
    pairs,
):
    deep, across, span = p_ref.shape
    mid[...] = mid_ref[...]
    for j, side, beyond in ((0, left, first_col), (across - 1, right, last_col)):
        mid[:, j, :] = mid_ref[:, j, :] + c_ref[:, j, :] * side[0:deep]
        beyond[...] = side[2 * deep : 3 * deep] + side[deep : 2 * deep] * p_ref[:, j, :]
    top = 3 * deep

    def row_beyond(side, edge, k):
        c = side[across : 2 * across]
        corners = at_ends(c.shape, left[top + k : top + k + 1], right[top + k : top + k + 1])
        return side[2 * across : 3 * across] + c * (p_ref[edge] + corners)

    def step(i, up, down):
        m, p, c, a = mid[i], p_ref[i], c_ref[i], a_ref[i]
        sides = beside(m, first_col[pl.ds(i, 1), :], last_col[pl.ds(i, 1), :])
        lap = up + down + sides + lateral(m) - 6.0 * m
        result = wave(m, p, lap, c, n_ref[i], a)
        new[i] = result
        return 0.1 * a * (m * m + result * result) * lax.rsqrt(c)

    def put(k, value):
        at = pl.ds(pl.multiple_of(k * across, across), across)
        for part in range(span // 128):
            pairs[part, at, :] = value[:, part * 128 : part * 128 + 128]

    put(0, step(0, row_beyond(before, 0, 0), mid[1]) + step(1, mid[0], mid[2]))
    put(
        deep // 2 - 1,
        step(deep - 2, mid[deep - 3], mid[deep - 1])
        + step(deep - 1, mid[deep - 2], row_beyond(after, deep - 1, 1)),
    )

    def body(k, carry):
        i = 2 * k
        put(k, step(i, mid[i - 1], mid[i + 1]) + step(i + 1, mid[i], mid[i + 2]))
        return carry

    lax.fori_loop(1, deep // 2 - 1, body, 0)
    count = deep // 2 * (across // 2)
    paired = jnp.concatenate(
        [
            pairs[part, pl.ds(0, count, stride=2), :] + pairs[part, pl.ds(1, count, stride=2), :]
            for part in range(span // 128)
        ],
        axis=1,
    )
    pairing = iota((256, 128), 0) // 2 == iota((256, 128), 1)
    pairing = pairing.astype(jnp.float32).astype(jnp.bfloat16)
    high = paired.astype(jnp.bfloat16)
    low = (paired - high.astype(jnp.float32)).astype(jnp.bfloat16)
    product = functools.partial(jnp.dot, preferred_element_type=jnp.float32)
    lines = 0.125 * jnp.concatenate(
        [
            product(high[:, at : at + 256], pairing) + product(low[:, at : at + 256], pairing)
            for at in range(0, span, 256)
        ],
        axis=1,
    )
    wide, tall = own_ref.shape
    spread = (iota((tall, count), 1) // wide == iota((tall, count), 0)).astype(jnp.float32)
    mine = iota((wide, count), 1) % wide == iota((wide, count), 0)
    spread_t = (iota((count, tall), 0) // wide == iota((count, tall), 1)).astype(jnp.float32)
    mine_t = iota((count, wide), 0) % wide == iota((count, wide), 1)

    def flat(ref):
        x = ref[...].astype(jnp.float32)
        along = jnp.sum(jnp.where(mine, dot(x, spread), 0.0), axis=0, keepdims=True)
        down = dot(spread_t, x, ((1,), (1,)))
        return along, jnp.sum(jnp.where(mine_t, down, 0.0), axis=1, keepdims=True)

    own_row, own_col = flat(own_ref)
    _, slot_col = flat(slot_ref)
    same = own_row == own_col
    before_it = iota((count, count), 0) < iota((count, count), 1)
    after_it = iota((count, count), 0) > iota((count, count), 1)
    ones = lambda x: jnp.where(x, 1.0, 0.0)
    rank_row = jnp.sum(ones(same & before_it), axis=0, keepdims=True)
    rank_col = jnp.sum(ones(same & after_it), axis=1, keepdims=True)
    total = blocks * chunk
    at = iota((total, count), 0)
    owner = own_row.astype(jnp.int32)
    match = ones(at == owner * chunk + rank_row.astype(jnp.int32))
    placing = ones(at == owner * chunk + capacity)
    depth = lines.shape[1]
    places = jnp.where(iota((count, depth), 1) == rank_col.astype(jnp.int32), slot_col + 1.0, 0.0)
    send[...] = selected(match, lines) + selected(placing, places)


def second_elastic(
    free_ref, d_ref, b_ref, l_ref, shear, viscosity, before, after, left, right, free, after_free,
    d_first, d_last, f_first, f_last
):
    rows, cols, depth = d_ref.shape
    half = cols // 2
    across = (before.shape[0] - 2 * cols) // 3
    base = 3 * across
    top = left.shape[0] - 2 * rows - 8
    free[...] = free_ref[...]
    for j, side, d_col, f_col in ((0, left, d_first, f_first), (cols - 1, right, d_last, f_last)):
        labels = l_ref[:, j, :]
        s, v = lookup(labels, shear, 0), lookup(labels, viscosity, 0)
        d_side = side[top + 8 : top + 8 + rows, 0:depth]
        e_side = side[top + 8 : top + 8 + rows, depth : 2 * depth]
        free[:, j, :] = free_ref[:, j, :] + s * d_side + v * e_side
        kinds = side[top + 8 + rows : top + 8 + 2 * rows, 0:depth]
        s, v = lookup(kinds, shear, 1.0), lookup(kinds, viscosity, 1.0)
        d = d_ref[:, j, :]
        d_col[...] = d_side
        f_col[...] = (
            side[top + 8 + rows : top + 8 + 2 * rows, depth : 2 * depth]
            + s * d
            + v * (d - b_ref[:, j, :])
        )

    def beyond(side, edge, k):
        part = lambda n: whole(side, base + n * half, half, depth)
        d, kinds = part(0), part(3)
        s, v = lookup(kinds, shear, 1.0), lookup(kinds, viscosity, 1.0)
        d_edge = d_ref[edge]
        corner = lambda ref, lane: ref[top + k : top + k + 1, lane : lane + depth]
        d_ends = at_ends(d.shape, corner(left, 0), corner(right, 0))
        e_ends = at_ends(d.shape, corner(left, depth), corner(right, depth))
        f = part(2) + s * (d_edge + d_ends) + v * (d_edge - b_ref[edge] + e_ends)
        return f, d

    def step(i, f_up, f_down, d_up, d_down):
        f, d = free[i], d_ref[i]
        s, v = lookup(l_ref[i], shear, 0), lookup(l_ref[i], viscosity, 0)
        at = lambda ref: ref[pl.ds(i, 1), :]
        lap_f = f_up + f_down + beside(f, at(f_first), at(f_last)) + lateral(f) - 6.0 * f
        lap_d = d_up + d_down + beside(d, at(d_first), at(d_last)) + lateral(d) - 6.0 * d
        after_free[i] = 2.0 * f - d + s * lap_f + v * (lap_f - lap_d)

    f_up, d_up = beyond(before, 0, 2)
    step(0, f_up, free[1], d_up, d_ref[1])
    f_down, d_down = beyond(after, rows - 1, 3)
    step(rows - 1, free[rows - 2], f_down, d_ref[rows - 2], d_down)

    def body(i, carry):
        step(i, free[i - 1], free[i + 1], d_ref[i - 1], d_ref[i + 1])
        return carry

    lax.fori_loop(1, rows - 1, body, 0)


def land(capacity, chunk, got_ref, force):
    total, depth = got_ref.shape
    got = got_ref[...]
    pick = iota((total, total), 1) // chunk * chunk + capacity == iota((total, total), 0)
    lanes = dot(got[:, 0:128], jnp.where(pick, 1.0, 0.0), ((0,), (0,)))
    mine = iota(lanes.shape, 1) % chunk == iota(lanes.shape, 0)
    place = jnp.sum(jnp.where(mine, lanes, 0.0), axis=0, keepdims=True)
    rows, cols, _ = force.shape
    cells = rows * cols
    landing = jnp.where(iota((cells, total), 0) + 1 == place.astype(jnp.int32), 1.0, 0.0)
    force[...] = selected(landing, got).reshape(rows, cols, depth)


def last_steps(force, free, after_free, l_ref, shear, viscosity, up, down, left, right, mid, new):
    rows, cols, depth = force.shape

    def step(i, f_up, f_down):
        f = force[i]
        s, v = lookup(l_ref[i], shear, 0), lookup(l_ref[i], viscosity, 0)
        at = lambda ref: ref[pl.ds(i, 1), :]
        lap = f_up + f_down + beside(f, at(left), at(right)) + lateral(f) - 6.0 * f
        mid[i] = free[i] + 0.25 * f
        new[i] = after_free[i] + 0.75 * f + 0.25 * (s + v) * lap

    step(0, up[...], force[1])
    step(rows - 1, force[rows - 2], down[...])

    def body(i, carry):
        step(i, force[i - 1], force[i + 1])
        return carry

    lax.fori_loop(1, rows - 1, body, 0)


def swap(first, last, axis):
    size = lax.axis_size(axis)
    up = [(i, i + 1) for i in range(size - 1)]
    down = [(j, i) for i, j in up]
    return lax.ppermute(last, axis, up), lax.ppermute(first, axis, down)


def local(
    pressure,
    pressure_prev,
    courant,
    nonlinearity,
    absorption,
    own_map,
    slot_table,
    displacement,
    displacement_prev,
    layer_labels,
    shear_table,
    viscosity_table,
):
    deep, across, span = pressure.shape
    rows, cols, depth = displacement.shape
    f32 = lambda *shape: jax.ShapeDtypeStruct(shape, jnp.float32)
    params = pltpu.CompilerParams(vmem_limit_bytes=8 << 20)
    scratch = lambda *shape: pltpu.VMEM(shape, jnp.float32)

    def run(kernel, out, *args, scratch_shapes=(), tables=()):
        specs = [SMEM if k in tables else VMEM for k in range(len(args))]
        moved = 4 * sum(x.size for x in args) + 4 * sum(x.size for x in jax.tree.leaves(out))
        cost = pl.CostEstimate(flops=20 * moved, bytes_accessed=moved, transcendentals=0)
        return pl.pallas_call(
            kernel,
            out_shape=out,
            in_specs=specs,
            out_specs=jax.tree.map(lambda _: VMEM, out),
            scratch_shapes=scratch_shapes,
            compiler_params=params,
            cost_estimate=cost,
        )(*args)

    fields = (
        (pressure, 2),
        (pressure_prev, 1),
        (courant, 1),
        (nonlinearity, 1),
        (absorption, 1),
        (displacement, 2),
        (displacement_prev, 2),
        (layer_labels, 1),
    )
    face = 3 * across + 2 * cols
    first, last = pl.pallas_call(
        border_rows,
        out_shape=(f32(face, span), f32(face, span)),
        in_specs=[pl.BlockSpec(memory_space=pltpu.HBM)] * len(fields) + [SMEM, SMEM],
        out_specs=(VMEM, VMEM),
        scratch_shapes=[
            pltpu.VMEM((count,) + x.shape[1:], x.dtype) for x, count in fields for _ in range(2)
        ]
        + [pltpu.SemaphoreType.DMA((2 * len(fields),))],
        compiler_params=pltpu.CompilerParams(vmem_limit_bytes=55 << 20),
    )(*[x for x, _ in fields], shear_table, viscosity_table)
    before, after = swap(first, last, "gx")
    inputs = tuple(x for x, _ in fields) + (shear_table, viscosity_table, before, after)
    side = 3 * deep + 8 + 2 * rows
    first, last = run(border_columns, (f32(side, span),) * 2, *inputs, tables=(8, 9))
    left, right = swap(first, last, "gy")
    mid, free = run(
        first_steps, (f32(deep, across, span), f32(rows, cols, depth)), *inputs, tables=(8, 9)
    )
    blocks = lax.axis_size("gx") * lax.axis_size("gy")
    capacity = max(2, deep // 2 * (across // 2) // blocks)
    chunk = -(-(capacity + 1) // 8) * 8
    pressure_mid, pressure_new, send = run(
        functools.partial(second_acoustic, blocks, capacity, chunk),
        (f32(deep, across, span), f32(deep, across, span), f32(blocks * chunk, depth)),
        mid,
        pressure,
        courant,
        nonlinearity,
        absorption,
        own_map.T,
        slot_table.T,
        before,
        after,
        left,
        right,
        scratch_shapes=[scratch(deep, span), scratch(deep, span), scratch(span // 128, deep // 2 * across, 128)],
    )
    got = lax.all_to_all(send, ("gx", "gy"), split_axis=0, concat_axis=0, tiled=True)
    free, after_free = run(
        second_elastic,
        (f32(rows, cols, depth),) * 2,
        free,
        displacement,
        displacement_prev,
        layer_labels,
        shear_table,
        viscosity_table,
        before,
        after,
        left,
        right,
        scratch_shapes=[scratch(rows, depth)] * 4,
        tables=(4, 5),
    )
    tissue_force = run(functools.partial(land, capacity, chunk), f32(rows, cols, depth), got)
    up, down = swap(tissue_force[0], tissue_force[rows - 1], "gx")
    beside_l, beside_r = swap(tissue_force[:, 0], tissue_force[:, cols - 1], "gy")
    displacement_mid, displacement_new = run(
        last_steps,
        (f32(rows, cols, depth),) * 2,
        tissue_force,
        free,
        after_free,
        layer_labels,
        shear_table,
        viscosity_table,
        up,
        down,
        beside_l,
        beside_r,
        tables=(4, 5),
    )
    return (pressure_mid, pressure_new, tissue_force, displacement_mid, displacement_new)


def solution(mesh):
    block = P(("group", "gx"), "gy", None)
    plane = P(("group", "gx"), "gy")
    return jax.shard_map(
        local,
        mesh=mesh,
        in_specs=(block,) * 5 + (plane,) * 2 + (block,) * 3 + (P("group"),) * 2,
        out_specs=(block,) * 5,
        check_vma=False,
    )
```

time: 127 us -> 67.1 us (0.53); the launches traced: 124 us -> 66.6 us
  starting transfers between devices: 53.6 us -> 17 us
  other arithmetic: 33.3 us -> 0 us
  Pallas kernels: 0 us -> 21.3 us
  blocking collectives: 0 us -> 16.5 us
  local copies, waits for them, and re-layouts: 18.1 us -> 1.96 us
  waiting for transfers between devices: 15.6 us -> 8.9 us
  matrix products: 2.46 us -> 0 us
    pallas_call x0 -> x7, Pallas kernels: none -> 21.3 us  [the longest x6 17.6 us: run(): pl.pallas_call(kernel, out_shape=out, in_specs=specs, out_specs=jax.tree....]
    ppermute x16 -> x8, starting transfers between devices: 38 us -> 17 us  [swap(): return (lax.ppermute(last, axis, up), lax.ppermute(first, axis, down))]
    all_to_all x0 -> x1, blocking collectives: none -> 16.5 us  [local(): lax.all_to_all(send, ('gx', 'gy'), split_axis=0, concat_axis=0, tiled=True)]
    all_to_all x2 -> x0, starting transfers between devices: 15.7 us -> none  [the longest x1 8.29 us: local(): lax.all_to_all(send_lines.reshape(blocks, capacity, lateral // 2), ('gx',...]
    another operation x2 -> x0, other arithmetic: 10.1 us -> none  [elastic_step(): ext = extended(jnp.stack([now, now - before]), (('gx', 1), ('gy', 2)), 1)]
    add x3 -> x0, other arithmetic: 7.98 us -> none  [the longest x1 7.28 us: elastic_step(): 2.0 * now - before + shear * laplace_ext(ext[0])]
    slice x11 -> x1, local copies, waits for them, and re-layouts: 7.35 us -> 1.06 us  [local(): tissue_force[:, 0]]
    sub x2 -> x0, other arithmetic: 6.14 us -> none  [the longest x1 6.11 us: wave_update(): 2.0 * now - before + courant * laplace_ext(now_ext)]
  transfers between devices with their start and end apart: 18 -> 8, of which waited for: 6 -> 4; matrix products, arithmetic and copies ran while one was open for 15% -> 2% of each run, Pallas kernels for 0% -> 12%
where the time goes in v1:
time: 67.1 us; the launch traced here: 66.6 us
  Pallas kernels  21.3 us (32%)
  starting transfers between devices  17 us (25%)
  blocking collectives  16.5 us (25%)
  waiting for transfers between devices  8.9 us (13%)
  local copies, waits for them, and re-layouts  1.96 us (3%)
  between operations  0.93 us (1%)
    pallas_call x6, Pallas kernels, run(): pl.pallas_call(kernel, out_shape=out, in_specs=specs, out_specs=jax.tree....  17.6 us
    ppermute x8, starting transfers between devices, swap(): return (lax.ppermute(last, axis, up), lax.ppermute(first, axis, down))  17 us
    all_to_all x1, blocking collectives, local(): lax.all_to_all(send, ('gx', 'gy'), split_axis=0, concat_axis=0, tiled=True)  16.5 us
    ppermute x8, waiting for transfers between devices, swap(): return (lax.ppermute(last, axis, up), lax.ppermute(first, axis, down))  8.9 us
    pallas_call x1, Pallas kernels, local(): pl.pallas_call(border_rows, out_shape=(f32(face, span), f32(face, span)),...  3.67 us
  transfers between devices with their start and end apart: 8, of which 4 were waited for; matrix products, arithmetic and copies ran while one was open for 2% of the time, Pallas kernels for 12%

profile of v1, /device:TPU:0, one launch (start us, length us, event | category | flops | bytes accessed | tf_op | source)
XLA Modules:
  0.0 66.6 jit_solution(15415590890674149162)
XLA Ops:
  0.7 3.7 %shard_map.155 = (f32[112,768]{1,0:T(8,128)}, f32[112,768]{1,0:T(8,128)}) custom-call(f32[24,16,768]{2,1,0:T(8,128)} %p_ref.5, f32[24,16,768]{2,1,0:T(8,128)} %q_ref.3, f32[24,16,768]{2,1,0:T(8,128)} %c_ref.5, f32[24,16,768]{2,1,0:T(8,128)} %n_ref.5, f32[24,16,768]{2,1,0:T(8,128)} %a_ref.5, f32[16,32,384]{2,1,0:T(8,128)} %d_ref.5, f32[16,32,384]{2,1,0:T(8,128)} %b_ref.5, ...), custom_call_target="tpu_custom_call" | custom-call | tf_op jit(solution)/shard_map/pallas_call | solution.py:476
  4.4 2.4 %collective-permute-start = (f32[112,768]{1,0:T(8,128)}, f32[112,768]{1,0:T(8,128)S(1)}, u32[]{:S(2)}, u32[]{:S(2)}) collective-permute-start(f32[112,768]{1,0:T(8,128)} %get-tuple-element.18), channel_id=1, source_target_pairs={{0,4},{4,8},{8,12},{1,5},{5,9},{9,13},{2,6},{6,10},{10,14},{3,7},{... | collective-permute-start | bytes 1032200 | tf_op jit(solution)/shard_map/ppermute | solution.py:428
  6.8 1.3 %collective-permute-start.1 = (f32[112,768]{1,0:T(8,128)}, f32[112,768]{1,0:T(8,128)S(1)}, u32[]{:S(2)}, u32[]{:S(2)}) collective-permute-start(f32[112,768]{1,0:T(8,128)} %get-tuple-element.19), channel_id=1, source_target_pairs={{4,0},{8,4},{12,8},{5,1},{9,5},{13,9},{6,2},{10,6},{14,10},{7,3},{... | collective-permute-start | bytes 1032200 | tf_op jit(solution)/shard_map/ppermute | solution.py:428
  8.1 0.2 collective-permute-done.before
  8.3 4.4 %collective-permute-done.1.after = f32[112,768]{1,0:T(8,128)S(1)} collective-permute-done((f32[112,768]{1,0:T(8,128)}, f32[112,768]{1,0:T(8,128)S(1)}, u32[]{:S(2)}, u32[]{:S(2)}) %collective-permute-start.1) | collective-permute-done | bytes 344096 | tf_op jit(solution)/shard_map/ppermute | solution.py:428
  12.8 1.4 %shard_map.157 = (f32[112,768]{1,0:T(8,128)S(1)}, f32[112,768]{1,0:T(8,128)S(1)}) custom-call(f32[24,16,768]{2,1,0:T(8,128)S(1)} %copy-done.1, f32[24,16,768]{2,1,0:T(8,128)S(1)} %copy-done.7, f32[24,16,768]{2,1,0:T(8,128)S(1)} %copy-done.2, f32[24,16,768]{2,1,0:T(8,128)S(1)} %copy-done.3, f32[24,16,768]{2,1,0:T(8,128)S(1)} %copy-done.4, ...), custom_call_target="tpu_custom_call" | custom-call | flops 192676480 | bytes 9633824 | tf_op jit(solution)/shard_map/pallas_call | solution.py:455
  14.1 3.5 %collective-permute-start.2 = (f32[112,768]{1,0:T(8,128)S(1)}, f32[112,768]{1,0:T(8,128)S(1)}, u32[]{:S(2)}, u32[]{:S(2)}) collective-permute-start(f32[112,768]{1,0:T(8,128)S(1)} %get-tuple-element.21), channel_id=1, source_target_pairs={{0,1},{1,2},{2,3},{4,5},{5,6},{6,7},{8,9},{9,10},{10,11},{12,13},{... | collective-permute-start | bytes 1032200 | tf_op jit(solution)/shard_map/ppermute | solution.py:428
  17.6 0.0 copy-start.11
  17.6 0.0 copy-start.12
  17.7 1.3 %collective-permute-start.3 = (f32[112,768]{1,0:T(8,128)S(1)}, f32[112,768]{1,0:T(8,128)S(1)}, u32[]{:S(2)}, u32[]{:S(2)}) collective-permute-start(f32[112,768]{1,0:T(8,128)S(1)} %get-tuple-element.22), channel_id=1, source_target_pairs={{1,0},{2,1},{3,2},{5,4},{6,5},{7,6},{9,8},{10,9},{11,10},{13,12},{... | collective-permute-start | bytes 1032200 | tf_op jit(solution)/shard_map/ppermute | solution.py:428
  19.0 5.0 %shard_map.156 = (f32[24,16,768]{2,1,0:T(8,128)S(1)}, f32[16,32,384]{2,1,0:T(8,128)S(1)}) custom-call(f32[24,16,768]{2,1,0:T(8,128)S(1)} %copy-done.1, f32[24,16,768]{2,1,0:T(8,128)S(1)} %copy-done.7, f32[24,16,768]{2,1,0:T(8,128)S(1)} %copy-done.2, f32[24,16,768]{2,1,0:T(8,128)S(1)} %copy-done.3, f32[24,16,768]{2,1,0:T(8,128)S(1)} %copy-done.4, ...), custom_call_target="tpu_custom_call" | custom-call | flops 218235520 | bytes 10911776 | tf_op jit(solution)/shard_map/pallas_call | solution.py:455
  24.0 2.9 %collective-permute-done.3.right = f32[112,768]{1,0:T(8,128)S(1)} collective-permute-done((f32[112,768]{1,0:T(8,128)S(1)}, f32[112,768]{1,0:T(8,128)S(1)}, u32[]{:S(2)}, u32[]{:S(2)}) %collective-permute-start.3) | collective-permute-done | bytes 344096 | tf_op jit(solution)/shard_map/ppermute | solution.py:428
  26.8 3.4 %shard_map.158 = (f32[24,16,768]{2,1,0:T(8,128)}, f32[24,16,768]{2,1,0:T(8,128)}, f32[128,384]{1,0:T(8,128)S(1)}) custom-call(f32[24,16,768]{2,1,0:T(8,128)S(1)} %get-tuple-element.20.mid_ref, f32[24,16,768]{2,1,0:T(8,128)S(1)} %copy-done.1, f32[24,16,768]{2,1,0:T(8,128)S(1)} %copy-done.2, f32[24,16,768]{2,1,0:T(8,128)S(1)} %copy-done.3, ...), custom_call_target="tpu_custom_call" | custom-call | flops 196623360 | bytes 9831168 | tf_op jit(solution)/shard_map/pallas_call | solution.py:455
  30.2 16.5 %all_to_all.11 = f32[16,8,384]{2,1,0:T(8,128)S(1)} all-to-all(f32[16,8,384]{2,1,0:T(8,128)S(1)} %bitcast.15), channel_id=1, replica_groups=mesh['group'=2,'gx'=4,'gy'=4] {'gx','gy'}, dimensions={0} | all-to-all | bytes 393216 | tf_op jit(solution)/shard_map/all_to_all | solution.py:514
  46.7 1.6 %shard_map.159.force = f32[16,32,384]{2,1,0:T(8,128)} custom-call(f32[128,384]{1,0:T(8,128)S(1)} %bitcast.14), custom_call_target="tpu_custom_call" | custom-call | flops 19660800 | bytes 983040 | tf_op jit(solution)/shard_map/pallas_call | solution.py:455
  48.3 0.8 %slice_bitcast_fusion = (f32[32,384]{1,0:T(8,128)S(1)}, f32[32,384]{1,0:T(8,128)S(1)}) fusion(f32[16,32,384]{2,1,0:T(8,128)} %shard_map.159.force), kind=kLoop, calls=%fused_computation | loop fusion | bytes 196608 | tf_op jit(solution)/shard_map/squeeze | solution.py:532
  49.1 1.3 %collective-permute-start.5 = (f32[32,384]{1,0:T(8,128)S(1)}, f32[32,384]{1,0:T(8,128)S(1)}, u32[]{:S(2)}, u32[]{:S(2)}) collective-permute-start(f32[32,384]{1,0:T(8,128)S(1)} %get-tuple-element.33), channel_id=1, source_target_pairs={{4,0},{8,4},{12,8},{5,1},{9,5},{13,9},{6,2},{10,6},{14,10},{7,3},{... | collective-permute-start | bytes 147464 | tf_op jit(solution)/shard_map/ppermute | solution.py:428
  50.4 3.0 %collective-permute-start.4 = (f32[32,384]{1,0:T(8,128)S(1)}, f32[32,384]{1,0:T(8,128)S(1)}, u32[]{:S(2)}, u32[]{:S(2)}) collective-permute-start(f32[32,384]{1,0:T(8,128)S(1)} %get-tuple-element.34), channel_id=1, source_target_pairs={{0,4},{4,8},{8,12},{1,5},{5,9},{9,13},{2,6},{6,10},{10,14},{3,7},{... | collective-permute-start | bytes 147464 | tf_op jit(solution)/shard_map/ppermute | solution.py:428
  53.4 1.1 %fusion = (f32[16,1,384]{2,1,0:T(1,128)S(1)}, f32[16,1,384]{2,1,0:T(1,128)S(1)}) fusion(f32[16,32,384]{2,1,0:T(8,128)} %shard_map.159.force), kind=kLoop, calls=%fused_computation.4 | loop fusion | bytes 98304 | tf_op jit(solution)/shard_map/slice | solution.py:533
  54.5 2.9 %collective-permute-start.6 = (f32[16,384]{1,0:T(8,128)S(1)}, f32[16,384]{1,0:T(8,128)S(1)}, u32[]{:S(2)}, u32[]{:S(2)}) collective-permute-start(f32[16,384]{1,0:T(8,128)S(1)} %bitcast.19), channel_id=1, source_target_pairs={{0,1},{1,2},{2,3},{4,5},{5,6},{6,7},{8,9},{9,10},{10,11},{12,13},{... | collective-permute-start | bytes 73736 | tf_op jit(solution)/shard_map/ppermute | solution.py:428
  57.4 1.3 %collective-permute-start.7 = (f32[16,384]{1,0:T(8,128)S(1)}, f32[16,384]{1,0:T(8,128)S(1)}, u32[]{:S(2)}, u32[]{:S(2)}) collective-permute-start(f32[16,384]{1,0:T(8,128)S(1)} %bitcast.18), channel_id=1, source_target_pairs={{1,0},{2,1},{3,2},{5,4},{6,5},{7,6},{9,8},{10,9},{11,10},{13,12},{... | collective-permute-start | bytes 73736 | tf_op jit(solution)/shard_map/ppermute | solution.py:428
  58.8 3.0 %shard_map.160 = (f32[16,32,384]{2,1,0:T(8,128)S(1)}, f32[16,32,384]{2,1,0:T(8,128)S(1)}) custom-call(f32[16,32,384]{2,1,0:T(8,128)S(1)} %get-tuple-element.26.free_ref, f32[16,32,384]{2,1,0:T(8,128)S(1)} %copy-done.5, f32[16,32,384]{2,1,0:T(8,128)S(1)} %copy-done.6, s32[16,32,384]{2,1,0:T(8,128)S(1)} %copy-done, f32[4]{0:T(128)S(1)} %copy-done.9, ...), custom_call_target="tpu_custom_call" | custom-call | flops 121897600 | bytes 6094880 | tf_op jit(solution)/shard_map/pallas_call | solution.py:455
  61.8 1.5 %collective-permute-done.7.right = f32[16,384]{1,0:T(8,128)S(1)} collective-permute-done((f32[16,384]{1,0:T(8,128)S(1)}, f32[16,384]{1,0:T(8,128)S(1)}, u32[]{:S(2)}, u32[]{:S(2)}) %collective-permute-start.7) | collective-permute-done | bytes 24608 | tf_op jit(solution)/shard_map/ppermute | solution.py:428
  63.3 3.3 %shard_map.161 = (f32[16,32,384]{2,1,0:T(8,128)}, f32[16,32,384]{2,1,0:T(8,128)}) custom-call(f32[16,32,384]{2,1,0:T(8,128)S(1)} %copy-done.8, f32[16,32,384]{2,1,0:T(8,128)S(1)} %get-tuple-element.27.free, f32[16,32,384]{2,1,0:T(8,128)S(1)} %get-tuple-element.28.after_free, s32[16,32,384]{2,1,0:T(8,128)S(1)} %copy-done, f32[4]{0:T(128)S(1)} %copy-done.9, ...), custom_call_target="tpu_custom_call" | custom-call | flops 97321600 | bytes 4866080 | tf_op jit(solution)/shard_map/pallas_call | solution.py:455
  (30 shorter events, 0.1 us)
Async XLA Ops:
  0.6 12.0 %copy-start.10 = (f32[4]{0:T(128)S(1)}, f32[4]{0:T(128)}, u32[]{:S(2)}) copy-start(f32[4]{0:T(128)} %viscosity.7) | copy-start | bytes 52
  0.6 12.0 %copy-start.9 = (f32[4]{0:T(128)S(1)}, f32[4]{0:T(128)}, u32[]{:S(2)}) copy-start(f32[4]{0:T(128)} %shear.7) | copy-start | bytes 52
  0.7 12.0 %copy-start = (s32[16,32,384]{2,1,0:T(8,128)S(1)}, s32[16,32,384]{2,1,0:T(8,128)}, u32[]{:S(2)}) copy-start(s32[16,32,384]{2,1,0:T(8,128)} %l_ref.7) | copy-start | bytes 2359300
  0.7 12.0 %copy-start.6 = (f32[16,32,384]{2,1,0:T(8,128)S(1)}, f32[16,32,384]{2,1,0:T(8,128)}, u32[]{:S(2)}) copy-start(f32[16,32,384]{2,1,0:T(8,128)} %b_ref.5) | copy-start | bytes 2359300
  0.7 12.0 %copy-start.5 = (f32[16,32,384]{2,1,0:T(8,128)S(1)}, f32[16,32,384]{2,1,0:T(8,128)}, u32[]{:S(2)}) copy-start(f32[16,32,384]{2,1,0:T(8,128)} %d_ref.5) | copy-start | bytes 2359300
  0.7 12.0 %copy-start.4 = (f32[24,16,768]{2,1,0:T(8,128)S(1)}, f32[24,16,768]{2,1,0:T(8,128)}, u32[]{:S(2)}) copy-start(f32[24,16,768]{2,1,0:T(8,128)} %a_ref.5) | copy-start | bytes 3538948
  0.7 12.0 %copy-start.3 = (f32[24,16,768]{2,1,0:T(8,128)S(1)}, f32[24,16,768]{2,1,0:T(8,128)}, u32[]{:S(2)}) copy-start(f32[24,16,768]{2,1,0:T(8,128)} %n_ref.5) | copy-start | bytes 3538948
  0.7 12.0 %copy-start.2 = (f32[24,16,768]{2,1,0:T(8,128)S(1)}, f32[24,16,768]{2,1,0:T(8,128)}, u32[]{:S(2)}) copy-start(f32[24,16,768]{2,1,0:T(8,128)} %c_ref.5) | copy-start | bytes 3538948
  0.7 12.0 %copy-start.1 = (f32[24,16,768]{2,1,0:T(8,128)S(1)}, f32[24,16,768]{2,1,0:T(8,128)}, u32[]{:S(2)}) copy-start(f32[24,16,768]{2,1,0:T(8,128)} %p_ref.5) | copy-start | bytes 3538948
  0.7 12.0 %copy-start.7 = (f32[24,16,768]{2,1,0:T(8,128)S(1)}, f32[24,16,768]{2,1,0:T(8,128)}, u32[]{:S(2)}) copy-start(f32[24,16,768]{2,1,0:T(8,128)} %q_ref.3) | copy-start | bytes 3538948
  4.4 3.9 %collective-permute-start = (f32[112,768]{1,0:T(8,128)}, f32[112,768]{1,0:T(8,128)S(1)}, u32[]{:S(2)}, u32[]{:S(2)}) collective-permute-start(f32[112,768]{1,0:T(8,128)} %get-tuple-element.18), channel_id=1, source_target_pairs={{0,4},{4,8},{8,12},{1,5},{5,9},{9,13},{2,6},{6,10},{10,14},{3,7},{... | collective-permute-start | bytes 1032200 | tf_op jit(solution)/shard_map/ppermute | solution.py:428
  6.8 5.8 %collective-permute-start.1 = (f32[112,768]{1,0:T(8,128)}, f32[112,768]{1,0:T(8,128)S(1)}, u32[]{:S(2)}, u32[]{:S(2)}) collective-permute-start(f32[112,768]{1,0:T(8,128)} %get-tuple-element.19), channel_id=1, source_target_pairs={{4,0},{8,4},{12,8},{5,1},{9,5},{13,9},{6,2},{10,6},{14,10},{7,3},{... | collective-permute-start | bytes 1032200 | tf_op jit(solution)/shard_map/ppermute | solution.py:428
  14.1 9.8 %collective-permute-start.2 = (f32[112,768]{1,0:T(8,128)S(1)}, f32[112,768]{1,0:T(8,128)S(1)}, u32[]{:S(2)}, u32[]{:S(2)}) collective-permute-start(f32[112,768]{1,0:T(8,128)S(1)} %get-tuple-element.21), channel_id=1, source_target_pairs={{0,1},{1,2},{2,3},{4,5},{5,6},{6,7},{8,9},{9,10},{10,11},{12,13},{... | collective-permute-start | bytes 1032200 | tf_op jit(solution)/shard_map/ppermute | solution.py:428
  17.6 9.2 %copy-start.11 = (s32[12,8]{0,1:T(8,128)S(1)}, s32[12,8]{0,1:T(8,128)}, u32[]{:S(2)}) copy-start(s32[12,8]{0,1:T(8,128)} %param.17) | copy-start | bytes 1156
  17.6 9.2 %copy-start.12 = (s32[12,8]{0,1:T(8,128)S(1)}, s32[12,8]{0,1:T(8,128)}, u32[]{:S(2)}) copy-start(s32[12,8]{0,1:T(8,128)} %param.18) | copy-start | bytes 1156
  17.7 9.1 %collective-permute-start.3 = (f32[112,768]{1,0:T(8,128)S(1)}, f32[112,768]{1,0:T(8,128)S(1)}, u32[]{:S(2)}, u32[]{:S(2)}) collective-permute-start(f32[112,768]{1,0:T(8,128)S(1)} %get-tuple-element.22), channel_id=1, source_target_pairs={{1,0},{2,1},{3,2},{5,4},{6,5},{7,6},{9,8},{10,9},{11,10},{13,12},{... | collective-permute-start | bytes 1032200 | tf_op jit(solution)/shard_map/ppermute | solution.py:428
  49.1 14.2 %collective-permute-start.5 = (f32[32,384]{1,0:T(8,128)S(1)}, f32[32,384]{1,0:T(8,128)S(1)}, u32[]{:S(2)}, u32[]{:S(2)}) collective-permute-start(f32[32,384]{1,0:T(8,128)S(1)} %get-tuple-element.33), channel_id=1, source_target_pairs={{4,0},{8,4},{12,8},{5,1},{9,5},{13,9},{6,2},{10,6},{14,10},{7,3},{... | collective-permute-start | bytes 147464 | tf_op jit(solution)/shard_map/ppermute | solution.py:428
  50.4 12.9 %collective-permute-start.4 = (f32[32,384]{1,0:T(8,128)S(1)}, f32[32,384]{1,0:T(8,128)S(1)}, u32[]{:S(2)}, u32[]{:S(2)}) collective-permute-start(f32[32,384]{1,0:T(8,128)S(1)} %get-tuple-element.34), channel_id=1, source_target_pairs={{0,4},{4,8},{8,12},{1,5},{5,9},{9,13},{2,6},{6,10},{10,14},{3,7},{... | collective-permute-start | bytes 147464 | tf_op jit(solution)/shard_map/ppermute | solution.py:428
  54.5 7.3 %collective-permute-start.6 = (f32[16,384]{1,0:T(8,128)S(1)}, f32[16,384]{1,0:T(8,128)S(1)}, u32[]{:S(2)}, u32[]{:S(2)}) collective-permute-start(f32[16,384]{1,0:T(8,128)S(1)} %bitcast.19), channel_id=1, source_target_pairs={{0,1},{1,2},{2,3},{4,5},{5,6},{6,7},{8,9},{9,10},{10,11},{12,13},{... | collective-permute-start | bytes 73736 | tf_op jit(solution)/shard_map/ppermute | solution.py:428
  57.4 5.9 %collective-permute-start.7 = (f32[16,384]{1,0:T(8,128)S(1)}, f32[16,384]{1,0:T(8,128)S(1)}, u32[]{:S(2)}, u32[]{:S(2)}) collective-permute-start(f32[16,384]{1,0:T(8,128)S(1)} %bitcast.18), channel_id=1, source_target_pairs={{1,0},{2,1},{3,2},{5,4},{6,5},{7,6},{9,8},{10,9},{11,10},{13,12},{... | collective-permute-start | bytes 73736 | tf_op jit(solution)/shard_map/ppermute | solution.py:428
  58.7 4.6 %copy-start.8 = (f32[16,32,384]{2,1,0:T(8,128)S(1)}, f32[16,32,384]{2,1,0:T(8,128)}, u32[]{:S(2)}) copy-start(f32[16,32,384]{2,1,0:T(8,128)} %shard_map.159.force) | copy-start | bytes 2359300

commit v2 on v1

--- a/solution.py
+++ b/solution.py
@@ -220,17 +220,88 @@
     return lax.broadcasted_iota(jnp.int32, shape, dim)
 
 
+def address(grid, tile, room, chunk, own_ref, slot_ref, match, placed):
+    (tiles_down, tiles_across), (rows, cols) = grid, tile
+    blocks, cells = tiles_down * tiles_across, rows * cols
+    wide, tall = own_ref.shape
+    count = wide * tall
+    parts = match.shape[1] // count
+
+    spread = (iota((tall, count), 1) // wide == iota((tall, count), 0)).astype(jnp.float32)
+    mine = iota((wide, count), 1) % wide == iota((wide, count), 0)
+    spread_t = (iota((count, tall), 0) // wide == iota((count, tall), 1)).astype(jnp.float32)
+    mine_t = iota((count, wide), 0) % wide == iota((count, wide), 1)
+
+    def flat(ref):
+        x = ref[...].astype(jnp.float32)
+        along = jnp.sum(jnp.where(mine, dot(x, spread), 0.0), axis=0, keepdims=True)
+        down = dot(spread_t, x, ((1,), (1,)))
+        down = jnp.sum(jnp.where(mine_t, down, 0.0), axis=1, keepdims=True)
+        return along.astype(jnp.int32), down.astype(jnp.int32)
+
+    def entries(own, slot):
+        r, c = slot // cols, slot % cols
+        tile_r, tile_c = own // tiles_across, own % tiles_across
+        focal = own < blocks
+        nobody = jnp.full(own.shape, -1, jnp.int32)
+        up = focal & (r == 0) & (tile_r > 0)
+        down = focal & (r == rows - 1) & (tile_r < tiles_down - 1)
+        left = focal & (c == 0) & (tile_c > 0)
+        right = focal & (c == cols - 1) & (tile_c < tiles_across - 1)
+        to = (
+            jnp.where(focal, own, nobody),
+            jnp.where(up, own - tiles_across, jnp.where(down, own + tiles_across, nobody)),
+            jnp.where(left, own - 1, jnp.where(right, own + 1, nobody)),
+        )
+        place = (
+            slot,
+            cells + c + jnp.where(up, cols, 0),
+            cells + 2 * cols + r + jnp.where(left, rows, 0),
+        )
+        return to, place
+
+    (own_row, own_col), (slot_row, slot_col) = flat(own_ref), flat(slot_ref)
+    to_row, place_row = entries(own_row, slot_row)
+    to_col, _ = entries(own_col, slot_col)
+    ones = lambda x: jnp.where(x, 1.0, 0.0)
+    earlier = iota((count, count), 0) < iota((count, count), 1)
+    used, ranks = jnp.zeros(own_row.shape, jnp.float32), []
+    for k in range(3):
+        rank = jnp.zeros(own_row.shape, jnp.float32)
+        for other in range(k + 1):
+            same = to_col[other] == to_row[k]
+            same = same & earlier if other == k else same
+            rank = rank + jnp.sum(ones(same), axis=0, keepdims=True)
+        ranks.append(rank.astype(jnp.int32))
+        used = jnp.maximum(used, jnp.where(to_row[k] >= 0, rank + 1.0, 0.0))
+    full = jnp.where(jnp.max(used) > room, 1.0, 0.0)
+    total = blocks * chunk
+    at = iota((total, count), 0)
+    fits = [(to >= 0) & (rank < room) for to, rank in zip(to_row, ranks)]
+    base = [
+        jnp.where(fit, to * chunk + rank, -total) for fit, to, rank in zip(fits, to_row, ranks)
+    ]
+    for part in range(parts):
+        here = at - part * room
+        match[:, part * count : part * count + count] = sum(ones(here == b) for b in base)
+    lanes = (128, count)
+    row, lane = iota((total, 128), 0), iota((total, 128), 1)
+    result = jnp.where((row % chunk == chunk - 1) & (lane == room), full, 0.0)
+    for fit, to, rank, place in zip(fits, to_row, ranks, place_row):
+        target = ones(at == jnp.where(fit, to * chunk + chunk - 1, -1))
+        value = jnp.where(iota(lanes, 0) == rank, place.astype(jnp.float32) + 1.0, 0.0)
+        result = result + dot(target, value, ((1,), (1,)))
+    placed[...] = result
+
+
 def second_acoustic(
-    blocks,
-    capacity,
-    chunk,
     mid_ref,
     p_ref,
     c_ref,
     n_ref,
     a_ref,
-    own_ref,
-    slot_ref,
+    match_ref,
+    placed_ref,
     before,
     after,
     left,
@@ -300,34 +371,9 @@
         ],
         axis=1,
     )
-    wide, tall = own_ref.shape
-    spread = (iota((tall, count), 1) // wide == iota((tall, count), 0)).astype(jnp.float32)
-    mine = iota((wide, count), 1) % wide == iota((wide, count), 0)
-    spread_t = (iota((count, tall), 0) // wide == iota((count, tall), 1)).astype(jnp.float32)
-    mine_t = iota((count, wide), 0) % wide == iota((count, wide), 1)
-
-    def flat(ref):
-        x = ref[...].astype(jnp.float32)
-        along = jnp.sum(jnp.where(mine, dot(x, spread), 0.0), axis=0, keepdims=True)
-        down = dot(spread_t, x, ((1,), (1,)))
-        return along, jnp.sum(jnp.where(mine_t, down, 0.0), axis=1, keepdims=True)
-
-    own_row, own_col = flat(own_ref)
-    _, slot_col = flat(slot_ref)
-    same = own_row == own_col
-    before_it = iota((count, count), 0) < iota((count, count), 1)
-    after_it = iota((count, count), 0) > iota((count, count), 1)
-    ones = lambda x: jnp.where(x, 1.0, 0.0)
-    rank_row = jnp.sum(ones(same & before_it), axis=0, keepdims=True)
-    rank_col = jnp.sum(ones(same & after_it), axis=1, keepdims=True)
-    total = blocks * chunk
-    at = iota((total, count), 0)
-    owner = own_row.astype(jnp.int32)
-    match = ones(at == owner * chunk + rank_row.astype(jnp.int32))
-    placing = ones(at == owner * chunk + capacity)
-    depth = lines.shape[1]
-    places = jnp.where(iota((count, depth), 1) == rank_col.astype(jnp.int32), slot_col + 1.0, 0.0)
-    send[...] = selected(match, lines) + selected(placing, places)
+    count, depth = lines.shape
+    parts = [lines[:, at : at + 128] for at in range(0, depth, 128)]
+    send[...] = selected(match_ref[...], jnp.concatenate(parts, axis=0)) + placed_ref[...]
 
 
 def second_elastic(
@@ -387,21 +433,31 @@
     lax.fori_loop(1, rows - 1, body, 0)
 
 
-def land(capacity, chunk, got_ref, force):
-    total, depth = got_ref.shape
-    got = got_ref[...]
-    pick = iota((total, total), 1) // chunk * chunk + capacity == iota((total, total), 0)
-    lanes = dot(got[:, 0:128], jnp.where(pick, 1.0, 0.0), ((0,), (0,)))
-    mine = iota(lanes.shape, 1) % chunk == iota(lanes.shape, 0)
-    place = jnp.sum(jnp.where(mine, lanes, 0.0), axis=0, keepdims=True)
+def landed(room, chunk, cells, got_ref, rows_of):
+    total = got_ref.shape[0]
+    parts, slots, _ = rows_of.shape
+    blocks = total // chunk
+    places = got_ref[pl.ds(chunk - 1, blocks, stride=chunk), :]
+    for source in range(blocks):
+        for part in range(parts):
+            start = source * chunk + part * room
+            rows_of[part, source * room : source * room + room, :] = got_ref[start : start + room, :]
+    pick = jnp.where(iota((blocks, slots), 1) // room == iota((blocks, slots), 0), 1.0, 0.0)
+    lanes = dot(places, pick, ((0,), (0,)))
+    mine = iota(lanes.shape, 1) % room == iota(lanes.shape, 0)
+    place = jnp.sum(jnp.where(mine, lanes, 0.0), axis=0, keepdims=True).astype(jnp.int32)
+    landing = jnp.where(iota((cells, slots), 0) + 1 == place, 1.0, 0.0)
+    return [selected(landing, rows_of[part]) for part in range(parts)]
+
+
+def land(room, chunk, got_ref, force, rows_of):
     rows, cols, _ = force.shape
-    cells = rows * cols
-    landing = jnp.where(iota((cells, total), 0) + 1 == place.astype(jnp.int32), 1.0, 0.0)
-    force[...] = selected(landing, got).reshape(rows, cols, depth)
-
-
-def last_steps(force, free, after_free, l_ref, shear, viscosity, up, down, left, right, mid, new):
-    rows, cols, depth = force.shape
+    for part, x in enumerate(landed(room, chunk, rows * cols, got_ref, rows_of)):
+        force[:, :, part * 128 : part * 128 + 128] = x.reshape(rows, cols, 128)
+
+
+def tissue_steps(force, free, after_free, l_ref, shear, viscosity, up, down, left, right, mid, new):
+    rows = force.shape[0]
 
     def step(i, f_up, f_down):
         f = force[i]
@@ -419,6 +475,26 @@
         return carry
 
     lax.fori_loop(1, rows - 1, body, 0)
+
+
+def land_and_step(
+    room, chunk, got_ref, free, after_free, l_ref, shear, viscosity, force, mid, new,
+    rows_of, up, down, left, right
+):
+    rows, cols, _ = force.shape
+    cells = rows * cols
+    borders, start = [], cells
+    for ref in (up, down, left, right):
+        borders.append((ref, start))
+        start += ref.shape[0]
+    for part, x in enumerate(landed(room, chunk, start, got_ref, rows_of)):
+        lanes = slice(part * 128, part * 128 + 128)
+        force[:, :, lanes] = x[:cells].reshape(rows, cols, 128)
+        for ref, first in borders:
+            ref[:, lanes] = x[first : first + ref.shape[0]]
+    tissue_steps(
+        force, free, after_free, l_ref, shear, viscosity, up, down, left, right, mid, new
+    )
 
 
 def swap(first, last, axis):
@@ -485,6 +561,19 @@
         compiler_params=pltpu.CompilerParams(vmem_limit_bytes=55 << 20),
     )(*[x for x, _ in fields], shear_table, viscosity_table)
     before, after = swap(first, last, "gx")
+    grid = (lax.axis_size("gx"), lax.axis_size("gy"))
+    blocks = grid[0] * grid[1]
+    capacity = max(2, deep // 2 * (across // 2) // blocks)
+    parts = depth // 128
+    room = 2 * capacity + 1
+    chunk = -(-(room * parts + 1) // 8) * 8
+    count = own_map.size
+    match, placed = run(
+        functools.partial(address, grid, (rows, cols), room, chunk),
+        (f32(blocks * chunk, parts * count), f32(blocks * chunk, 128)),
+        own_map.T,
+        slot_table.T,
+    )
     inputs = tuple(x for x, _ in fields) + (shear_table, viscosity_table, before, after)
     side = 3 * deep + 8 + 2 * rows
     first, last = run(border_columns, (f32(side, span),) * 2, *inputs, tables=(8, 9))
@@ -492,25 +581,27 @@
     mid, free = run(
         first_steps, (f32(deep, across, span), f32(rows, cols, depth)), *inputs, tables=(8, 9)
     )
-    blocks = lax.axis_size("gx") * lax.axis_size("gy")
-    capacity = max(2, deep // 2 * (across // 2) // blocks)
-    chunk = -(-(capacity + 1) // 8) * 8
     pressure_mid, pressure_new, send = run(
-        functools.partial(second_acoustic, blocks, capacity, chunk),
-        (f32(deep, across, span), f32(deep, across, span), f32(blocks * chunk, depth)),
+        second_acoustic,
+        (f32(deep, across, span), f32(deep, across, span), f32(blocks * chunk, 128)),
         mid,
         pressure,
         courant,
         nonlinearity,
         absorption,
-        own_map.T,
-        slot_table.T,
+        match,
+        placed,
         before,
         after,
         left,
         right,
-        scratch_shapes=[scratch(deep, span), scratch(deep, span), scratch(span // 128, deep // 2 * across, 128)],
-    )
+        scratch_shapes=[
+            scratch(deep, span),
+            scratch(deep, span),
+            scratch(span // 128, deep // 2 * across, 128),
+        ],
+    )
+    send = send.reshape(blocks, chunk, 128)
     got = lax.all_to_all(send, ("gx", "gy"), split_axis=0, concat_axis=0, tiled=True)
     free, after_free = run(
         second_elastic,
@@ -528,23 +619,48 @@
         scratch_shapes=[scratch(rows, depth)] * 4,
         tables=(4, 5),
     )
-    tissue_force = run(functools.partial(land, capacity, chunk), f32(rows, cols, depth), got)
-    up, down = swap(tissue_force[0], tissue_force[rows - 1], "gx")
-    beside_l, beside_r = swap(tissue_force[:, 0], tissue_force[:, cols - 1], "gy")
-    displacement_mid, displacement_new = run(
-        last_steps,
-        (f32(rows, cols, depth),) * 2,
-        tissue_force,
+    whole_block = f32(rows, cols, depth)
+    arrived = scratch(depth // 128, blocks * room, 128)
+
+    def direct(got, *rest):
+        return run(
+            functools.partial(land_and_step, room, chunk),
+            (whole_block,) * 3,
+            got,
+            *rest,
+            scratch_shapes=[arrived] + [scratch(n, depth) for n in (cols, cols, rows, rows)],
+            tables=(4, 5),
+        )
+
+    def by_faces(got, *rest):
+        force = run(
+            functools.partial(land, room, chunk), whole_block, got, scratch_shapes=[arrived]
+        )
+        up, down = swap(force[0], force[rows - 1], "gx")
+        at_left, at_right = swap(force[:, 0], force[:, cols - 1], "gy")
+        mid, new = run(
+            tissue_steps,
+            (whole_block,) * 2,
+            force,
+            *rest,
+            up,
+            down,
+            at_left,
+            at_right,
+            tables=(4, 5),
+        )
+        return force, mid, new
+
+    tissue_force, displacement_mid, displacement_new = lax.cond(
+        jnp.max(got[:, chunk - 1, room]) > 0.0,
+        by_faces,
+        direct,
+        got.reshape(blocks * chunk, 128),
         free,
         after_free,
         layer_labels,
         shear_table,
         viscosity_table,
-        up,
-        down,
-        beside_l,
-        beside_r,
-        tables=(4, 5),
     )
     return (pressure_mid, pressure_new, tissue_force, displacement_mid, displacement_new)
 

time: 67.1 us -> 59.5 us (0.89)
  blocking collectives: 16.5 us -> 0 us
  Pallas kernels: 21.3 us -> 25.4 us
  starting transfers between devices: 17 us -> 18.5 us
  local copies, waits for them, and re-layouts: 1.96 us -> 3.16 us
  other arithmetic: 0 us -> 0.69 us
  waiting for transfers between devices: 8.9 us -> 9.59 us
    all_to_all x1 -> x0, blocking collectives: 16.5 us -> none  [local(): lax.all_to_all(send, ('gx', 'gy'), split_axis=0, concat_axis=0, tiled=True)]
    all_to_all x0 -> x1, starting transfers between devices: none -> 9.88 us  [local(): lax.all_to_all(send, ('gx', 'gy'), split_axis=0, concat_axis=0, tiled=True)]
    ppermute x8 -> x4, starting transfers between devices: 17 us -> 8.63 us  [swap(): return (lax.ppermute(last, axis, up), lax.ppermute(first, axis, down))]
    pallas_call x6, Pallas kernels: 17.6 us -> 21.8 us  [run(): pl.pallas_call(kernel, out_shape=out, in_specs=specs, out_specs=jax.tree....]
    all_to_all x0 -> x1, waiting for transfers between devices: none -> 4.06 us  [local(): lax.all_to_all(send, ('gx', 'gy'), split_axis=0, concat_axis=0, tiled=True)]
    ppermute x8 -> x4, waiting for transfers between devices: 8.9 us -> 5.52 us  [swap(): return (lax.ppermute(last, axis, up), lax.ppermute(first, axis, down))]
    unnamed x28 -> x38, local copies, waits for them, and re-layouts: 0.07 us -> 3.16 us
    slice x1 -> x0, local copies, waits for them, and re-layouts: 1.06 us -> none  [local(): tissue_force[:, 0]]
  transfers between devices with their start and end apart: 8 -> 5, of which waited for: 4 -> 3; matrix products, arithmetic and copies ran while one was open for 2% -> 0% of each run, Pallas kernels for 12% -> 19%
where the time goes in v2:
time: 59.5 us; the launch traced here: 59 us
  Pallas kernels  25.4 us (43%)
  starting transfers between devices  18.5 us (31%)
  waiting for transfers between devices  9.59 us (16%)
  local copies, waits for them, and re-layouts  3.16 us (5%)
  between operations  1.58 us (3%)
  other arithmetic  0.69 us (1%)
    pallas_call x6, Pallas kernels, run(): pl.pallas_call(kernel, out_shape=out, in_specs=specs, out_specs=jax.tree....  21.8 us
    all_to_all x1, starting transfers between devices, local(): lax.all_to_all(send, ('gx', 'gy'), split_axis=0, concat_axis=0, tiled=True)  9.88 us
    ppermute x4, starting transfers between devices, swap(): return (lax.ppermute(last, axis, up), lax.ppermute(first, axis, down))  8.63 us
    ppermute x4, waiting for transfers between devices, swap(): return (lax.ppermute(last, axis, up), lax.ppermute(first, axis, down))  5.52 us
    all_to_all x1, waiting for transfers between devices, local(): lax.all_to_all(send, ('gx', 'gy'), split_axis=0, concat_axis=0, tiled=True)  4.06 us
    pallas_call x1, Pallas kernels, local(): pl.pallas_call(border_rows, out_shape=(f32(face, span), f32(face, span)),...  3.67 us
    unnamed x38, local copies, waits for them, and re-layouts  3.16 us
  transfers between devices with their start and end apart: 5, of which 3 were waited for; matrix products, arithmetic and copies ran while one was open for 0% of the time, Pallas kernels for 19%

profile of v2, /device:TPU:0, one launch (start us, length us, event | category | flops | bytes accessed | tf_op | source)
XLA Modules:
  0.0 59.0 jit_solution(6877995622213210639)
XLA Ops:
  0.7 3.7 %shard_map.155 = (f32[112,768]{1,0:T(8,128)}, f32[112,768]{1,0:T(8,128)}) custom-call(f32[24,16,768]{2,1,0:T(8,128)} %p_ref.5, f32[24,16,768]{2,1,0:T(8,128)} %q_ref.3, f32[24,16,768]{2,1,0:T(8,128)} %c_ref.5, f32[24,16,768]{2,1,0:T(8,128)} %n_ref.5, f32[24,16,768]{2,1,0:T(8,128)} %a_ref.5, f32[16,32,384]{2,1,0:T(8,128)} %d_ref.5, f32[16,32,384]{2,1,0:T(8,128)} %b_ref.5, ...), custom_call_target="tpu_custom_call" | custom-call | tf_op jit(solution)/shard_map/pallas_call | solution.py:552
  4.4 2.4 %collective-permute-start.4 = (f32[112,768]{1,0:T(8,128)}, f32[112,768]{1,0:T(8,128)S(1)}, u32[]{:S(2)}, u32[]{:S(2)}) collective-permute-start(f32[112,768]{1,0:T(8,128)} %get-tuple-element.59), channel_id=1, source_target_pairs={{0,4},{4,8},{8,12},{1,5},{5,9},{9,13},{2,6},{6,10},{10,14},{3,7},{... | collective-permute-start | bytes 1032200 | tf_op jit(solution)/shard_map/ppermute | solution.py:504
  6.8 0.0 copy-start.13
  6.8 0.0 copy-start.15
  6.9 1.4 %collective-permute-start.5 = (f32[112,768]{1,0:T(8,128)}, f32[112,768]{1,0:T(8,128)S(1)}, u32[]{:S(2)}, u32[]{:S(2)}) collective-permute-start(f32[112,768]{1,0:T(8,128)} %get-tuple-element.60), channel_id=1, source_target_pairs={{4,0},{8,4},{12,8},{5,1},{9,5},{13,9},{6,2},{10,6},{14,10},{7,3},{... | collective-permute-start | bytes 1032200 | tf_op jit(solution)/shard_map/ppermute | solution.py:504
  8.3 4.5 %collective-permute-done.5.after = f32[112,768]{1,0:T(8,128)S(1)} collective-permute-done((f32[112,768]{1,0:T(8,128)}, f32[112,768]{1,0:T(8,128)S(1)}, u32[]{:S(2)}, u32[]{:S(2)}) %collective-permute-start.5) | collective-permute-done | bytes 344096 | tf_op jit(solution)/shard_map/ppermute | solution.py:504
  12.9 2.0 %shard_map.158 = (f32[112,768]{1,0:T(8,128)S(1)}, f32[112,768]{1,0:T(8,128)S(1)}) custom-call(f32[24,16,768]{2,1,0:T(8,128)S(1)} %copy-done, f32[24,16,768]{2,1,0:T(8,128)S(1)} %copy-done.6, f32[24,16,768]{2,1,0:T(8,128)S(1)} %copy-done.1, f32[24,16,768]{2,1,0:T(8,128)S(1)} %copy-done.2, f32[24,16,768]{2,1,0:T(8,128)S(1)} %copy-done.3, ...), custom_call_target="tpu_custom_call" | custom-call | flops 192676480 | bytes 9633824 | tf_op jit(solution)/shard_map/pallas_call | solution.py:531
  14.9 3.5 %collective-permute-start.6 = (f32[112,768]{1,0:T(8,128)S(1)}, f32[112,768]{1,0:T(8,128)S(1)}, u32[]{:S(2)}, u32[]{:S(2)}) collective-permute-start(f32[112,768]{1,0:T(8,128)S(1)} %get-tuple-element.64), channel_id=1, source_target_pairs={{0,1},{1,2},{2,3},{4,5},{5,6},{6,7},{8,9},{9,10},{10,11},{12,13},{... | collective-permute-start | bytes 1032200 | tf_op jit(solution)/shard_map/ppermute | solution.py:504
  18.4 1.3 %collective-permute-start.7 = (f32[112,768]{1,0:T(8,128)S(1)}, f32[112,768]{1,0:T(8,128)S(1)}, u32[]{:S(2)}, u32[]{:S(2)}) collective-permute-start(f32[112,768]{1,0:T(8,128)S(1)} %get-tuple-element.65), channel_id=1, source_target_pairs={{1,0},{2,1},{3,2},{5,4},{6,5},{7,6},{9,8},{10,9},{11,10},{13,12},{... | collective-permute-start | bytes 1032200 | tf_op jit(solution)/shard_map/ppermute | solution.py:504
  19.7 1.8 %shard_map.157 = (f32[640,288]{1,0:T(8,128)S(1)}, f32[640,128]{1,0:T(8,128)S(1)}) custom-call(s32[8,12]{1,0:T(8,128)S(1)} %bitcast.14, s32[8,12]{1,0:T(8,128)S(1)} %bitcast.15), custom_call_target="tpu_custom_call" | custom-call | flops 21314560 | bytes 1065728 | tf_op jit(solution)/shard_map/pallas_call | solution.py:531
  21.5 5.0 %shard_map.156 = (f32[24,16,768]{2,1,0:T(8,128)S(1)}, f32[16,32,384]{2,1,0:T(8,128)S(1)}) custom-call(f32[24,16,768]{2,1,0:T(8,128)S(1)} %copy-done, f32[24,16,768]{2,1,0:T(8,128)S(1)} %copy-done.6, f32[24,16,768]{2,1,0:T(8,128)S(1)} %copy-done.1, f32[24,16,768]{2,1,0:T(8,128)S(1)} %copy-done.2, f32[24,16,768]{2,1,0:T(8,128)S(1)} %copy-done.3, ...), custom_call_target="tpu_custom_call" | custom-call | flops 218235520 | bytes 10911776 | tf_op jit(solution)/shard_map/pallas_call | solution.py:531
  26.5 0.0 copy-start.7
  26.5 1.0 %collective-permute-done.7.right = f32[112,768]{1,0:T(8,128)S(1)} collective-permute-done((f32[112,768]{1,0:T(8,128)S(1)}, f32[112,768]{1,0:T(8,128)S(1)}, u32[]{:S(2)}, u32[]{:S(2)}) %collective-permute-start.7) | collective-permute-done | bytes 344096 | tf_op jit(solution)/shard_map/ppermute | solution.py:504
  27.5 3.4 %shard_map.159 = (f32[24,16,768]{2,1,0:T(8,128)}, f32[24,16,768]{2,1,0:T(8,128)}, f32[640,128]{1,0:T(8,128)}) custom-call(f32[24,16,768]{2,1,0:T(8,128)S(1)} %get-tuple-element.61.mid_ref, f32[24,16,768]{2,1,0:T(8,128)S(1)} %copy-done, f32[24,16,768]{2,1,0:T(8,128)S(1)} %copy-done.1, f32[24,16,768]{2,1,0:T(8,128)S(1)} %copy-done.2, ...), custom_call_target="tpu_custom_call" | custom-call | flops 220528640 | bytes 11026432 | tf_op jit(solution)/shard_map/pallas_call | solution.py:531
  31.0 9.9 %all-to-all-start = ((f32[16,40,128]{2,1,0:T(8,128)}), f32[16,40,128]{2,1,0:T(8,128)S(1)}, u32[]{:S(2)}, u32[]{:S(2)}) async-start(f32[16,40,128]{2,1,0:T(8,128)} %bitcast.6), calls=%async_computation | async-start | bytes 655360 | tf_op jit(solution)/shard_map/all_to_all | solution.py:605
  40.9 0.0 copy-start.8
  40.9 1.0 %copy-done.8 = f32[112,768]{1,0:T(8,128)S(1)} copy-done((f32[112,768]{1,0:T(8,128)S(1)}, f32[112,768]{1,0:T(8,128)}, u32[]{:S(2)}) %copy-start.8) | copy-done | bytes 344088
  41.9 1.0 %copy-done.10 = f32[112,768]{1,0:T(8,128)S(1)} copy-done((f32[112,768]{1,0:T(8,128)S(1)}, f32[112,768]{1,0:T(8,128)}, u32[]{:S(2)}) %copy-start.10) | copy-done | bytes 344088
  42.9 1.1 %copy-done.12 = f32[16,32,384]{2,1,0:T(8,128)S(1)} copy-done((f32[16,32,384]{2,1,0:T(8,128)S(1)}, f32[16,32,384]{2,1,0:T(8,128)}, u32[]{:S(2)}) %copy-start.12) | copy-done | bytes 786456
  44.0 4.2 %shard_map.160 = (f32[16,32,384]{2,1,0:T(8,128)}, f32[16,32,384]{2,1,0:T(8,128)}) custom-call(f32[16,32,384]{2,1,0:T(8,128)S(1)} %copy-done.12, f32[16,32,384]{2,1,0:T(8,128)S(1)} %copy-done.4, f32[16,32,384]{2,1,0:T(8,128)S(1)} %copy-done.5, s32[16,32,384]{2,1,0:T(8,128)S(1)} %copy-done.16, f32[4]{0:T(128)S(1)} %copy-done.18, f32[4]{0:T(128)S(1)} %copy-done.19, ...), custom_call_target="tpu_custom_call" | custom-call | flops 121897600 | bytes 6094880 | tf_op jit(solution)/shard_map/pallas_call | solution.py:531
  48.2 4.1 %all-to-all-done = f32[16,40,128]{2,1,0:T(8,128)S(1)} async-done(((f32[16,40,128]{2,1,0:T(8,128)}), f32[16,40,128]{2,1,0:T(8,128)S(1)}, u32[]{:S(2)}, u32[]{:S(2)}) %all-to-all-start) | async-done | bytes 327712 | tf_op jit(solution)/shard_map/all_to_all | solution.py:605
  52.2 0.7 %slice_reduce_fusion = f32[]{:T(128)} fusion(f32[16,40,128]{2,1,0:T(8,128)S(1)} %all-to-all-done), kind=kLoop, calls=%fused_computation.4 | loop fusion | flops 15 | bytes 68 | tf_op jit(solution)/shard_map/reduce_max | solution.py:655
  53.6 5.4 %conditional.1 = ((f32[16,32,384]{2,1,0:T(8,128)}, f32[16,32,384]{2,1,0:T(8,128)}, f32[16,32,384]{2,1,0:T(8,128)})) conditional(s32[]{:T(128)} %convert_element_type.3, (f32[640,128]{1,0:T(8,128)S(1)}, f32[16,32,384]{2,1,0:T(8,128)}, f32[16,32,384]{2,1,0:T(8,128)}, s32[16,32,384]{2,1,0:T(8,128)S(1)}, f32[4]{0:T(128)S(1)}, ...), branch_computations={%region_1.0_spmd, %region_2.0_spmd} | conditional | flops 119603840 | bytes 10109180 | solution.py:654
  53.6 5.4 %branch_0_fun.1 = (f32[16,32,384]{2,1,0:T(8,128)}, f32[16,32,384]{2,1,0:T(8,128)}, f32[16,32,384]{2,1,0:T(8,128)}) custom-call(f32[640,128]{1,0:T(8,128)S(1)} %get-tuple-element.24.got_ref, f32[16,32,384]{2,1,0:T(8,128)} %get-tuple-element.25.free, f32[16,32,384]{2,1,0:T(8,128)} %get-tuple-element.26.after_free, s32[16,32,384]{2,1,0:T(8,128)S(1)} %get-tuple-element.27.l_ref, ...), custom_call_target="tpu_custom_call" | custom-call | flops 100926080 | bytes 5046304 | tf_op jit(solution)/shard_map/cond/branch_0_fun/pallas_call | solution.py:531
  (33 shorter events, 0.1 us)
Async XLA Ops:
  0.6 12.2 %copy-start.19 = (f32[4]{0:T(128)S(1)}, f32[4]{0:T(128)}, u32[]{:S(2)}) copy-start(f32[4]{0:T(128)} %viscosity.5) | copy-start | bytes 52
  0.6 12.2 %copy-start.18 = (f32[4]{0:T(128)S(1)}, f32[4]{0:T(128)}, u32[]{:S(2)}) copy-start(f32[4]{0:T(128)} %shear.5) | copy-start | bytes 52
  0.7 12.2 %copy-start.5 = (f32[16,32,384]{2,1,0:T(8,128)S(1)}, f32[16,32,384]{2,1,0:T(8,128)}, u32[]{:S(2)}) copy-start(f32[16,32,384]{2,1,0:T(8,128)} %b_ref.5) | copy-start | bytes 2359300
  0.7 12.2 %copy-start.4 = (f32[16,32,384]{2,1,0:T(8,128)S(1)}, f32[16,32,384]{2,1,0:T(8,128)}, u32[]{:S(2)}) copy-start(f32[16,32,384]{2,1,0:T(8,128)} %d_ref.5) | copy-start | bytes 2359300
  0.7 12.2 %copy-start.3 = (f32[24,16,768]{2,1,0:T(8,128)S(1)}, f32[24,16,768]{2,1,0:T(8,128)}, u32[]{:S(2)}) copy-start(f32[24,16,768]{2,1,0:T(8,128)} %a_ref.5) | copy-start | bytes 3538948
  0.7 12.2 %copy-start.2 = (f32[24,16,768]{2,1,0:T(8,128)S(1)}, f32[24,16,768]{2,1,0:T(8,128)}, u32[]{:S(2)}) copy-start(f32[24,16,768]{2,1,0:T(8,128)} %n_ref.5) | copy-start | bytes 3538948
  0.7 12.2 %copy-start.1 = (f32[24,16,768]{2,1,0:T(8,128)S(1)}, f32[24,16,768]{2,1,0:T(8,128)}, u32[]{:S(2)}) copy-start(f32[24,16,768]{2,1,0:T(8,128)} %c_ref.5) | copy-start | bytes 3538948
  0.7 12.2 %copy-start = (f32[24,16,768]{2,1,0:T(8,128)S(1)}, f32[24,16,768]{2,1,0:T(8,128)}, u32[]{:S(2)}) copy-start(f32[24,16,768]{2,1,0:T(8,128)} %p_ref.5) | copy-start | bytes 3538948
  0.7 12.2 %copy-start.6 = (f32[24,16,768]{2,1,0:T(8,128)S(1)}, f32[24,16,768]{2,1,0:T(8,128)}, u32[]{:S(2)}) copy-start(f32[24,16,768]{2,1,0:T(8,128)} %q_ref.3) | copy-start | bytes 3538948
  4.4 3.9 %collective-permute-start.4 = (f32[112,768]{1,0:T(8,128)}, f32[112,768]{1,0:T(8,128)S(1)}, u32[]{:S(2)}, u32[]{:S(2)}) collective-permute-start(f32[112,768]{1,0:T(8,128)} %get-tuple-element.59), channel_id=1, source_target_pairs={{0,4},{4,8},{8,12},{1,5},{5,9},{9,13},{2,6},{6,10},{10,14},{3,7},{... | collective-permute-start | bytes 1032200 | tf_op jit(solution)/shard_map/ppermute | solution.py:504
  6.8 12.9 %copy-start.13 = (s32[12,8]{0,1:T(8,128)S(1)}, s32[12,8]{0,1:T(8,128)}, u32[]{:S(2)}) copy-start(s32[12,8]{0,1:T(8,128)} %param.19) | copy-start | bytes 1156
  6.8 12.9 %copy-start.14 = (s32[12,8]{0,1:T(8,128)S(1)}, s32[12,8]{0,1:T(8,128)}, u32[]{:S(2)}) copy-start(s32[12,8]{0,1:T(8,128)} %param.20) | copy-start | bytes 1156
  6.8 14.7 %copy-start.15 = (s32[16,32,384]{2,1,0:T(8,128)S(1)}, s32[16,32,384]{2,1,0:T(8,128)}, u32[]{:S(2)}) copy-start(s32[16,32,384]{2,1,0:T(8,128)} %l_ref.5) | copy-start | bytes 2359300
  6.9 6.0 %collective-permute-start.5 = (f32[112,768]{1,0:T(8,128)}, f32[112,768]{1,0:T(8,128)S(1)}, u32[]{:S(2)}, u32[]{:S(2)}) collective-permute-start(f32[112,768]{1,0:T(8,128)} %get-tuple-element.60), channel_id=1, source_target_pairs={{4,0},{8,4},{12,8},{5,1},{9,5},{13,9},{6,2},{10,6},{14,10},{7,3},{... | collective-permute-start | bytes 1032200 | tf_op jit(solution)/shard_map/ppermute | solution.py:504
  14.9 11.6 %collective-permute-start.6 = (f32[112,768]{1,0:T(8,128)S(1)}, f32[112,768]{1,0:T(8,128)S(1)}, u32[]{:S(2)}, u32[]{:S(2)}) collective-permute-start(f32[112,768]{1,0:T(8,128)S(1)} %get-tuple-element.64), channel_id=1, source_target_pairs={{0,1},{1,2},{2,3},{4,5},{5,6},{6,7},{8,9},{9,10},{10,11},{12,13},{... | collective-permute-start | bytes 1032200 | tf_op jit(solution)/shard_map/ppermute | solution.py:504
  18.4 9.1 %collective-permute-start.7 = (f32[112,768]{1,0:T(8,128)S(1)}, f32[112,768]{1,0:T(8,128)S(1)}, u32[]{:S(2)}, u32[]{:S(2)}) collective-permute-start(f32[112,768]{1,0:T(8,128)S(1)} %get-tuple-element.65), channel_id=1, source_target_pairs={{1,0},{2,1},{3,2},{5,4},{6,5},{7,6},{9,8},{10,9},{11,10},{13,12},{... | collective-permute-start | bytes 1032200 | tf_op jit(solution)/shard_map/ppermute | solution.py:504
  26.5 4.5 %copy-start.11 = (f32[16,32,384]{2,1,0:T(8,128)}, f32[16,32,384]{2,1,0:T(8,128)S(1)}, u32[]{:S(2)}) copy-start(f32[16,32,384]{2,1,0:T(8,128)S(1)} %get-tuple-element.69.free_ref) | copy-start | bytes 2359300
  26.5 4.5 %copy-start.7 = (f32[112,768]{1,0:T(8,128)}, f32[112,768]{1,0:T(8,128)S(1)}, u32[]{:S(2)}) copy-start(f32[112,768]{1,0:T(8,128)S(1)} %collective-permute-done.6.left) | copy-start | bytes 1032196
  27.5 3.5 %copy-start.9 = (f32[112,768]{1,0:T(8,128)}, f32[112,768]{1,0:T(8,128)S(1)}, u32[]{:S(2)}) copy-start(f32[112,768]{1,0:T(8,128)S(1)} %collective-permute-done.7.right) | copy-start | bytes 1032196
  27.5 13.4 %copy-start.16 = (s32[16,32,384]{2,1,0:T(8,128)S(1)}, s32[16,32,384]{2,1,0:T(8,128)}, u32[]{:S(2)}) copy-start(s32[16,32,384]{2,1,0:T(8,128)} %l_ref.5) | copy-start | bytes 2359300
  31.0 21.2 %all-to-all-start = ((f32[16,40,128]{2,1,0:T(8,128)}), f32[16,40,128]{2,1,0:T(8,128)S(1)}, u32[]{:S(2)}, u32[]{:S(2)}) async-start(f32[16,40,128]{2,1,0:T(8,128)} %bitcast.6), calls=%async_computation | async-start | bytes 655360 | tf_op jit(solution)/shard_map/all_to_all | solution.py:605
  40.9 1.0 %copy-start.8 = (f32[112,768]{1,0:T(8,128)S(1)}, f32[112,768]{1,0:T(8,128)}, u32[]{:S(2)}) copy-start(f32[112,768]{1,0:T(8,128)} %copy-done.7) | copy-start | bytes 1032196
  41.9 1.0 %copy-start.10 = (f32[112,768]{1,0:T(8,128)S(1)}, f32[112,768]{1,0:T(8,128)}, u32[]{:S(2)}) copy-start(f32[112,768]{1,0:T(8,128)} %copy-done.9) | copy-start | bytes 1032196
  42.9 1.1 %copy-start.12 = (f32[16,32,384]{2,1,0:T(8,128)S(1)}, f32[16,32,384]{2,1,0:T(8,128)}, u32[]{:S(2)}) copy-start(f32[16,32,384]{2,1,0:T(8,128)} %copy-done.11) | copy-start | bytes 2359300

commit v3 on v2

v3 whole, which is shorter than its diff:
```python
import functools
import math

import jax
import jax.numpy as jnp
from jax import lax
from jax.experimental import pallas as pl
from jax.experimental.pallas import tpu as pltpu
from jax.sharding import PartitionSpec as P

VMEM = pl.BlockSpec(memory_space=pltpu.VMEM)
SMEM = pl.BlockSpec(memory_space=pltpu.SMEM)
EXACT = lax.Precision.HIGHEST


def lateral(x):
    dim, size = x.ndim - 1, x.shape[-1]
    lane = lax.broadcasted_iota(jnp.int32, x.shape, dim)
    lower = jnp.where(lane == 0, 0.0, pltpu.roll(x, 1, dim))
    upper = jnp.where(lane == size - 1, 0.0, pltpu.roll(x, size - 1, dim))
    return lower + upper


def beside(x, before, after):
    size = x.shape[0]
    row = lax.broadcasted_iota(jnp.int32, x.shape, 0)
    up = jnp.where(row == 0, before, pltpu.roll(x, 1, 0))
    down = jnp.where(row == size - 1, after, pltpu.roll(x, size - 1, 0))
    return up + down


def at_ends(shape, first, last):
    row = lax.broadcasted_iota(jnp.int32, shape, 0)
    return jnp.where(row == 0, first, jnp.where(row == shape[0] - 1, last, 0.0))


def wave(now, before, lap, courant, nonlinearity, absorption):
    return (
        2.0 * now
        - before
        + courant * lap
        + nonlinearity * (now * now - before * before)
        - 0.1 * absorption * (now - before)
    )


def lookup(kinds, table, first):
    result = jnp.zeros(kinds.shape, jnp.float32)
    for kind in range(table.shape[0]):
        result = jnp.where(kinds == kind + first, table[kind], result)
    return result


def halves(ref, base, x):
    half, depth = x.shape[0] // 2, x.shape[1]
    ref[base : base + half, 0:depth] = x[:half]
    ref[base : base + half, depth : 2 * depth] = x[half:]


def whole(ref, base, half, depth):
    return jnp.concatenate(
        [ref[base : base + half, 0:depth], ref[base : base + half, depth : 2 * depth]], axis=0
    )


def border_columns(inner, *refs):
    count = len(inner)
    fields, (shear, viscosity, left, right) = refs[:count], refs[count : count + 4]
    buffers, sems = refs[count + 4 : -1], refs[-1]
    copies, sides, k = [], ([], []), 0
    for field, more in zip(fields, inner):
        last = field.shape[1] - 1
        for side, js in enumerate(((0, 1)[: 1 + more], (last, last - 1)[: 1 + more])):
            for j in js:
                copies.append(pltpu.make_async_copy(field.at[:, j, :], buffers[k], sems.at[k]))
                sides[side].append(buffers[k])
                k += 1
    for copy in copies:
        copy.start()
    for copy in copies:
        copy.wait()
    for columns, out in zip(sides, (left, right)):
        p, p_in, q, c, n, a, d, d_in, b, b_in, labels = [column[...] for column in columns]
        deep, (rows, depth) = p.shape[0], d.shape
        lap = beside(p, 0.0, 0.0) + p_in + lateral(p) - 6.0 * p
        out[0:deep] = p
        out[deep : 2 * deep] = c
        out[2 * deep : 3 * deep] = wave(p, q, lap, c, n, a)
        e, e_in = d - b, d_in - b_in
        s, v = lookup(labels, shear, 0), lookup(labels, viscosity, 0)
        lap_d = beside(d, 0.0, 0.0) + d_in + lateral(d) - 6.0 * d
        lap_e = beside(e, 0.0, 0.0) + e_in + lateral(e) - 6.0 * e
        top = 3 * deep
        first, last = slice(0, depth), slice(depth, 2 * depth)
        out[top : top + rows, first] = d
        out[top : top + rows, last] = e
        out[top + rows : top + 2 * rows, first] = labels.astype(jnp.float32) + 1.0
        out[top + rows : top + 2 * rows, last] = d + e + s * lap_d + v * lap_e


def cover(_, out):
    out[...] = jnp.zeros_like(out)


def first_steps(p_ref, q_ref, c_ref, n_ref, a_ref, d_ref, b_ref, l_ref, shear, viscosity, _, mid, free):
    deep, rows = p_ref.shape[0], d_ref.shape[0]

    def acoustic(i, p_up, p_down):
        p = p_ref[i]
        lap = p_up + p_down + beside(p, 0.0, 0.0) + lateral(p) - 6.0 * p
        mid[i] = wave(p, q_ref[i], lap, c_ref[i], n_ref[i], a_ref[i])

    acoustic(0, 0.0, p_ref[1])
    acoustic(deep - 1, p_ref[deep - 2], 0.0)

    def acoustic_body(i, carry):
        acoustic(i, p_ref[i - 1], p_ref[i + 1])
        return carry

    lax.fori_loop(1, deep - 1, acoustic_body, 0)

    def elastic(i, d_up, d_down, e_up, e_down):
        d = d_ref[i]
        e = d - b_ref[i]
        s, v = lookup(l_ref[i], shear, 0), lookup(l_ref[i], viscosity, 0)
        lap_d = d_up + d_down + beside(d, 0.0, 0.0) + lateral(d) - 6.0 * d
        lap_e = e_up + e_down + beside(e, 0.0, 0.0) + lateral(e) - 6.0 * e
        free[i] = d + e + s * lap_d + v * lap_e

    change = lambda i: d_ref[i] - b_ref[i]
    elastic(0, 0.0, d_ref[1], 0.0, change(1))
    elastic(rows - 1, d_ref[rows - 2], 0.0, change(rows - 2), 0.0)

    def elastic_body(i, carry):
        elastic(i, d_ref[i - 1], d_ref[i + 1], change(i - 1), change(i + 1))
        return carry

    lax.fori_loop(1, rows - 1, elastic_body, 0)


def border_rows(
    p_ref, c_ref, mid_ref, d_ref, b_ref, l_ref, free_ref, shear, viscosity, left, right, up, down
):
    deep, across, _ = p_ref.shape
    rows, cols, depth = d_ref.shape
    half = cols // 2
    top, base, end = 3 * deep, 3 * across, 3 * across + 2 * cols
    first, last = slice(0, depth), slice(depth, 2 * depth)
    for i, k, out in ((0, 0, up), (deep - 1, rows - 1, down)):
        p, c = p_ref[i], c_ref[i]
        p_left, p_right = left[i : i + 1], right[i : i + 1]
        out[0:across] = p
        out[across : 2 * across] = c
        out[2 * across : 3 * across] = mid_ref[i] + c * at_ends(c.shape, p_left, p_right)
        d, labels = d_ref[k], l_ref[k]
        s, v = lookup(labels, shear, 0), lookup(labels, viscosity, 0)
        at = slice(top + k, top + k + 1)
        d_ends = at_ends(d.shape, left[at, first], right[at, first])
        e_ends = at_ends(d.shape, left[at, last], right[at, last])
        halves(out, base, d)
        halves(out, base + half, d - b_ref[k])
        halves(out, base + 2 * half, free_ref[k] + s * d_ends + v * e_ends)
        halves(out, base + 3 * half, labels.astype(jnp.float32) + 1.0)
        out[end : end + 1] = p_left
        out[end + 1 : end + 2] = p_right
        out[end + 2 : end + 3] = left[at]
        out[end + 3 : end + 4] = right[at]
        out[end + 4 : end + 8] = jnp.zeros((4, out.shape[1]), jnp.float32)


def dot(x, y, contract=((1,), (0,))):
    return lax.dot_general(
        x, y, (contract, ((), ())), precision=EXACT, preferred_element_type=jnp.float32
    )


def selected(x, y):
    high = y.astype(jnp.bfloat16)
    low = (y - high.astype(jnp.float32)).astype(jnp.bfloat16)
    x = x.astype(jnp.bfloat16)
    product = functools.partial(jnp.dot, preferred_element_type=jnp.float32)
    return product(x, high) + product(x, low)


def iota(shape, dim):
    return lax.broadcasted_iota(jnp.int32, shape, dim)


def address(grid, tile, room, chunk, own_ref, slot_ref, _, match, placed):
    (tiles_down, tiles_across), (rows, cols) = grid, tile
    blocks, cells = tiles_down * tiles_across, rows * cols
    wide, tall = own_ref.shape
    count = wide * tall
    parts = match.shape[1] // count

    spread = (iota((tall, count), 1) // wide == iota((tall, count), 0)).astype(jnp.float32)
    mine = iota((wide, count), 1) % wide == iota((wide, count), 0)
    spread_t = (iota((count, tall), 0) // wide == iota((count, tall), 1)).astype(jnp.float32)
    mine_t = iota((count, wide), 0) % wide == iota((count, wide), 1)

    def flat(ref):
        x = ref[...].astype(jnp.float32)
        along = jnp.sum(jnp.where(mine, dot(x, spread), 0.0), axis=0, keepdims=True)
        down = dot(spread_t, x, ((1,), (1,)))
        down = jnp.sum(jnp.where(mine_t, down, 0.0), axis=1, keepdims=True)
        return along.astype(jnp.int32), down.astype(jnp.int32)

    def entries(own, slot):
        r, c = slot // cols, slot % cols
        tile_r, tile_c = own // tiles_across, own % tiles_across
        focal = own < blocks
        nobody = jnp.full(own.shape, -1, jnp.int32)
        up = focal & (r == 0) & (tile_r > 0)
        down = focal & (r == rows - 1) & (tile_r < tiles_down - 1)
        left = focal & (c == 0) & (tile_c > 0)
        right = focal & (c == cols - 1) & (tile_c < tiles_across - 1)
        to = (
            jnp.where(focal, own, nobody),
            jnp.where(up, own - tiles_across, jnp.where(down, own + tiles_across, nobody)),
            jnp.where(left, own - 1, jnp.where(right, own + 1, nobody)),
        )
        place = (
            slot,
            cells + c + jnp.where(up, cols, 0),
            cells + 2 * cols + r + jnp.where(left, rows, 0),
        )
        return to, place

    (own_row, own_col), (slot_row, slot_col) = flat(own_ref), flat(slot_ref)
    to_row, place_row = entries(own_row, slot_row)
    to_col, _ = entries(own_col, slot_col)
    ones = lambda x: jnp.where(x, 1.0, 0.0)
    earlier = iota((count, count), 0) < iota((count, count), 1)
    used, ranks = jnp.zeros(own_row.shape, jnp.float32), []
    for k in range(3):
        rank = jnp.zeros(own_row.shape, jnp.float32)
        for other in range(k + 1):
            same = to_col[other] == to_row[k]
            same = same & earlier if other == k else same
            rank = rank + jnp.sum(ones(same), axis=0, keepdims=True)
        ranks.append(rank.astype(jnp.int32))
        used = jnp.maximum(used, jnp.where(to_row[k] >= 0, rank + 1.0, 0.0))
    full = jnp.where(jnp.max(used) > room, 1.0, 0.0)
    total = blocks * chunk
    at = iota((total, count), 0)
    fits = [(to >= 0) & (rank < room) for to, rank in zip(to_row, ranks)]
    base = [
        jnp.where(fit, to * chunk + rank, -total) for fit, to, rank in zip(fits, to_row, ranks)
    ]
    for part in range(parts):
        here = at - part * room
        match[:, part * count : part * count + count] = sum(ones(here == b) for b in base)
    lanes = (128, count)
    row, lane = iota((total, 128), 0), iota((total, 128), 1)
    result = jnp.where((row % chunk == chunk - 1) & (lane == room), full, 0.0)
    for fit, to, rank, place in zip(fits, to_row, ranks, place_row):
        target = ones(at == jnp.where(fit, to * chunk + chunk - 1, -1))
        value = jnp.where(iota(lanes, 0) == rank, place.astype(jnp.float32) + 1.0, 0.0)
        result = result + dot(target, value, ((1,), (1,)))
    placed[...] = result


def radiated(m, new, courant, absorption):
    return 0.1 * absorption * (m * m + new * new) * lax.rsqrt(courant)


def paired_lanes(x):
    pairing = iota((256, 128), 0) // 2 == iota((256, 128), 1)
    pairing = pairing.astype(jnp.float32).astype(jnp.bfloat16)
    high = x.astype(jnp.bfloat16)
    low = (x - high.astype(jnp.float32)).astype(jnp.bfloat16)
    product = functools.partial(jnp.dot, preferred_element_type=jnp.float32)
    return [
        product(high[:, at : at + 256], pairing) + product(low[:, at : at + 256], pairing)
        for at in range(0, x.shape[1], 256)
    ]


def even_and_odd(ref, count):
    return jnp.concatenate(
        [
            ref[part, pl.ds(0, count, stride=2), :] + ref[part, pl.ds(1, count, stride=2), :]
            for part in range(ref.shape[0])
        ],
        axis=1,
    )


def step_rows(i, m, up, down, first, last, p_ref, c_ref, n_ref, a_ref):
    c, a = c_ref[i], a_ref[i]
    lap = up + down + beside(m, first, last) + lateral(m) - 6.0 * m
    new = wave(m, p_ref[i], lap, c, n_ref[i], a)
    return new, radiated(m, new, c, a)


def put(ref, start, value):
    for part in range(ref.shape[0]):
        ref[part, pl.ds(start, value.shape[0]), :] = value[:, part * 128 : part * 128 + 128]


def second_acoustic(
    p_ref, c_ref, n_ref, a_ref, mid_ref, left, right, mid, new, lines, beyond_l, beyond_r, pairs
):
    deep, across, _ = p_ref.shape
    mid[...] = mid_ref[...]
    for j, side, beyond in ((0, left, beyond_l), (across - 1, right, beyond_r)):
        mid[:, j, :] = mid_ref[:, j, :] + c_ref[:, j, :] * side[0:deep]
        beyond[...] = side[2 * deep : 3 * deep] + side[deep : 2 * deep] * p_ref[:, j, :]

    def body(k, carry):
        i = 2 * k
        total = 0.0
        for at in (i, i + 1):
            one = pl.ds(at, 1)
            result, force = step_rows(
                at, mid[at], mid[at - 1], mid[at + 1], beyond_l[one, :], beyond_r[one, :],
                p_ref, c_ref, n_ref, a_ref,
            )
            new[at] = result
            total = total + force
        put(pairs, pl.multiple_of(k * across, across), total)
        return carry

    for at in (0, 1, deep - 2, deep - 1):
        new[at] = jnp.zeros(new.shape[1:], jnp.float32)
    put(pairs, 0, jnp.zeros(new.shape[1:], jnp.float32))
    put(pairs, (deep // 2 - 1) * across, jnp.zeros(new.shape[1:], jnp.float32))
    lax.fori_loop(1, deep // 2 - 1, body, 0)
    count = deep // 2 * (across // 2)
    for part, x in enumerate(paired_lanes(even_and_odd(pairs, count))):
        lines[part * count : part * count + count] = 0.125 * x


def ends_and_send(
    p_ref, c_ref, n_ref, a_ref, mid_ref, lines_ref, match_ref, placed_ref,
    before, after, left, right, mids, news, send, lines, pairs
):
    deep, across, _ = p_ref.shape
    count = deep // 2 * (across // 2)
    cols = (before.shape[0] - 8 - 3 * across) // 2
    corners = 3 * across + 2 * cols
    lines[...] = lines_ref[...]
    media = (p_ref, c_ref, n_ref, a_ref)

    def beyond(side, j, i):
        return side[2 * deep + i : 2 * deep + i + 1] + side[deep + i : deep + i + 1] * p_ref[
            i, j : j + 1, :
        ]

    for k, (i, inner, more, side) in enumerate(
        ((0, 1, 2, before), (deep - 1, deep - 2, deep - 3, after))
    ):
        m = mid_ref[i] + c_ref[i] * side[0:across]
        m_in = mid_ref[inner]
        outer = side[2 * across : 3 * across] + side[across : 2 * across] * p_ref[i]
        first = beyond(left, 0, i) + left[deep + i : deep + i + 1] * side[corners : corners + 1]
        last = (
            beyond(right, across - 1, i)
            + right[deep + i : deep + i + 1] * side[corners + 1 : corners + 2]
        )
        new, force = step_rows(i, m, outer, m_in, first, last, *media)
        first, last = beyond(left, 0, inner), beyond(right, across - 1, inner)
        new_in, force_in = step_rows(inner, m_in, m, mid_ref[more], first, last, *media)
        mids[k] = m
        news[2 * k] = new
        news[2 * k + 1] = new_in
        put(pairs, 0, force + force_in)
        half = across // 2
        for part, x in enumerate(paired_lanes(even_and_odd(pairs, half))):
            at = part * count + (0 if k == 0 else count - half)
            lines[at : at + half] = 0.125 * x
    send[...] = selected(match_ref[...], lines[...]) + placed_ref[...]


def second_elastic(
    mid_ref, new_ref, mids, news, free_ref, d_ref, b_ref, l_ref, shear, viscosity,
    before, after, left, right, mid, new, free, after_free, d_first, d_last, f_first, f_last
):
    deep, across, _ = mid.shape
    mid[...] = mid_ref[...]
    new[...] = new_ref[...]
    for k, (i, inner) in enumerate(((0, 1), (deep - 1, deep - 2))):
        mid[i] = mids[k]
        new[i] = news[2 * k]
        new[inner] = news[2 * k + 1]
    rows, cols, depth = d_ref.shape
    half = cols // 2
    top, base, corners = 3 * deep, 3 * across, 3 * across + 2 * cols
    lanes, others = slice(0, depth), slice(depth, 2 * depth)
    free[...] = free_ref[...]
    for i, side in ((0, before), (rows - 1, after)):
        s, v = lookup(l_ref[i], shear, 0), lookup(l_ref[i], viscosity, 0)
        free[i] = (
            free_ref[i]
            + s * whole(side, base, half, depth)
            + v * whole(side, base + half, half, depth)
        )
    now, then = slice(top, top + rows), slice(top + rows, top + 2 * rows)
    for k, (j, side, d_col, f_col) in enumerate(
        ((0, left, d_first, f_first), (cols - 1, right, d_last, f_last))
    ):
        labels = l_ref[:, j, :]
        s, v = lookup(labels, shear, 0), lookup(labels, viscosity, 0)
        d_side, e_side = side[now, lanes], side[now, others]
        free[:, j, :] = free[:, j, :] + s * d_side + v * e_side
        kinds = side[then, lanes]
        s, v = lookup(kinds, shear, 1.0), lookup(kinds, viscosity, 1.0)
        d = d_ref[:, j, :]
        at = slice(corners + 2 + k, corners + 3 + k)
        d_ends = at_ends(d.shape, before[at, lanes], after[at, lanes])
        e_ends = at_ends(d.shape, before[at, others], after[at, others])
        d_col[...] = d_side
        f_col[...] = side[then, others] + s * (d + d_ends) + v * (d - b_ref[:, j, :] + e_ends)

    def beyond(side, edge):
        part = lambda n: whole(side, base + n * half, half, depth)
        d, kinds = part(0), part(3)
        s, v = lookup(kinds, shear, 1.0), lookup(kinds, viscosity, 1.0)
        d_edge = d_ref[edge]
        return part(2) + s * d_edge + v * (d_edge - b_ref[edge]), d

    def step(i, f_up, f_down, d_up, d_down):
        f, d = free[i], d_ref[i]
        s, v = lookup(l_ref[i], shear, 0), lookup(l_ref[i], viscosity, 0)
        at = lambda ref: ref[pl.ds(i, 1), :]
        lap_f = f_up + f_down + beside(f, at(f_first), at(f_last)) + lateral(f) - 6.0 * f
        lap_d = d_up + d_down + beside(d, at(d_first), at(d_last)) + lateral(d) - 6.0 * d
        after_free[i] = 2.0 * f - d + s * lap_f + v * (lap_f - lap_d)

    f_up, d_up = beyond(before, 0)
    step(0, f_up, free[1], d_up, d_ref[1])
    f_down, d_down = beyond(after, rows - 1)
    step(rows - 1, free[rows - 2], f_down, d_ref[rows - 2], d_down)

    def body(i, carry):
        step(i, free[i - 1], free[i + 1], d_ref[i - 1], d_ref[i + 1])
        return carry

    lax.fori_loop(1, rows - 1, body, 0)


def landed(room, chunk, cells, got_ref, rows_of):
    total = got_ref.shape[0]
    parts, slots, _ = rows_of.shape
    blocks = total // chunk
    places = got_ref[pl.ds(chunk - 1, blocks, stride=chunk), :]
    for source in range(blocks):
        for part in range(parts):
            start = source * chunk + part * room
            rows_of[part, source * room : source * room + room, :] = got_ref[start : start + room, :]
    pick = jnp.where(iota((blocks, slots), 1) // room == iota((blocks, slots), 0), 1.0, 0.0)
    lanes = dot(places, pick, ((0,), (0,)))
    mine = iota(lanes.shape, 1) % room == iota(lanes.shape, 0)
    place = jnp.sum(jnp.where(mine, lanes, 0.0), axis=0, keepdims=True).astype(jnp.int32)
    landing = jnp.where(iota((cells, slots), 0) + 1 == place, 1.0, 0.0)
    return [selected(landing, rows_of[part]) for part in range(parts)]


def land(room, chunk, got_ref, force, rows_of):
    rows, cols, _ = force.shape
    for part, x in enumerate(landed(room, chunk, rows * cols, got_ref, rows_of)):
        force[:, :, part * 128 : part * 128 + 128] = x.reshape(rows, cols, 128)


def tissue_steps(force, free, after_free, l_ref, shear, viscosity, up, down, left, right, mid, new):
    rows = force.shape[0]

    def step(i, f_up, f_down):
        f = force[i]
        s, v = lookup(l_ref[i], shear, 0), lookup(l_ref[i], viscosity, 0)
        at = lambda ref: ref[pl.ds(i, 1), :]
        lap = f_up + f_down + beside(f, at(left), at(right)) + lateral(f) - 6.0 * f
        mid[i] = free[i] + 0.25 * f
        new[i] = after_free[i] + 0.75 * f + 0.25 * (s + v) * lap

    step(0, up[...], force[1])
    step(rows - 1, force[rows - 2], down[...])

    def body(i, carry):
        step(i, force[i - 1], force[i + 1])
        return carry

    lax.fori_loop(1, rows - 1, body, 0)


def land_and_step(
    room, chunk, got_ref, free, after_free, l_ref, shear, viscosity, force, mid, new,
    rows_of, up, down, left, right
):
    rows, cols, _ = force.shape
    cells = rows * cols
    borders, start = [], cells
    for ref in (up, down, left, right):
        borders.append((ref, start))
        start += ref.shape[0]
    for part, x in enumerate(landed(room, chunk, start, got_ref, rows_of)):
        lanes = slice(part * 128, part * 128 + 128)
        force[:, :, lanes] = x[:cells].reshape(rows, cols, 128)
        for ref, first in borders:
            ref[:, lanes] = x[first : first + ref.shape[0]]
    tissue_steps(
        force, free, after_free, l_ref, shear, viscosity, up, down, left, right, mid, new
    )


def far(*arrays):
    return [pltpu.with_memory_space_constraint(x, pltpu.HBM) for x in arrays]


def swap(first, last, axis):
    size = lax.axis_size(axis)
    up = [(i, i + 1) for i in range(size - 1)]
    down = [(j, i) for i, j in up]
    return lax.ppermute(last, axis, up), lax.ppermute(first, axis, down)


def local(
    pressure,
    pressure_prev,
    courant,
    nonlinearity,
    absorption,
    own_map,
    slot_table,
    displacement,
    displacement_prev,
    layer_labels,
    shear_table,
    viscosity_table,
):
    deep, across, span = pressure.shape
    rows, cols, depth = displacement.shape
    f32 = lambda *shape: jax.ShapeDtypeStruct(shape, jnp.float32)
    hbm = lambda *shape: pltpu.HBM(shape, jnp.float32)
    scratch = lambda *shape: pltpu.VMEM(shape, jnp.float32)

    def run(kernel, out, *args, scratch_shapes=(), tables=(), weight=1, limit=8):
        specs = [SMEM if k in tables else VMEM for k in range(len(args))]
        moved = weight * 4 * sum(math.prod(x.shape) for x in args + tuple(jax.tree.leaves(out)))
        cost = pl.CostEstimate(flops=20 * moved, bytes_accessed=moved, transcendentals=0)
        return pl.pallas_call(
            kernel,
            out_shape=out,
            in_specs=specs,
            out_specs=jax.tree.map(lambda _: VMEM, out),
            scratch_shapes=scratch_shapes,
            compiler_params=pltpu.CompilerParams(vmem_limit_bytes=limit << 20),
            cost_estimate=cost,
        )(*args)

    fields = (
        (pressure, 1),
        (pressure_prev, 0),
        (courant, 0),
        (nonlinearity, 0),
        (absorption, 0),
        (displacement, 1),
        (displacement_prev, 1),
        (layer_labels, 0),
    )
    arrays, inner = [x for x, _ in fields], [more for _, more in fields]
    side = 3 * deep + 2 * rows
    buffers = [
        pltpu.VMEM((x.shape[0], x.shape[2]), x.dtype)
        for x, more in fields
        for _ in range(2 * (1 + more))
    ]
    near = pl.BlockSpec(memory_space=pltpu.HBM)
    first, last = pl.pallas_call(
        functools.partial(border_columns, inner),
        out_shape=(f32(side, span),) * 2,
        in_specs=[near] * len(fields) + [SMEM, SMEM],
        out_specs=(VMEM, VMEM),
        scratch_shapes=buffers + [pltpu.SemaphoreType.DMA((len(buffers),))],
        compiler_params=pltpu.CompilerParams(vmem_limit_bytes=63 << 20),
    )(*far(*arrays), shear_table, viscosity_table)
    left, right = swap(first, last, "gy")
    pause = pl.pallas_call(
        cover,
        out_shape=f32(8, 128),
        in_specs=[near],
        out_specs=VMEM,
        compiler_params=pltpu.CompilerParams(vmem_limit_bytes=1 << 20),
        cost_estimate=pl.CostEstimate(flops=2 * 10**10, bytes_accessed=10**9, transcendentals=0),
    )(*far(first))
    block, tissue = f32(deep, across, span), f32(rows, cols, depth)
    mid, free = run(
        first_steps,
        (block, tissue),
        *arrays,
        shear_table,
        viscosity_table,
        pause,
        tables=(8, 9),
    )
    first, last = run(
        border_rows,
        (f32(3 * across + 2 * cols + 8, span),) * 2,
        pressure,
        courant,
        mid,
        displacement,
        displacement_prev,
        layer_labels,
        free,
        shear_table,
        viscosity_table,
        left,
        right,
        tables=(7, 8),
    )
    before, after = swap(first, last, "gx")
    grid = (lax.axis_size("gx"), lax.axis_size("gy"))
    blocks = grid[0] * grid[1]
    capacity = max(2, deep // 2 * (across // 2) // blocks)
    parts = depth // 128
    room = 2 * capacity + 1
    chunk = -(-(room * parts + 1) // 8) * 8
    count = own_map.size
    match, placed = pl.pallas_call(
        functools.partial(address, grid, (rows, cols), room, chunk),
        out_shape=(f32(blocks * chunk, parts * count), f32(blocks * chunk, 128)),
        in_specs=[VMEM, VMEM, near],
        out_specs=(VMEM, VMEM),
        compiler_params=pltpu.CompilerParams(vmem_limit_bytes=16 << 20),
        cost_estimate=pl.CostEstimate(flops=10**8, bytes_accessed=10**7, transcendentals=0),
    )(own_map.T, slot_table.T, *far(first))
    media = (pressure, courant, nonlinearity, absorption)
    mid, new, lines = run(
        second_acoustic,
        (block, block, f32(parts * count, 128)),
        *media,
        mid,
        left,
        right,
        scratch_shapes=[
            scratch(deep, span),
            scratch(deep, span),
            scratch(span // 128, deep // 2 * across, 128),
        ],
    )
    mids, news, send = run(
        ends_and_send,
        (hbm(2, across, span), hbm(4, across, span), hbm(blocks * chunk, 128)),
        *media,
        mid,
        lines,
        match,
        placed,
        before,
        after,
        left,
        right,
        scratch_shapes=[scratch(parts * count, 128), scratch(span // 128, across, 128)],
    )
    send = send.reshape(blocks, chunk, 128)
    got = lax.all_to_all(send, ("gx", "gy"), split_axis=0, concat_axis=0, tiled=True)
    pressure_mid, pressure_new, free, after_free = run(
        second_elastic,
        (block, block, tissue, tissue),
        *far(mid, new, mids, news, free, displacement, displacement_prev, layer_labels),
        shear_table,
        viscosity_table,
        *far(before, after, left, right),
        scratch_shapes=[scratch(rows, depth)] * 4,
        tables=(8, 9),
        limit=24,
    )
    arrived = scratch(depth // 128, blocks * room, 128)

    def direct(got, *rest):
        return run(
            functools.partial(land_and_step, room, chunk),
            (tissue,) * 3,
            got,
            *rest,
            scratch_shapes=[arrived] + [scratch(n, depth) for n in (cols, cols, rows, rows)],
            tables=(4, 5),
        )

    def by_faces(got, *rest):
        force = run(
            functools.partial(land, room, chunk), tissue, got, scratch_shapes=[arrived]
        )
        up, down = swap(force[0], force[rows - 1], "gx")
        at_left, at_right = swap(force[:, 0], force[:, cols - 1], "gy")
        mid, new = run(
            tissue_steps,
            (tissue,) * 2,
            force,
            *rest,
            up,
            down,
            at_left,
            at_right,
            tables=(4, 5),
        )
        return force, mid, new

    tissue_force, displacement_mid, displacement_new = lax.cond(
        jnp.max(got[:, chunk - 1, room]) > 0.0,
        by_faces,
        direct,
        got.reshape(blocks * chunk, 128),
        free,
        after_free,
        layer_labels,
        shear_table,
        viscosity_table,
    )
    return (pressure_mid, pressure_new, tissue_force, displacement_mid, displacement_new)


def solution(mesh):
    block = P(("group", "gx"), "gy", None)
    plane = P(("group", "gx"), "gy")
    return jax.shard_map(
        local,
        mesh=mesh,
        in_specs=(block,) * 5 + (plane,) * 2 + (block,) * 3 + (P("group"),) * 2,
        out_specs=(block,) * 5,
        check_vma=False,
    )
```

time: 59.5 us -> 56.2 us (0.945)
  waiting for transfers between devices: 9.59 us -> 7.46 us
  local copies, waits for them, and re-layouts: 3.16 us -> 1.76 us
  Pallas kernels: 25.4 us -> 26.2 us
    ppermute x4, waiting for transfers between devices: 5.52 us -> 3.2 us  [swap(): return (lax.ppermute(last, axis, up), lax.ppermute(first, axis, down))]
    unnamed x38 -> x42, local copies, waits for them, and re-layouts: 3.16 us -> 1.76 us
    pallas_call x1 -> x3, Pallas kernels: 3.67 us -> 5.05 us  [the longest x1 3.25 us: local(): pl.pallas_call(functools.partial(border_columns, inner), out_shape=(f32(s...]
    all_to_all x1, starting transfers between devices: 9.88 us -> 8.99 us  [local(): lax.all_to_all(send, ('gx', 'gy'), split_axis=0, concat_axis=0, tiled=True)]
    pallas_call x6, Pallas kernels: 21.8 us -> 21.2 us  [run(): pl.pallas_call(kernel, out_shape=out, in_specs=specs, out_specs=jax.tree....]
  transfers between devices with their start and end apart: 5 -> 5, of which waited for: 3 -> 2; matrix products, arithmetic and copies ran while one was open for 0% -> 0% of each run, Pallas kernels for 19% -> 29%
where the time goes in v3:
time: 56.2 us; the launch traced here: 55.9 us
  Pallas kernels  26.2 us (47%)
  starting transfers between devices  18.1 us (32%)
  waiting for transfers between devices  7.46 us (13%)
  local copies, waits for them, and re-layouts  1.76 us (3%)
  between operations  1.62 us (3%)
  other arithmetic  0.69 us (1%)
    pallas_call x6, Pallas kernels, run(): pl.pallas_call(kernel, out_shape=out, in_specs=specs, out_specs=jax.tree....  21.2 us
    ppermute x4, starting transfers between devices, swap(): return (lax.ppermute(last, axis, up), lax.ppermute(first, axis, down))  9.14 us
    all_to_all x1, starting transfers between devices, local(): lax.all_to_all(send, ('gx', 'gy'), split_axis=0, concat_axis=0, tiled=True)  8.99 us
    all_to_all x1, waiting for transfers between devices, local(): lax.all_to_all(send, ('gx', 'gy'), split_axis=0, concat_axis=0, tiled=True)  4.26 us
    pallas_call x1, Pallas kernels, local(): pl.pallas_call(functools.partial(border_columns, inner), out_shape=(f32(s...  3.25 us
    ppermute x4, waiting for transfers between devices, swap(): return (lax.ppermute(last, axis, up), lax.ppermute(first, axis, down))  3.2 us
    pallas_call x1, Pallas kernels, local(): pl.pallas_call(functools.partial(address, grid, (rows, cols), room, chunk...  1.8 us
    unnamed x42, local copies, waits for them, and re-layouts  1.76 us
  transfers between devices with their start and end apart: 5, of which 2 were waited for; matrix products, arithmetic and copies ran while one was open for 0% of the time, Pallas kernels for 29%

profile of v3, /device:TPU:0, one launch (start us, length us, event | category | flops | bytes accessed | tf_op | source)
XLA Modules:
  0.0 55.9 jit_solution(2281919530463834069)
XLA Ops:
  0.6 3.2 %shard_map.155 = (f32[104,768]{1,0:T(8,128)}, f32[104,768]{1,0:T(8,128)}) custom-call(f32[24,16,768]{2,1,0:T(8,128)} %p_ref.7, f32[24,16,768]{2,1,0:T(8,128)} %q_ref.1, f32[24,16,768]{2,1,0:T(8,128)} %c_ref.7, f32[24,16,768]{2,1,0:T(8,128)} %n_ref.5, f32[24,16,768]{2,1,0:T(8,128)} %a_ref.5, f32[16,32,384]{2,1,0:T(8,128)} %d_ref.5, f32[16,32,384]{2,1,0:T(8,128)} %b_ref.5, ...), custom_call_target="tpu_custom_call" | custom-call | tf_op jit(solution)/shard_map/pallas_call | solution.py:569
  3.9 5.0 %collective-permute-start.4 = (f32[104,768]{1,0:T(8,128)}, f32[104,768]{1,0:T(8,128)S(1)}, u32[]{:S(2)}, u32[]{:S(2)}) collective-permute-start(f32[104,768]{1,0:T(8,128)} %get-tuple-element.66), channel_id=1, source_target_pairs={{0,1},{1,2},{2,3},{4,5},{5,6},{6,7},{8,9},{9,10},{10,11},{12,13},{... | collective-permute-start | bytes 958472 | tf_op jit(solution)/shard_map/ppermute | solution.py:514
  9.0 1.6 %collective-permute-start.5 = (f32[104,768]{1,0:T(8,128)}, f32[104,768]{1,0:T(8,128)S(1)}, u32[]{:S(2)}, u32[]{:S(2)}) collective-permute-start(f32[104,768]{1,0:T(8,128)} %get-tuple-element.64._), channel_id=1, source_target_pairs={{1,0},{2,1},{3,2},{5,4},{6,5},{7,6},{9,8},{10,9},{11,10},{13,12},{... | collective-permute-start | bytes 958472 | tf_op jit(solution)/shard_map/ppermute | solution.py:514
  10.6 0.3 copy-done.2
  10.9 0.4 copy-done.3
  11.2 0.2 copy-done.4
  11.4 0.2 copy-done.5
  11.7 0.4 copy-done.8
  12.0 0.2 copy-done.17
  12.2 5.0 %shard_map.157 = (f32[24,16,768]{2,1,0:T(8,128)S(1)}, f32[16,32,384]{2,1,0:T(8,128)S(1)}) custom-call(f32[24,16,768]{2,1,0:T(8,128)S(1)} %copy-done, f32[24,16,768]{2,1,0:T(8,128)S(1)} %copy-done.8, f32[24,16,768]{2,1,0:T(8,128)S(1)} %copy-done.1, f32[24,16,768]{2,1,0:T(8,128)S(1)} %copy-done.2, f32[24,16,768]{2,1,0:T(8,128)S(1)} %copy-done.3, ...), custom_call_target="tpu_custom_call" | custom-call | flops 204554880 | bytes 10227744 | tf_op jit(solution)/shard_map/pallas_call | solution.py:541
  17.3 3.2 %collective-permute-done.5.right = f32[104,768]{1,0:T(8,128)S(1)} collective-permute-done((f32[104,768]{1,0:T(8,128)}, f32[104,768]{1,0:T(8,128)S(1)}, u32[]{:S(2)}, u32[]{:S(2)}) %collective-permute-start.5) | collective-permute-done | bytes 319520 | tf_op jit(solution)/shard_map/ppermute | solution.py:514
  20.5 0.6 %shard_map.159 = (f32[120,768]{1,0:T(8,128)S(1)}, f32[120,768]{1,0:T(8,128)S(1)}) custom-call(f32[24,16,768]{2,1,0:T(8,128)S(1)} %copy-done, f32[24,16,768]{2,1,0:T(8,128)S(1)} %copy-done.1, f32[24,16,768]{2,1,0:T(8,128)S(1)} %get-tuple-element.65.mid_ref, f32[16,32,384]{2,1,0:T(8,128)S(1)} %copy-done.4, f32[16,32,384]{2,1,0:T(8,128)S(1)} %copy-done.5, ...), custom_call_target="tpu_custom_call" | custom-call | flops 161219200 | bytes 8060960 | tf_op jit(solution)/shard_map/pallas_call | solution.py:541
  21.2 1.3 %collective-permute-start.6 = (f32[120,768]{1,0:T(8,128)S(1)}, f32[120,768]{1,0:T(8,128)S(1)}, u32[]{:S(2)}, u32[]{:S(2)}) collective-permute-start(f32[120,768]{1,0:T(8,128)S(1)} %get-tuple-element.74), channel_id=1, source_target_pairs={{0,4},{4,8},{8,12},{1,5},{5,9},{9,13},{2,6},{6,10},{10,14},{3,7},{... | collective-permute-start | bytes 1105928 | tf_op jit(solution)/shard_map/ppermute | solution.py:514
  22.5 1.3 %collective-permute-start.7 = (f32[120,768]{1,0:T(8,128)S(1)}, f32[120,768]{1,0:T(8,128)S(1)}, u32[]{:S(2)}, u32[]{:S(2)}) collective-permute-start(f32[120,768]{1,0:T(8,128)S(1)} %get-tuple-element.71._), channel_id=1, source_target_pairs={{4,0},{8,4},{12,8},{5,1},{9,5},{13,9},{6,2},{10,6},{14,10},{7,3},{... | collective-permute-start | bytes 1105928 | tf_op jit(solution)/shard_map/ppermute | solution.py:514
  23.8 1.8 %shard_map.160 = (f32[640,288]{1,0:T(8,128)S(1)}, f32[640,128]{1,0:T(8,128)S(1)}) custom-call(s32[8,12]{1,0:T(8,128)S(1)} %bitcast.14, s32[8,12]{1,0:T(8,128)S(1)} %bitcast.15, f32[120,768]{1,0:T(8,128)} %copy-done.14), custom_call_target="tpu_custom_call" | custom-call | flops 100000000 | bytes 10000000 | tf_op jit(solution)/shard_map/pallas_call | solution.py:620
  25.6 2.1 %shard_map.158 = (f32[24,16,768]{2,1,0:T(8,128)S(1)}, f32[24,16,768]{2,1,0:T(8,128)S(1)}, f32[288,128]{1,0:T(8,128)S(1)}) custom-call(f32[24,16,768]{2,1,0:T(8,128)S(1)} %copy-done, f32[24,16,768]{2,1,0:T(8,128)S(1)} %copy-done.1, f32[24,16,768]{2,1,0:T(8,128)S(1)} %copy-done.2, f32[24,16,768]{2,1,0:T(8,128)S(1)} %copy-done.3, ...), custom_call_target="tpu_custom_call" | custom-call | flops 180879360 | bytes 9043968 | tf_op jit(solution)/shard_map/pallas_call | solution.py:541
  27.8 0.0 collective-permute-done.7.after
  27.8 1.8 %shard_map.161 = (f32[2,16,768]{2,1,0:T(8,128)}, f32[4,16,768]{2,1,0:T(8,128)}, f32[640,128]{1,0:T(8,128)}) custom-call(f32[24,16,768]{2,1,0:T(8,128)S(1)} %copy-done, f32[24,16,768]{2,1,0:T(8,128)S(1)} %copy-done.1, f32[24,16,768]{2,1,0:T(8,128)S(1)} %copy-done.2, f32[24,16,768]{2,1,0:T(8,128)S(1)} %copy-done.3, ...), custom_call_target="tpu_custom_call" | custom-call | flops 182190080 | bytes 9109504 | tf_op jit(solution)/shard_map/pallas_call | solution.py:541
  29.6 9.0 %all-to-all-start = ((f32[16,40,128]{2,1,0:T(8,128)}), f32[16,40,128]{2,1,0:T(8,128)S(1)}, u32[]{:S(2)}, u32[]{:S(2)}) async-start(f32[16,40,128]{2,1,0:T(8,128)} %bitcast.18), calls=%async_computation | async-start | bytes 655360 | tf_op jit(solution)/shard_map/all_to_all | solution.py:657
  38.6 7.1 %shard_map.162 = (f32[24,16,768]{2,1,0:T(8,128)}, f32[24,16,768]{2,1,0:T(8,128)}, f32[16,32,384]{2,1,0:T(8,128)S(1)}, f32[16,32,384]{2,1,0:T(8,128)S(1)}) custom-call(f32[24,16,768]{2,1,0:T(8,128)} %copy-done.9, f32[24,16,768]{2,1,0:T(8,128)} %copy-done.13, f32[2,16,768]{2,1,0:T(8,128)} %get-tuple-element.75.mids, f32[4,16,768]{2,1,0:T(8,128)} %get-tuple-element.76.news, ...), custom_call_target="tpu_custom_call" | custom-call | flops 222167680 | bytes 11108384 | tf_op jit(solution)/shard_map/pallas_call | solution.py:541
  45.7 4.3 %all-to-all-done = f32[16,40,128]{2,1,0:T(8,128)S(1)} async-done(((f32[16,40,128]{2,1,0:T(8,128)}), f32[16,40,128]{2,1,0:T(8,128)S(1)}, u32[]{:S(2)}, u32[]{:S(2)}) %all-to-all-start) | async-done | bytes 327712 | tf_op jit(solution)/shard_map/all_to_all | solution.py:657
  49.9 0.7 %slice_reduce_fusion = f32[]{:T(128)} fusion(f32[16,40,128]{2,1,0:T(8,128)S(1)} %all-to-all-done), kind=kLoop, calls=%fused_computation.4 | loop fusion | flops 15 | bytes 68 | tf_op jit(solution)/shard_map/reduce_max | solution.py:701
  51.3 4.6 %conditional.1 = ((f32[16,32,384]{2,1,0:T(8,128)}, f32[16,32,384]{2,1,0:T(8,128)}, f32[16,32,384]{2,1,0:T(8,128)})) conditional(s32[]{:T(128)} %convert_element_type.3, (f32[640,128]{1,0:T(8,128)S(1)}, f32[16,32,384]{2,1,0:T(8,128)S(1)}, f32[16,32,384]{2,1,0:T(8,128)S(1)}, s32[16,32,384]{2,1,0:T(8,128)S(1)}, f32[4]{0:T(128)S(1)}, ...), branch_computations={%region_1.0_spmd, %region_2.0_spmd} | conditional | flops 119603840 | bytes 6963424 | solution.py:700
  51.3 4.6 %branch_0_fun.1 = (f32[16,32,384]{2,1,0:T(8,128)}, f32[16,32,384]{2,1,0:T(8,128)}, f32[16,32,384]{2,1,0:T(8,128)}) custom-call(f32[640,128]{1,0:T(8,128)S(1)} %get-tuple-element.24.got_ref, f32[16,32,384]{2,1,0:T(8,128)S(1)} %get-tuple-element.25.free, f32[16,32,384]{2,1,0:T(8,128)S(1)} %get-tuple-element.26.after_free, ...), custom_call_target="tpu_custom_call" | custom-call | flops 100926080 | bytes 5046304 | tf_op jit(solution)/shard_map/cond/branch_0_fun/pallas_call | solution.py:541
  (39 shorter events, 0.1 us)
Async XLA Ops:
  3.9 13.4 %collective-permute-start.4 = (f32[104,768]{1,0:T(8,128)}, f32[104,768]{1,0:T(8,128)S(1)}, u32[]{:S(2)}, u32[]{:S(2)}) collective-permute-start(f32[104,768]{1,0:T(8,128)} %get-tuple-element.66), channel_id=1, source_target_pairs={{0,1},{1,2},{2,3},{4,5},{5,6},{6,7},{8,9},{9,10},{10,11},{12,13},{... | collective-permute-start | bytes 958472 | tf_op jit(solution)/shard_map/ppermute | solution.py:514
  8.9 2.0 %copy-start.2 = (f32[24,16,768]{2,1,0:T(8,128)S(1)}, f32[24,16,768]{2,1,0:T(8,128)}, u32[]{:S(2)}) copy-start(f32[24,16,768]{2,1,0:T(8,128)} %n_ref.5) | copy-start | bytes 3538948
  8.9 2.3 %copy-start.3 = (f32[24,16,768]{2,1,0:T(8,128)S(1)}, f32[24,16,768]{2,1,0:T(8,128)}, u32[]{:S(2)}) copy-start(f32[24,16,768]{2,1,0:T(8,128)} %a_ref.5) | copy-start | bytes 3538948
  8.9 2.5 %copy-start.4 = (f32[16,32,384]{2,1,0:T(8,128)S(1)}, f32[16,32,384]{2,1,0:T(8,128)}, u32[]{:S(2)}) copy-start(f32[16,32,384]{2,1,0:T(8,128)} %d_ref.5) | copy-start | bytes 2359300
  8.9 2.7 %copy-start.5 = (f32[16,32,384]{2,1,0:T(8,128)S(1)}, f32[16,32,384]{2,1,0:T(8,128)}, u32[]{:S(2)}) copy-start(f32[16,32,384]{2,1,0:T(8,128)} %b_ref.5) | copy-start | bytes 2359300
  8.9 3.1 %copy-start.8 = (f32[24,16,768]{2,1,0:T(8,128)S(1)}, f32[24,16,768]{2,1,0:T(8,128)}, u32[]{:S(2)}) copy-start(f32[24,16,768]{2,1,0:T(8,128)} %q_ref.1) | copy-start | bytes 3538948
  9.0 3.3 %copy-start.17 = (s32[16,32,384]{2,1,0:T(8,128)S(1)}, s32[16,32,384]{2,1,0:T(8,128)}, u32[]{:S(2)}) copy-start(s32[16,32,384]{2,1,0:T(8,128)} %l_ref.5) | copy-start | bytes 2359300
  9.0 3.3 %copy-start.19 = (f32[4]{0:T(128)S(1)}, f32[4]{0:T(128)}, u32[]{:S(2)}) copy-start(f32[4]{0:T(128)} %shear.5) | copy-start | bytes 52
  9.0 3.3 %copy-start.20 = (f32[4]{0:T(128)S(1)}, f32[4]{0:T(128)}, u32[]{:S(2)}) copy-start(f32[4]{0:T(128)} %viscosity.5) | copy-start | bytes 52
  9.0 11.5 %collective-permute-start.5 = (f32[104,768]{1,0:T(8,128)}, f32[104,768]{1,0:T(8,128)S(1)}, u32[]{:S(2)}, u32[]{:S(2)}) collective-permute-start(f32[104,768]{1,0:T(8,128)} %get-tuple-element.64._), channel_id=1, source_target_pairs={{1,0},{2,1},{3,2},{5,4},{6,5},{7,6},{9,8},{10,9},{11,10},{13,12},{... | collective-permute-start | bytes 958472 | tf_op jit(solution)/shard_map/ppermute | solution.py:514
  17.3 3.9 %copy-start.10 = (f32[16,32,384]{2,1,0:T(8,128)}, f32[16,32,384]{2,1,0:T(8,128)S(1)}, u32[]{:S(2)}) copy-start(f32[16,32,384]{2,1,0:T(8,128)S(1)} %get-tuple-element.70.free_ref) | copy-start | bytes 2359300
  17.3 10.5 %copy-start.6 = (f32[104,768]{1,0:T(8,128)}, f32[104,768]{1,0:T(8,128)S(1)}, u32[]{:S(2)}) copy-start(f32[104,768]{1,0:T(8,128)S(1)} %collective-permute-done.4.left) | copy-start | bytes 958468
  20.5 7.3 %copy-start.7 = (f32[104,768]{1,0:T(8,128)}, f32[104,768]{1,0:T(8,128)S(1)}, u32[]{:S(2)}) copy-start(f32[104,768]{1,0:T(8,128)S(1)} %collective-permute-done.5.right) | copy-start | bytes 958468
  20.5 3.3 %copy-start.15 = (s32[12,8]{0,1:T(8,128)S(1)}, s32[12,8]{0,1:T(8,128)}, u32[]{:S(2)}) copy-start(s32[12,8]{0,1:T(8,128)} %param.19) | copy-start | bytes 1156
  20.5 3.3 %copy-start.16 = (s32[12,8]{0,1:T(8,128)S(1)}, s32[12,8]{0,1:T(8,128)}, u32[]{:S(2)}) copy-start(s32[12,8]{0,1:T(8,128)} %param.20) | copy-start | bytes 1156
  21.1 2.6 %copy-start.14 = (f32[120,768]{1,0:T(8,128)}, f32[120,768]{1,0:T(8,128)S(1)}, u32[]{:S(2)}) copy-start(f32[120,768]{1,0:T(8,128)S(1)} %get-tuple-element.71._) | copy-start | bytes 1105924
  21.2 6.6 %collective-permute-start.6 = (f32[120,768]{1,0:T(8,128)S(1)}, f32[120,768]{1,0:T(8,128)S(1)}, u32[]{:S(2)}, u32[]{:S(2)}) collective-permute-start(f32[120,768]{1,0:T(8,128)S(1)} %get-tuple-element.74), channel_id=1, source_target_pairs={{0,4},{4,8},{8,12},{1,5},{5,9},{9,13},{2,6},{6,10},{10,14},{3,7},{... | collective-permute-start | bytes 1105928 | tf_op jit(solution)/shard_map/ppermute | solution.py:514
  22.5 5.3 %collective-permute-start.7 = (f32[120,768]{1,0:T(8,128)S(1)}, f32[120,768]{1,0:T(8,128)S(1)}, u32[]{:S(2)}, u32[]{:S(2)}) collective-permute-start(f32[120,768]{1,0:T(8,128)S(1)} %get-tuple-element.71._), channel_id=1, source_target_pairs={{4,0},{8,4},{12,8},{5,1},{9,5},{13,9},{6,2},{10,6},{14,10},{7,3},{... | collective-permute-start | bytes 1105928 | tf_op jit(solution)/shard_map/ppermute | solution.py:514
  27.7 1.9 %copy-start.9 = (f32[24,16,768]{2,1,0:T(8,128)}, f32[24,16,768]{2,1,0:T(8,128)S(1)}, u32[]{:S(2)}) copy-start(f32[24,16,768]{2,1,0:T(8,128)S(1)} %get-tuple-element.67.mid_ref) | copy-start | bytes 3538948
  27.7 1.9 %copy-start.13 = (f32[24,16,768]{2,1,0:T(8,128)}, f32[24,16,768]{2,1,0:T(8,128)S(1)}, u32[]{:S(2)}) copy-start(f32[24,16,768]{2,1,0:T(8,128)S(1)} %get-tuple-element.68.new_ref) | copy-start | bytes 3538948
  27.7 1.8 %copy-start.11 = (f32[120,768]{1,0:T(8,128)}, f32[120,768]{1,0:T(8,128)S(1)}, u32[]{:S(2)}) copy-start(f32[120,768]{1,0:T(8,128)S(1)} %collective-permute-done.6.before) | copy-start | bytes 1105924
  27.8 1.8 %copy-start.12 = (f32[120,768]{1,0:T(8,128)}, f32[120,768]{1,0:T(8,128)S(1)}, u32[]{:S(2)}) copy-start(f32[120,768]{1,0:T(8,128)S(1)} %collective-permute-done.7.after) | copy-start | bytes 1105924
  29.6 20.3 %all-to-all-start = ((f32[16,40,128]{2,1,0:T(8,128)}), f32[16,40,128]{2,1,0:T(8,128)S(1)}, u32[]{:S(2)}, u32[]{:S(2)}) async-start(f32[16,40,128]{2,1,0:T(8,128)} %bitcast.18), calls=%async_computation | async-start | bytes 655360 | tf_op jit(solution)/shard_map/all_to_all | solution.py:657
  38.6 12.7 %copy-start.18 = (s32[16,32,384]{2,1,0:T(8,128)S(1)}, s32[16,32,384]{2,1,0:T(8,128)}, u32[]{:S(2)}) copy-start(s32[16,32,384]{2,1,0:T(8,128)} %l_ref.5) | copy-start | bytes 2359300
  (2 other events, 3.4 us)

commit v4 on v3

--- a/solution.py
+++ b/solution.py
@@ -14,19 +14,28 @@
 
 
 def lateral(x):
-    dim, size = x.ndim - 1, x.shape[-1]
-    lane = lax.broadcasted_iota(jnp.int32, x.shape, dim)
-    lower = jnp.where(lane == 0, 0.0, pltpu.roll(x, 1, dim))
-    upper = jnp.where(lane == size - 1, 0.0, pltpu.roll(x, size - 1, dim))
-    return lower + upper
+    tiles = [x[:, at : at + 128] for at in range(0, x.shape[1], 128)]
+    lane = lax.broadcasted_iota(jnp.int32, tiles[0].shape, 1)
+    lower = [0.0] + [pltpu.roll(tile, 1, 1) for tile in tiles]
+    upper = [pltpu.roll(tile, 127, 1) for tile in tiles] + [0.0]
+    sums = [
+        jnp.where(lane == 0, lower[k], lower[k + 1])
+        + jnp.where(lane == 127, upper[k + 1], upper[k])
+        for k in range(len(tiles))
+    ]
+    return jnp.concatenate(sums, axis=1)
 
 
 def beside(x, before, after):
-    size = x.shape[0]
-    row = lax.broadcasted_iota(jnp.int32, x.shape, 0)
-    up = jnp.where(row == 0, before, pltpu.roll(x, 1, 0))
-    down = jnp.where(row == size - 1, after, pltpu.roll(x, size - 1, 0))
-    return up + down
+    tiles = [x[at : at + 8] for at in range(0, x.shape[0], 8)]
+    row = lax.broadcasted_iota(jnp.int32, tiles[0].shape, 0)
+    up = [before] + [pltpu.roll(tile, 1, 0) for tile in tiles]
+    down = [pltpu.roll(tile, 7, 0) for tile in tiles] + [after]
+    sums = [
+        jnp.where(row == 0, up[k], up[k + 1]) + jnp.where(row == 7, down[k + 1], down[k])
+        for k in range(len(tiles))
+    ]
+    return jnp.concatenate(sums, axis=0)
 
 
 def at_ends(shape, first, last):
@@ -45,9 +54,10 @@
 
 
 def lookup(kinds, table, first):
-    result = jnp.zeros(kinds.shape, jnp.float32)
-    for kind in range(table.shape[0]):
-        result = jnp.where(kinds == kind + first, table[kind], result)
+    values = [table[kind] for kind in range(len(table) if isinstance(table, list) else table.shape[0])]
+    result = jnp.full(kinds.shape, 0.0 if first else values[0], jnp.float32)
+    for kind in range(0 if first else 1, len(values)):
+        result = jnp.where(kinds == kind + first, values[kind], result)
     return result
 
 
@@ -374,7 +384,7 @@
 
 def second_elastic(
     mid_ref, new_ref, mids, news, free_ref, d_ref, b_ref, l_ref, shear, viscosity,
-    before, after, left, right, mid, new, free, after_free, d_first, d_last, f_first, f_last
+    before, after, left, right, mid, new, free, after_free, quarter, d_first, d_last, f_first, f_last
 ):
     deep, across, _ = mid.shape
     mid[...] = mid_ref[...]
@@ -426,6 +436,7 @@
         lap_f = f_up + f_down + beside(f, at(f_first), at(f_last)) + lateral(f) - 6.0 * f
         lap_d = d_up + d_down + beside(d, at(d_first), at(d_last)) + lateral(d) - 6.0 * d
         after_free[i] = 2.0 * f - d + s * lap_f + v * (lap_f - lap_d)
+        quarter[i] = 0.25 * (s + v)
 
     f_up, d_up = beyond(before, 0)
     step(0, f_up, free[1], d_up, d_ref[1])
@@ -443,35 +454,40 @@
     total = got_ref.shape[0]
     parts, slots, _ = rows_of.shape
     blocks = total // chunk
-    places = got_ref[pl.ds(chunk - 1, blocks, stride=chunk), :]
+    slot = slots // blocks
     for source in range(blocks):
         for part in range(parts):
             start = source * chunk + part * room
-            rows_of[part, source * room : source * room + room, :] = got_ref[start : start + room, :]
-    pick = jnp.where(iota((blocks, slots), 1) // room == iota((blocks, slots), 0), 1.0, 0.0)
-    lanes = dot(places, pick, ((0,), (0,)))
-    mine = iota(lanes.shape, 1) % room == iota(lanes.shape, 0)
-    place = jnp.sum(jnp.where(mine, lanes, 0.0), axis=0, keepdims=True).astype(jnp.int32)
+            size = min(slot, total - start)
+            at = source * slot
+            rows_of[part, at : at + size, :] = got_ref[start : start + size, :]
+            if size < slot:
+                rows_of[part, at + size : at + slot, :] = jnp.zeros((slot - size, 128), jnp.float32)
+    places, group = [], 128 // slot
+    for first in range(0, blocks, group):
+        x = got_ref[pl.ds(first * chunk + chunk - 1, group, stride=chunk), :]
+        x = jnp.where(iota(x.shape, 1) < room, x, 0.0)
+        x = pltpu.roll(x, 0, 1, stride=slot, stride_axis=0)
+        places.append(jnp.sum(x, axis=0, keepdims=True))
+    place = jnp.concatenate(places, axis=1).astype(jnp.int32)
     landing = jnp.where(iota((cells, slots), 0) + 1 == place, 1.0, 0.0)
-    return [selected(landing, rows_of[part]) for part in range(parts)]
+    return selected(landing, jnp.concatenate([rows_of[part] for part in range(parts)], axis=1))
 
 
 def land(room, chunk, got_ref, force, rows_of):
     rows, cols, _ = force.shape
-    for part, x in enumerate(landed(room, chunk, rows * cols, got_ref, rows_of)):
-        force[:, :, part * 128 : part * 128 + 128] = x.reshape(rows, cols, 128)
-
-
-def tissue_steps(force, free, after_free, l_ref, shear, viscosity, up, down, left, right, mid, new):
+    force[...] = landed(room, chunk, rows * cols, got_ref, rows_of).reshape(force.shape)
+
+
+def tissue_steps(force, free, after_free, quarter, up, down, left, right, mid, new):
     rows = force.shape[0]
 
     def step(i, f_up, f_down):
         f = force[i]
-        s, v = lookup(l_ref[i], shear, 0), lookup(l_ref[i], viscosity, 0)
         at = lambda ref: ref[pl.ds(i, 1), :]
         lap = f_up + f_down + beside(f, at(left), at(right)) + lateral(f) - 6.0 * f
         mid[i] = free[i] + 0.25 * f
-        new[i] = after_free[i] + 0.75 * f + 0.25 * (s + v) * lap
+        new[i] = after_free[i] + 0.75 * f + quarter[i] * lap
 
     step(0, up[...], force[1])
     step(rows - 1, force[rows - 2], down[...])
@@ -484,23 +500,56 @@
 
 
 def land_and_step(
-    room, chunk, got_ref, free, after_free, l_ref, shear, viscosity, force, mid, new,
-    rows_of, up, down, left, right
+    room, chunk, got_ref, free, after_free, quarter, force_out, mid_out, new_out,
+    rows_of, field, mid, new, sems
 ):
-    rows, cols, _ = force.shape
-    cells = rows * cols
-    borders, start = [], cells
-    for ref in (up, down, left, right):
-        borders.append((ref, start))
-        start += ref.shape[0]
-    for part, x in enumerate(landed(room, chunk, start, got_ref, rows_of)):
+    rows, cols, depth = mid.shape
+    cells, parts = rows * cols, depth // 128
+    x = landed(room, chunk, cells + 2 * (rows + cols), got_ref, rows_of)
+    inside, copies = slice(8, 8 + cols), []
+    for part in range(parts):
         lanes = slice(part * 128, part * 128 + 128)
-        force[:, :, lanes] = x[:cells].reshape(rows, cols, 128)
-        for ref, first in borders:
-            ref[:, lanes] = x[first : first + ref.shape[0]]
-    tissue_steps(
-        force, free, after_free, l_ref, shear, viscosity, up, down, left, right, mid, new
-    )
+        border = lambda start, size: x[cells + start : cells + start + size, lanes]
+        field[0, part, inside, :] = border(0, cols)
+        field[1 : rows + 1, part, inside, :] = x[:cells, lanes].reshape(rows, cols, 128)
+        field[rows + 1, part, inside, :] = border(cols, cols)
+        field[1 : rows + 1, part, 7, :] = border(2 * cols, rows)
+        field[1 : rows + 1, part, 8 + cols, :] = border(2 * cols + rows, rows)
+        copies.append(
+            pltpu.make_async_copy(
+                field.at[pl.ds(1, rows), part, pl.ds(8, cols), :],
+                force_out.at[:, :, pl.ds(part * 128, 128)],
+                sems.at[part],
+            )
+        )
+        copies[-1].start()
+
+    def step(i, carry):
+        at = lambda row, part, start: field[row, part, start : start + cols, :]
+        tiles = [at(i + 1, part, 8) for part in range(parts)]
+        lane = iota(tiles[0].shape, 1)
+        lower = [0.0] + [pltpu.roll(tile, 1, 1) for tile in tiles]
+        upper = [pltpu.roll(tile, 127, 1) for tile in tiles] + [0.0]
+        for part, f in enumerate(tiles):
+            lanes = slice(part * 128, part * 128 + 128)
+            lap = at(i, part, 8) + at(i + 2, part, 8) + at(i + 1, part, 7) + at(i + 1, part, 9)
+            lap = lap + jnp.where(lane == 0, lower[part], lower[part + 1])
+            lap = lap + jnp.where(lane == 127, upper[part + 1], upper[part]) - 6.0 * f
+            mid[i, :, lanes] = free[i, :, lanes] + 0.25 * f
+            new[i, :, lanes] = after_free[i, :, lanes] + 0.75 * f + quarter[i, :, lanes] * lap
+        return carry
+
+    pieces = (sems.shape[0] - parts) // 2
+    for piece in range(pieces):
+        first, last = rows * piece // pieces, rows * (piece + 1) // pieces
+        lax.fori_loop(first, last, step, 0)
+        part = pl.ds(first, last - first)
+        for k, (ref, out) in enumerate(((mid, mid_out), (new, new_out))):
+            sem = sems.at[parts + 2 * piece + k]
+            copies.append(pltpu.make_async_copy(ref.at[part], out.at[part], sem))
+            copies[-1].start()
+    for copy in copies:
+        copy.wait()
 
 
 def far(*arrays):
@@ -568,21 +617,21 @@
     near = pl.BlockSpec(memory_space=pltpu.HBM)
     first, last = pl.pallas_call(
         functools.partial(border_columns, inner),
-        out_shape=(f32(side, span),) * 2,
+        out_shape=(pltpu.VMEM((side, span), jnp.float32),) * 2,
         in_specs=[near] * len(fields) + [SMEM, SMEM],
         out_specs=(VMEM, VMEM),
         scratch_shapes=buffers + [pltpu.SemaphoreType.DMA((len(buffers),))],
-        compiler_params=pltpu.CompilerParams(vmem_limit_bytes=63 << 20),
-    )(*far(*arrays), shear_table, viscosity_table)
+        compiler_params=pltpu.CompilerParams(vmem_limit_bytes=40 << 20),
+    )(*far(*arrays, shear_table, viscosity_table))
     left, right = swap(first, last, "gy")
     pause = pl.pallas_call(
         cover,
         out_shape=f32(8, 128),
-        in_specs=[near],
+        in_specs=[pl.BlockSpec(memory_space=pl.ANY)],
         out_specs=VMEM,
         compiler_params=pltpu.CompilerParams(vmem_limit_bytes=1 << 20),
         cost_estimate=pl.CostEstimate(flops=2 * 10**10, bytes_accessed=10**9, transcendentals=0),
-    )(*far(first))
+    )(first)
     block, tissue = f32(deep, across, span), f32(rows, cols, depth)
     mid, free = run(
         first_steps,
@@ -620,11 +669,11 @@
     match, placed = pl.pallas_call(
         functools.partial(address, grid, (rows, cols), room, chunk),
         out_shape=(f32(blocks * chunk, parts * count), f32(blocks * chunk, 128)),
-        in_specs=[VMEM, VMEM, near],
+        in_specs=[VMEM, VMEM, pl.BlockSpec(memory_space=pl.ANY)],
         out_specs=(VMEM, VMEM),
         compiler_params=pltpu.CompilerParams(vmem_limit_bytes=16 << 20),
         cost_estimate=pl.CostEstimate(flops=10**8, bytes_accessed=10**7, transcendentals=0),
-    )(own_map.T, slot_table.T, *far(first))
+    )(own_map.T, slot_table.T, first)
     media = (pressure, courant, nonlinearity, absorption)
     mid, new, lines = run(
         second_acoustic,
@@ -655,9 +704,9 @@
     )
     send = send.reshape(blocks, chunk, 128)
     got = lax.all_to_all(send, ("gx", "gy"), split_axis=0, concat_axis=0, tiled=True)
-    pressure_mid, pressure_new, free, after_free = run(
+    pressure_mid, pressure_new, free, after_free, quarter = run(
         second_elastic,
-        (block, block, tissue, tissue),
+        (block, block, tissue, tissue, tissue),
         *far(mid, new, mids, news, free, displacement, displacement_prev, layer_labels),
         shear_table,
         viscosity_table,
@@ -666,34 +715,33 @@
         tables=(8, 9),
         limit=24,
     )
-    arrived = scratch(depth // 128, blocks * room, 128)
+    slot = 8
+    while slot < room:
+        slot *= 2
+    arrived = scratch(parts, blocks * slot, 128)
 
     def direct(got, *rest):
-        return run(
+        return pl.pallas_call(
             functools.partial(land_and_step, room, chunk),
-            (tissue,) * 3,
-            got,
-            *rest,
-            scratch_shapes=[arrived] + [scratch(n, depth) for n in (cols, cols, rows, rows)],
-            tables=(4, 5),
-        )
+            out_shape=(hbm(rows, cols, depth),) * 3,
+            in_specs=[VMEM] * 4,
+            out_specs=(near,) * 3,
+            scratch_shapes=[
+                arrived,
+                scratch(rows + 2, parts, cols + 16, 128),
+                scratch(rows, cols, depth),
+                scratch(rows, cols, depth),
+                pltpu.SemaphoreType.DMA((parts + 8,)),
+            ],
+            compiler_params=pltpu.CompilerParams(vmem_limit_bytes=24 << 20),
+        )(got, *rest)
 
     def by_faces(got, *rest):
-        force = run(
-            functools.partial(land, room, chunk), tissue, got, scratch_shapes=[arrived]
-        )
+        force = run(functools.partial(land, room, chunk), tissue, got, scratch_shapes=[arrived])
         up, down = swap(force[0], force[rows - 1], "gx")
         at_left, at_right = swap(force[:, 0], force[:, cols - 1], "gy")
         mid, new = run(
-            tissue_steps,
-            (tissue,) * 2,
-            force,
-            *rest,
-            up,
-            down,
-            at_left,
-            at_right,
-            tables=(4, 5),
+            tissue_steps, (tissue,) * 2, force, *rest, up, down, at_left, at_right, limit=16
         )
         return force, mid, new
 
@@ -704,9 +752,7 @@
         got.reshape(blocks * chunk, 128),
         free,
         after_free,
-        layer_labels,
-        shear_table,
-        viscosity_table,
+        quarter,
     )
     return (pressure_mid, pressure_new, tissue_force, displacement_mid, displacement_new)
 

time: 56.2 us -> 53.7 us (0.956)
  Pallas kernels: 26.2 us -> 23.5 us
    pallas_call x6 -> x5, Pallas kernels: 21.2 us -> 16.2 us  [run(): pl.pallas_call(kernel, out_shape=out, in_specs=specs, out_specs=jax.tree....]
    pallas_call x2 -> x3, Pallas kernels: 3.25 us -> 5.52 us  [the longest x1 3.01 us: direct(): pl.pallas_call(functools.partial(land_and_step, room, chunk), out_shape=(...]
    unnamed x42 -> x38, local copies, waits for them, and re-layouts: 1.76 us -> 1.77 us
  transfers between devices with their start and end apart: 5 -> 5, of which waited for: 2 -> 3; matrix products, arithmetic and copies ran while one was open for 0% -> 0% of each run, Pallas kernels for 29% -> 29%
where the time goes in v4:
time: 53.7 us; the launch traced here: 53.3 us
  Pallas kernels  23.5 us (44%)
  starting transfers between devices  18.2 us (34%)
  waiting for transfers between devices  7.64 us (14%)
  local copies, waits for them, and re-layouts  1.77 us (3%)
  between operations  1.56 us (3%)
  other arithmetic  0.69 us (1%)
    pallas_call x5, Pallas kernels, run(): pl.pallas_call(kernel, out_shape=out, in_specs=specs, out_specs=jax.tree....  16.2 us
    ppermute x4, starting transfers between devices, swap(): return (lax.ppermute(last, axis, up), lax.ppermute(first, axis, down))  9.14 us
    all_to_all x1, starting transfers between devices, local(): lax.all_to_all(send, ('gx', 'gy'), split_axis=0, concat_axis=0, tiled=True)  9.02 us
    all_to_all x1, waiting for transfers between devices, local(): lax.all_to_all(send, ('gx', 'gy'), split_axis=0, concat_axis=0, tiled=True)  4.58 us
    ppermute x4, waiting for transfers between devices, swap(): return (lax.ppermute(last, axis, up), lax.ppermute(first, axis, down))  3.06 us
    pallas_call x1, Pallas kernels, direct(): pl.pallas_call(functools.partial(land_and_step, room, chunk), out_shape=(...  3.01 us
    pallas_call x1, Pallas kernels, local(): pl.pallas_call(functools.partial(border_columns, inner), out_shape=(pltpu...  2.5 us
    pallas_call x1, Pallas kernels, local(): pl.pallas_call(functools.partial(address, grid, (rows, cols), room, chunk...  1.8 us
  transfers between devices with their start and end apart: 5, of which 3 were waited for; matrix products, arithmetic and copies ran while one was open for 0% of the time, Pallas kernels for 29%

profile of v4, /device:TPU:0, one launch (start us, length us, event | category | flops | bytes accessed | tf_op | source)
XLA Modules:
  0.0 53.3 jit_solution(15968227250981726563)
XLA Ops:
  0.6 2.5 %shard_map.155 = (f32[104,768]{1,0:T(8,128)S(1)}, f32[104,768]{1,0:T(8,128)S(1)}) custom-call(f32[24,16,768]{2,1,0:T(8,128)} %p_ref.7, f32[24,16,768]{2,1,0:T(8,128)} %q_ref.1, f32[24,16,768]{2,1,0:T(8,128)} %c_ref.7, f32[24,16,768]{2,1,0:T(8,128)} %n_ref.5, f32[24,16,768]{2,1,0:T(8,128)} %a_ref.5, f32[16,32,384]{2,1,0:T(8,128)} %d_ref.5, ...), custom_call_target="tpu_custom_call" | custom-call | tf_op jit(solution)/shard_map/pallas_call | solution.py:618
  3.1 5.0 %collective-permute-start.4 = (f32[104,768]{1,0:T(8,128)S(1)}, f32[104,768]{1,0:T(8,128)S(1)}, u32[]{:S(2)}, u32[]{:S(2)}) collective-permute-start(f32[104,768]{1,0:T(8,128)S(1)} %get-tuple-element.55), channel_id=1, source_target_pairs={{0,1},{1,2},{2,3},{4,5},{5,6},{6,7},{8,9},{9,10},{10,11},{12,13},{... | collective-permute-start | bytes 958472 | tf_op jit(solution)/shard_map/ppermute | solution.py:563
  8.2 1.6 %collective-permute-start.5 = (f32[104,768]{1,0:T(8,128)S(1)}, f32[104,768]{1,0:T(8,128)S(1)}, u32[]{:S(2)}, u32[]{:S(2)}) collective-permute-start(f32[104,768]{1,0:T(8,128)S(1)} %get-tuple-element.53._), channel_id=1, source_target_pairs={{1,0},{2,1},{3,2},{5,4},{6,5},{7,6},{9,8},{10,9},{11,10},{13,12},{... | collective-permute-start | bytes 958472 | tf_op jit(solution)/shard_map/ppermute | solution.py:563
  9.8 0.3 copy-done.2
  10.1 0.4 copy-done.3
  10.5 0.2 copy-done.4
  10.7 0.2 copy-done.5
  10.9 0.2 copy-done.6
  11.2 0.4 copy-done.9
  11.5 5.0 %shard_map.157 = (f32[24,16,768]{2,1,0:T(8,128)S(1)}, f32[16,32,384]{2,1,0:T(8,128)S(1)}) custom-call(f32[24,16,768]{2,1,0:T(8,128)S(1)} %copy-done, f32[24,16,768]{2,1,0:T(8,128)S(1)} %copy-done.9, f32[24,16,768]{2,1,0:T(8,128)S(1)} %copy-done.1, f32[24,16,768]{2,1,0:T(8,128)S(1)} %copy-done.2, f32[24,16,768]{2,1,0:T(8,128)S(1)} %copy-done.3, ...), custom_call_target="tpu_custom_call" | custom-call | flops 204554880 | bytes 10227744 | tf_op jit(solution)/shard_map/pallas_call | solution.py:590
  16.5 3.0 %collective-permute-done.5.right = f32[104,768]{1,0:T(8,128)S(1)} collective-permute-done((f32[104,768]{1,0:T(8,128)S(1)}, f32[104,768]{1,0:T(8,128)S(1)}, u32[]{:S(2)}, u32[]{:S(2)}) %collective-permute-start.5) | collective-permute-done | bytes 319520 | tf_op jit(solution)/shard_map/ppermute | solution.py:563
  19.5 0.6 %shard_map.159 = (f32[120,768]{1,0:T(8,128)S(1)}, f32[120,768]{1,0:T(8,128)S(1)}) custom-call(f32[24,16,768]{2,1,0:T(8,128)S(1)} %copy-done, f32[24,16,768]{2,1,0:T(8,128)S(1)} %copy-done.1, f32[24,16,768]{2,1,0:T(8,128)S(1)} %get-tuple-element.54.mid_ref, f32[16,32,384]{2,1,0:T(8,128)S(1)} %copy-done.4, f32[16,32,384]{2,1,0:T(8,128)S(1)} %copy-done.5, ...), custom_call_target="tpu_custom_call" | custom-call | flops 161219200 | bytes 8060960 | tf_op jit(solution)/shard_map/pallas_call | solution.py:590
  20.2 1.3 %collective-permute-start.6 = (f32[120,768]{1,0:T(8,128)S(1)}, f32[120,768]{1,0:T(8,128)S(1)}, u32[]{:S(2)}, u32[]{:S(2)}) collective-permute-start(f32[120,768]{1,0:T(8,128)S(1)} %get-tuple-element.63), channel_id=1, source_target_pairs={{0,4},{4,8},{8,12},{1,5},{5,9},{9,13},{2,6},{6,10},{10,14},{3,7},{... | collective-permute-start | bytes 1105928 | tf_op jit(solution)/shard_map/ppermute | solution.py:563
  21.5 1.3 %collective-permute-start.7 = (f32[120,768]{1,0:T(8,128)S(1)}, f32[120,768]{1,0:T(8,128)S(1)}, u32[]{:S(2)}, u32[]{:S(2)}) collective-permute-start(f32[120,768]{1,0:T(8,128)S(1)} %get-tuple-element.60._), channel_id=1, source_target_pairs={{4,0},{8,4},{12,8},{5,1},{9,5},{13,9},{6,2},{10,6},{14,10},{7,3},{... | collective-permute-start | bytes 1105928 | tf_op jit(solution)/shard_map/ppermute | solution.py:563
  22.8 1.8 %shard_map.160 = (f32[640,288]{1,0:T(8,128)S(1)}, f32[640,128]{1,0:T(8,128)S(1)}) custom-call(s32[8,12]{1,0:T(8,128)S(1)} %bitcast.14, s32[8,12]{1,0:T(8,128)S(1)} %bitcast.15, f32[120,768]{1,0:T(8,128)S(1)} %get-tuple-element.60._), custom_call_target="tpu_custom_call" | custom-call | flops 100000000 | bytes 10000000 | tf_op jit(solution)/shard_map/pallas_call | solution.py:669
  24.6 2.0 %shard_map.158 = (f32[24,16,768]{2,1,0:T(8,128)S(1)}, f32[24,16,768]{2,1,0:T(8,128)S(1)}, f32[288,128]{1,0:T(8,128)S(1)}) custom-call(f32[24,16,768]{2,1,0:T(8,128)S(1)} %copy-done, f32[24,16,768]{2,1,0:T(8,128)S(1)} %copy-done.1, f32[24,16,768]{2,1,0:T(8,128)S(1)} %copy-done.2, f32[24,16,768]{2,1,0:T(8,128)S(1)} %copy-done.3, ...), custom_call_target="tpu_custom_call" | custom-call | flops 180879360 | bytes 9043968 | tf_op jit(solution)/shard_map/pallas_call | solution.py:590
  26.7 0.1 collective-permute-done.7.after
  26.8 1.8 %shard_map.161 = (f32[2,16,768]{2,1,0:T(8,128)}, f32[4,16,768]{2,1,0:T(8,128)}, f32[640,128]{1,0:T(8,128)}) custom-call(f32[24,16,768]{2,1,0:T(8,128)S(1)} %copy-done, f32[24,16,768]{2,1,0:T(8,128)S(1)} %copy-done.1, f32[24,16,768]{2,1,0:T(8,128)S(1)} %copy-done.2, f32[24,16,768]{2,1,0:T(8,128)S(1)} %copy-done.3, ...), custom_call_target="tpu_custom_call" | custom-call | flops 182190080 | bytes 9109504 | tf_op jit(solution)/shard_map/pallas_call | solution.py:590
  28.6 9.0 %all-to-all-start = ((f32[16,40,128]{2,1,0:T(8,128)}), f32[16,40,128]{2,1,0:T(8,128)S(1)}, u32[]{:S(2)}, u32[]{:S(2)}) async-start(f32[16,40,128]{2,1,0:T(8,128)} %bitcast.18), calls=%async_computation | async-start | bytes 655360 | tf_op jit(solution)/shard_map/all_to_all | solution.py:706
  37.6 6.8 %shard_map.162 = (f32[24,16,768]{2,1,0:T(8,128)}, f32[24,16,768]{2,1,0:T(8,128)}, f32[16,32,384]{2,1,0:T(8,128)S(1)}, f32[16,32,384]{2,1,0:T(8,128)S(1)}, f32[16,32,384]{2,1,0:T(8,128)S(1)}) custom-call(f32[24,16,768]{2,1,0:T(8,128)} %copy-done.10, f32[24,16,768]{2,1,0:T(8,128)} %copy-done.14, f32[2,16,768]{2,1,0:T(8,128)} %get-tuple-element.64.mids, ...), custom_call_target="tpu_custom_call" | custom-call | flops 237896320 | bytes 11894816 | tf_op jit(solution)/shard_map/pallas_call | solution.py:590
  44.4 4.6 %all-to-all-done = f32[16,40,128]{2,1,0:T(8,128)S(1)} async-done(((f32[16,40,128]{2,1,0:T(8,128)}), f32[16,40,128]{2,1,0:T(8,128)S(1)}, u32[]{:S(2)}, u32[]{:S(2)}) %all-to-all-start) | async-done | bytes 327712 | tf_op jit(solution)/shard_map/all_to_all | solution.py:706
  48.9 0.7 %slice_reduce_fusion = f32[]{:T(128)} fusion(f32[16,40,128]{2,1,0:T(8,128)S(1)} %all-to-all-done), kind=kLoop, calls=%fused_computation.4 | loop fusion | flops 15 | bytes 68 | tf_op jit(solution)/shard_map/reduce_max | solution.py:749
  50.3 3.0 %conditional.1 = ((f32[16,32,384]{2,1,0:T(8,128)}, f32[16,32,384]{2,1,0:T(8,128)}, f32[16,32,384]{2,1,0:T(8,128)})) conditional(s32[]{:T(128)} %convert_element_type.3, (f32[640,128]{1,0:T(8,128)S(1)}, f32[16,32,384]{2,1,0:T(8,128)S(1)}, f32[16,32,384]{2,1,0:T(8,128)S(1)}, f32[16,32,384]{2,1,0:T(8,128)S(1)}) %tuple.23, (f32[640,128]{1,0:T(8,128)S(1)}, ...), branch_computations={%region_1.0_spmd, %region_2.0_spmd} | conditional | flops 119603200 | bytes 10109148 | solution.py:748
  50.3 3.0 %branch_0_fun.1 = (f32[16,32,384]{2,1,0:T(8,128)}, f32[16,32,384]{2,1,0:T(8,128)}, f32[16,32,384]{2,1,0:T(8,128)}) custom-call(f32[640,128]{1,0:T(8,128)S(1)} %get-tuple-element.16.got_ref, f32[16,32,384]{2,1,0:T(8,128)S(1)} %get-tuple-element.17.free, f32[16,32,384]{2,1,0:T(8,128)S(1)} %get-tuple-element.18.after_free, ...), custom_call_target="tpu_custom_call" | custom-call | tf_op jit(solution)/shard_map/cond/branch_0_fun/pallas_call | solution.py:724
  (35 shorter events, 0.1 us)
Async XLA Ops:
  3.1 13.4 %collective-permute-start.4 = (f32[104,768]{1,0:T(8,128)S(1)}, f32[104,768]{1,0:T(8,128)S(1)}, u32[]{:S(2)}, u32[]{:S(2)}) collective-permute-start(f32[104,768]{1,0:T(8,128)S(1)} %get-tuple-element.55), channel_id=1, source_target_pairs={{0,1},{1,2},{2,3},{4,5},{5,6},{6,7},{8,9},{9,10},{10,11},{12,13},{... | collective-permute-start | bytes 958472 | tf_op jit(solution)/shard_map/ppermute | solution.py:563
  8.1 1.7 %copy-start = (f32[24,16,768]{2,1,0:T(8,128)S(1)}, f32[24,16,768]{2,1,0:T(8,128)}, u32[]{:S(2)}) copy-start(f32[24,16,768]{2,1,0:T(8,128)} %p_ref.7) | copy-start | bytes 3538948
  8.1 1.7 %copy-start.1 = (f32[24,16,768]{2,1,0:T(8,128)S(1)}, f32[24,16,768]{2,1,0:T(8,128)}, u32[]{:S(2)}) copy-start(f32[24,16,768]{2,1,0:T(8,128)} %c_ref.7) | copy-start | bytes 3538948
  8.1 2.0 %copy-start.2 = (f32[24,16,768]{2,1,0:T(8,128)S(1)}, f32[24,16,768]{2,1,0:T(8,128)}, u32[]{:S(2)}) copy-start(f32[24,16,768]{2,1,0:T(8,128)} %n_ref.5) | copy-start | bytes 3538948
  8.2 2.3 %copy-start.3 = (f32[24,16,768]{2,1,0:T(8,128)S(1)}, f32[24,16,768]{2,1,0:T(8,128)}, u32[]{:S(2)}) copy-start(f32[24,16,768]{2,1,0:T(8,128)} %a_ref.5) | copy-start | bytes 3538948
  8.2 2.5 %copy-start.4 = (f32[16,32,384]{2,1,0:T(8,128)S(1)}, f32[16,32,384]{2,1,0:T(8,128)}, u32[]{:S(2)}) copy-start(f32[16,32,384]{2,1,0:T(8,128)} %d_ref.5) | copy-start | bytes 2359300
  8.2 2.7 %copy-start.5 = (f32[16,32,384]{2,1,0:T(8,128)S(1)}, f32[16,32,384]{2,1,0:T(8,128)}, u32[]{:S(2)}) copy-start(f32[16,32,384]{2,1,0:T(8,128)} %b_ref.5) | copy-start | bytes 2359300
  8.2 3.0 %copy-start.6 = (s32[16,32,384]{2,1,0:T(8,128)S(1)}, s32[16,32,384]{2,1,0:T(8,128)}, u32[]{:S(2)}) copy-start(s32[16,32,384]{2,1,0:T(8,128)} %l_ref.5) | copy-start | bytes 2359300
  8.2 3.3 %copy-start.9 = (f32[24,16,768]{2,1,0:T(8,128)S(1)}, f32[24,16,768]{2,1,0:T(8,128)}, u32[]{:S(2)}) copy-start(f32[24,16,768]{2,1,0:T(8,128)} %q_ref.1) | copy-start | bytes 3538948
  8.2 3.3 %copy-start.15 = (f32[4]{0:T(128)S(1)}, f32[4]{0:T(128)}, u32[]{:S(2)}) copy-start(f32[4]{0:T(128)} %shear.5) | copy-start | bytes 52
  8.2 3.3 %copy-start.16 = (f32[4]{0:T(128)S(1)}, f32[4]{0:T(128)}, u32[]{:S(2)}) copy-start(f32[4]{0:T(128)} %viscosity.5) | copy-start | bytes 52
  8.2 11.3 %collective-permute-start.5 = (f32[104,768]{1,0:T(8,128)S(1)}, f32[104,768]{1,0:T(8,128)S(1)}, u32[]{:S(2)}, u32[]{:S(2)}) collective-permute-start(f32[104,768]{1,0:T(8,128)S(1)} %get-tuple-element.53._), channel_id=1, source_target_pairs={{1,0},{2,1},{3,2},{5,4},{6,5},{7,6},{9,8},{10,9},{11,10},{13,12},{... | collective-permute-start | bytes 958472 | tf_op jit(solution)/shard_map/ppermute | solution.py:563
  16.5 3.7 %copy-start.11 = (f32[16,32,384]{2,1,0:T(8,128)}, f32[16,32,384]{2,1,0:T(8,128)S(1)}, u32[]{:S(2)}) copy-start(f32[16,32,384]{2,1,0:T(8,128)S(1)} %get-tuple-element.59.free_ref) | copy-start | bytes 2359300
  16.5 10.3 %copy-start.7 = (f32[104,768]{1,0:T(8,128)}, f32[104,768]{1,0:T(8,128)S(1)}, u32[]{:S(2)}) copy-start(f32[104,768]{1,0:T(8,128)S(1)} %collective-permute-done.4.left) | copy-start | bytes 958468
  19.5 7.3 %copy-start.8 = (f32[104,768]{1,0:T(8,128)}, f32[104,768]{1,0:T(8,128)S(1)}, u32[]{:S(2)}) copy-start(f32[104,768]{1,0:T(8,128)S(1)} %collective-permute-done.5.right) | copy-start | bytes 958468
  19.5 3.3 %copy-start.17 = (s32[12,8]{0,1:T(8,128)S(1)}, s32[12,8]{0,1:T(8,128)}, u32[]{:S(2)}) copy-start(s32[12,8]{0,1:T(8,128)} %param.19) | copy-start | bytes 1156
  19.5 3.3 %copy-start.18 = (s32[12,8]{0,1:T(8,128)S(1)}, s32[12,8]{0,1:T(8,128)}, u32[]{:S(2)}) copy-start(s32[12,8]{0,1:T(8,128)} %param.20) | copy-start | bytes 1156
  20.2 6.5 %collective-permute-start.6 = (f32[120,768]{1,0:T(8,128)S(1)}, f32[120,768]{1,0:T(8,128)S(1)}, u32[]{:S(2)}, u32[]{:S(2)}) collective-permute-start(f32[120,768]{1,0:T(8,128)S(1)} %get-tuple-element.63), channel_id=1, source_target_pairs={{0,4},{4,8},{8,12},{1,5},{5,9},{9,13},{2,6},{6,10},{10,14},{3,7},{... | collective-permute-start | bytes 1105928 | tf_op jit(solution)/shard_map/ppermute | solution.py:563
  21.5 5.3 %collective-permute-start.7 = (f32[120,768]{1,0:T(8,128)S(1)}, f32[120,768]{1,0:T(8,128)S(1)}, u32[]{:S(2)}, u32[]{:S(2)}) collective-permute-start(f32[120,768]{1,0:T(8,128)S(1)} %get-tuple-element.60._), channel_id=1, source_target_pairs={{4,0},{8,4},{12,8},{5,1},{9,5},{13,9},{6,2},{10,6},{14,10},{7,3},{... | collective-permute-start | bytes 1105928 | tf_op jit(solution)/shard_map/ppermute | solution.py:563
  26.7 1.9 %copy-start.10 = (f32[24,16,768]{2,1,0:T(8,128)}, f32[24,16,768]{2,1,0:T(8,128)S(1)}, u32[]{:S(2)}) copy-start(f32[24,16,768]{2,1,0:T(8,128)S(1)} %get-tuple-element.56.mid_ref) | copy-start | bytes 3538948
  26.7 1.9 %copy-start.14 = (f32[24,16,768]{2,1,0:T(8,128)}, f32[24,16,768]{2,1,0:T(8,128)S(1)}, u32[]{:S(2)}) copy-start(f32[24,16,768]{2,1,0:T(8,128)S(1)} %get-tuple-element.57.new_ref) | copy-start | bytes 3538948
  26.7 1.8 %copy-start.12 = (f32[120,768]{1,0:T(8,128)}, f32[120,768]{1,0:T(8,128)S(1)}, u32[]{:S(2)}) copy-start(f32[120,768]{1,0:T(8,128)S(1)} %collective-permute-done.6.before) | copy-start | bytes 1105924
  26.8 1.8 %copy-start.13 = (f32[120,768]{1,0:T(8,128)}, f32[120,768]{1,0:T(8,128)S(1)}, u32[]{:S(2)}) copy-start(f32[120,768]{1,0:T(8,128)S(1)} %collective-permute-done.7.after) | copy-start | bytes 1105924
  28.6 20.4 %all-to-all-start = ((f32[16,40,128]{2,1,0:T(8,128)}), f32[16,40,128]{2,1,0:T(8,128)S(1)}, u32[]{:S(2)}, u32[]{:S(2)}) async-start(f32[16,40,128]{2,1,0:T(8,128)} %bitcast.18), calls=%async_computation | async-start | bytes 655360 | tf_op jit(solution)/shard_map/all_to_all | solution.py:706

commit v5 on v4

--- a/solution.py
+++ b/solution.py
@@ -38,6 +38,26 @@
     return jnp.concatenate(sums, axis=0)
 
 
+class Facing:
+    def __init__(self, odd, at_even, at_odd):
+        self.odd, self.at_even, self.at_odd = odd, at_even, at_odd
+        self.shape = at_even.shape
+
+    def __getitem__(self, at):
+        return jnp.where(self.odd, self.at_odd[at], self.at_even[at])
+
+
+def facing(axis, inner, outer):
+    odd = lax.rem(lax.axis_index(axis), 2) == 1
+    return Facing(odd, outer, inner), Facing(odd, inner, outer)
+
+
+def by_parity(axis, both, inner, outer):
+    odd = lax.rem(lax.axis_index(axis), 2)
+    inner[...] = both[1 - odd]
+    outer[...] = both[odd]
+
+
 def at_ends(shape, first, last):
     row = lax.broadcasted_iota(jnp.int32, shape, 0)
     return jnp.where(row == 0, first, jnp.where(row == shape[0] - 1, last, 0.0))
@@ -75,37 +95,50 @@
 
 def border_columns(inner, *refs):
     count = len(inner)
-    fields, (shear, viscosity, left, right) = refs[:count], refs[count : count + 4]
-    buffers, sems = refs[count + 4 : -1], refs[-1]
-    copies, sides, k = [], ([], []), 0
-    for field, more in zip(fields, inner):
-        last = field.shape[1] - 1
-        for side, js in enumerate(((0, 1)[: 1 + more], (last, last - 1)[: 1 + more])):
-            for j in js:
-                copies.append(pltpu.make_async_copy(field.at[:, j, :], buffers[k], sems.at[k]))
-                sides[side].append(buffers[k])
-                k += 1
-    for copy in copies:
-        copy.start()
-    for copy in copies:
-        copy.wait()
-    for columns, out in zip(sides, (left, right)):
-        p, p_in, q, c, n, a, d, d_in, b, b_in, labels = [column[...] for column in columns]
-        deep, (rows, depth) = p.shape[0], d.shape
+    fields, (shear, viscosity, inner_out, outer_out) = refs[:count], refs[count : count + 4]
+    buffers, both, sems = refs[count + 4 : -2], refs[-2], refs[-1]
+    left, right = both.at[0], both.at[1]
+    groups, k = [], 0
+    for some in (range(0, 5), range(5, count)):
+        for side in range(2):
+            group = []
+            for field in some:
+                last = fields[field].shape[1] - 1
+                for step in range(1 + inner[field]):
+                    j = last - step if side else step
+                    source = fields[field].at[:, j, :]
+                    copy = pltpu.make_async_copy(source, buffers[k], sems.at[k])
+                    copy.start()
+                    group.append((copy, buffers[k]))
+                    k += 1
+            groups.append(group)
+
+    def columns(group):
+        for copy, _ in group:
+            copy.wait()
+        return [buffer[...] for _, buffer in group]
+
+    for group, out in zip(groups[:2], (left, right)):
+        p, p_in, q, c, n, a = columns(group)
+        deep = p.shape[0]
         lap = beside(p, 0.0, 0.0) + p_in + lateral(p) - 6.0 * p
         out[0:deep] = p
         out[deep : 2 * deep] = c
         out[2 * deep : 3 * deep] = wave(p, q, lap, c, n, a)
+    top = 3 * deep
+    for group, out in zip(groups[2:], (left, right)):
+        d, d_in, b, b_in, labels = columns(group)
+        rows, depth = d.shape
         e, e_in = d - b, d_in - b_in
         s, v = lookup(labels, shear, 0), lookup(labels, viscosity, 0)
         lap_d = beside(d, 0.0, 0.0) + d_in + lateral(d) - 6.0 * d
         lap_e = beside(e, 0.0, 0.0) + e_in + lateral(e) - 6.0 * e
-        top = 3 * deep
         first, last = slice(0, depth), slice(depth, 2 * depth)
         out[top : top + rows, first] = d
         out[top : top + rows, last] = e
         out[top + rows : top + 2 * rows, first] = labels.astype(jnp.float32) + 1.0
         out[top + rows : top + 2 * rows, last] = d + e + s * lap_d + v * lap_e
+    by_parity("gy", both, inner_out, outer_out)
 
 
 def cover(_, out):
@@ -149,8 +182,11 @@
 
 
 def border_rows(
-    p_ref, c_ref, mid_ref, d_ref, b_ref, l_ref, free_ref, shear, viscosity, left, right, up, down
+    p_ref, c_ref, mid_ref, d_ref, b_ref, l_ref, free_ref, shear, viscosity, beside_in, beside_out,
+    inner_out, outer_out, both
 ):
+    left, right = facing("gy", beside_in, beside_out)
+    up, down = both.at[0], both.at[1]
     deep, across, _ = p_ref.shape
     rows, cols, depth = d_ref.shape
     half = cols // 2
@@ -176,6 +212,7 @@
         out[end + 2 : end + 3] = left[at]
         out[end + 3 : end + 4] = right[at]
         out[end + 4 : end + 8] = jnp.zeros((4, out.shape[1]), jnp.float32)
+    by_parity("gx", both, inner_out, outer_out)
 
 
 def dot(x, y, contract=((1,), (0,))):
@@ -196,7 +233,7 @@
     return lax.broadcasted_iota(jnp.int32, shape, dim)
 
 
-def address(grid, tile, room, chunk, own_ref, slot_ref, _, match, placed):
+def address(grid, tile, room, chunk, own_ref, slot_ref, _, match, ends, placed):
     (tiles_down, tiles_across), (rows, cols) = grid, tile
     blocks, cells = tiles_down * tiles_across, rows * cols
     wide, tall = own_ref.shape
@@ -259,7 +296,11 @@
     ]
     for part in range(parts):
         here = at - part * room
-        match[:, part * count : part * count + count] = sum(ones(here == b) for b in base)
+        one_hot = sum(ones(here == b) for b in base).astype(jnp.bfloat16)
+        match[:, part * count : part * count + count] = one_hot
+        for k, lines in enumerate((slice(0, wide), slice(count - wide, count))):
+            first = (2 * part + k) * wide
+            ends[:, first : first + wide] = one_hot[:, lines]
     lanes = (128, count)
     row, lane = iota((total, 128), 0), iota((total, 128), 1)
     result = jnp.where((row % chunk == chunk - 1) & (lane == room), full, 0.0)
@@ -309,8 +350,10 @@
 
 
 def second_acoustic(
-    p_ref, c_ref, n_ref, a_ref, mid_ref, left, right, mid, new, lines, beyond_l, beyond_r, pairs
+    p_ref, c_ref, n_ref, a_ref, mid_ref, match_ref, placed_ref, beside_in, beside_out,
+    mid, new, send, beyond_l, beyond_r, pairs
 ):
+    left, right = facing("gy", beside_in, beside_out)
     deep, across, _ = p_ref.shape
     mid[...] = mid_ref[...]
     for j, side, beyond in ((0, left, beyond_l), (across - 1, right, beyond_r)):
@@ -336,20 +379,19 @@
     put(pairs, 0, jnp.zeros(new.shape[1:], jnp.float32))
     put(pairs, (deep // 2 - 1) * across, jnp.zeros(new.shape[1:], jnp.float32))
     lax.fori_loop(1, deep // 2 - 1, body, 0)
-    count = deep // 2 * (across // 2)
-    for part, x in enumerate(paired_lanes(even_and_odd(pairs, count))):
-        lines[part * count : part * count + count] = 0.125 * x
+    lines = paired_lanes(even_and_odd(pairs, deep // 2 * (across // 2)))
+    send[...] = selected(match_ref[...], 0.125 * jnp.concatenate(lines, axis=0)) + placed_ref[...]
 
 
 def ends_and_send(
-    p_ref, c_ref, n_ref, a_ref, mid_ref, lines_ref, match_ref, placed_ref,
-    before, after, left, right, mids, news, send, lines, pairs
+    p_ref, c_ref, n_ref, a_ref, mid_ref, sent_ref, ends_ref,
+    beside_in, beside_out, near_in, near_out, mids, news, send, pairs
 ):
+    left, right = facing("gy", beside_in, beside_out)
+    before, after = facing("gx", near_in, near_out)
     deep, across, _ = p_ref.shape
-    count = deep // 2 * (across // 2)
     cols = (before.shape[0] - 8 - 3 * across) // 2
     corners = 3 * across + 2 * cols
-    lines[...] = lines_ref[...]
     media = (p_ref, c_ref, n_ref, a_ref)
 
     def beyond(side, j, i):
@@ -357,6 +399,7 @@
             i, j : j + 1, :
         ]
 
+    lines = []
     for k, (i, inner, more, side) in enumerate(
         ((0, 1, 2, before), (deep - 1, deep - 2, deep - 3, after))
     ):
@@ -374,18 +417,19 @@
         mids[k] = m
         news[2 * k] = new
         news[2 * k + 1] = new_in
-        put(pairs, 0, force + force_in)
-        half = across // 2
-        for part, x in enumerate(paired_lanes(even_and_odd(pairs, half))):
-            at = part * count + (0 if k == 0 else count - half)
-            lines[at : at + half] = 0.125 * x
-    send[...] = selected(match_ref[...], lines[...]) + placed_ref[...]
+        put(pairs, k * across, force + force_in)
+    half = across // 2
+    lines = paired_lanes(even_and_odd(pairs, 2 * half))
+    send[...] = sent_ref[...] + selected(ends_ref[...], 0.125 * jnp.concatenate(lines, axis=0))
 
 
 def second_elastic(
     mid_ref, new_ref, mids, news, free_ref, d_ref, b_ref, l_ref, shear, viscosity,
-    before, after, left, right, mid, new, free, after_free, quarter, d_first, d_last, f_first, f_last
+    beside_in, beside_out, near_in, near_out,
+    mid, new, free, after_free, quarter, d_first, d_last, f_first, f_last
 ):
+    left, right = facing("gy", beside_in, beside_out)
+    before, after = facing("gx", near_in, near_out)
     deep, across, _ = mid.shape
     mid[...] = mid_ref[...]
     new[...] = new_ref[...]
@@ -563,6 +607,15 @@
     return lax.ppermute(last, axis, up), lax.ppermute(first, axis, down)
 
 
+def swap_pairs(inner, outer, axis):
+    size = lax.axis_size(axis)
+    pairs = lambda first: [
+        pair for i in range(first, size - 1, 2) for pair in ((i, i + 1), (i + 1, i))
+    ]
+    outer = lax.ppermute(outer, axis, pairs(1))
+    return lax.ppermute(inner, axis, pairs(0)), outer
+
+
 def local(
     pressure,
     pressure_prev,
@@ -581,6 +634,7 @@
     rows, cols, depth = displacement.shape
     f32 = lambda *shape: jax.ShapeDtypeStruct(shape, jnp.float32)
     hbm = lambda *shape: pltpu.HBM(shape, jnp.float32)
+    half = lambda *shape: jax.ShapeDtypeStruct(shape, jnp.bfloat16)
     scratch = lambda *shape: pltpu.VMEM(shape, jnp.float32)
 
     def run(kernel, out, *args, scratch_shapes=(), tables=(), weight=1, limit=8):
@@ -611,8 +665,10 @@
     side = 3 * deep + 2 * rows
     buffers = [
         pltpu.VMEM((x.shape[0], x.shape[2]), x.dtype)
-        for x, more in fields
-        for _ in range(2 * (1 + more))
+        for some in (fields[:5], fields[5:])
+        for _ in range(2)
+        for x, more in some
+        for _ in range(1 + more)
     ]
     near = pl.BlockSpec(memory_space=pltpu.HBM)
     first, last = pl.pallas_call(
@@ -620,10 +676,11 @@
         out_shape=(pltpu.VMEM((side, span), jnp.float32),) * 2,
         in_specs=[near] * len(fields) + [SMEM, SMEM],
         out_specs=(VMEM, VMEM),
-        scratch_shapes=buffers + [pltpu.SemaphoreType.DMA((len(buffers),))],
+        scratch_shapes=buffers
+        + [scratch(2, side, span), pltpu.SemaphoreType.DMA((len(buffers),))],
         compiler_params=pltpu.CompilerParams(vmem_limit_bytes=40 << 20),
     )(*far(*arrays, shear_table, viscosity_table))
-    left, right = swap(first, last, "gy")
+    beside_sides = swap_pairs(first, last, "gy")
     pause = pl.pallas_call(
         cover,
         out_shape=f32(8, 128),
@@ -654,11 +711,11 @@
         free,
         shear_table,
         viscosity_table,
-        left,
-        right,
+        *beside_sides,
+        scratch_shapes=[scratch(2, 3 * across + 2 * cols + 8, span)],
         tables=(7, 8),
     )
-    before, after = swap(first, last, "gx")
+    near_sides = swap_pairs(first, last, "gx")
     grid = (lax.axis_size("gx"), lax.axis_size("gy"))
     blocks = grid[0] * grid[1]
     capacity = max(2, deep // 2 * (across // 2) // blocks)
@@ -666,22 +723,27 @@
     room = 2 * capacity + 1
     chunk = -(-(room * parts + 1) // 8) * 8
     count = own_map.size
-    match, placed = pl.pallas_call(
+    match, ends, placed = pl.pallas_call(
         functools.partial(address, grid, (rows, cols), room, chunk),
-        out_shape=(f32(blocks * chunk, parts * count), f32(blocks * chunk, 128)),
+        out_shape=(
+            half(blocks * chunk, parts * count),
+            half(blocks * chunk, parts * across),
+            f32(blocks * chunk, 128),
+        ),
         in_specs=[VMEM, VMEM, pl.BlockSpec(memory_space=pl.ANY)],
-        out_specs=(VMEM, VMEM),
+        out_specs=(VMEM,) * 3,
         compiler_params=pltpu.CompilerParams(vmem_limit_bytes=16 << 20),
         cost_estimate=pl.CostEstimate(flops=10**8, bytes_accessed=10**7, transcendentals=0),
     )(own_map.T, slot_table.T, first)
     media = (pressure, courant, nonlinearity, absorption)
-    mid, new, lines = run(
+    mid, new, send = run(
         second_acoustic,
-        (block, block, f32(parts * count, 128)),
+        (block, block, f32(blocks * chunk, 128)),
         *media,
         mid,
-        left,
-        right,
+        match,
+        placed,
+        *beside_sides,
         scratch_shapes=[
             scratch(deep, span),
             scratch(deep, span),
@@ -693,14 +755,11 @@
         (hbm(2, across, span), hbm(4, across, span), hbm(blocks * chunk, 128)),
         *media,
         mid,
-        lines,
-        match,
-        placed,
-        before,
-        after,
-        left,
-        right,
-        scratch_shapes=[scratch(parts * count, 128), scratch(span // 128, across, 128)],
+        send,
+        ends,
+        *beside_sides,
+        *near_sides,
+        scratch_shapes=[scratch(span // 128, 2 * across, 128)],
     )
     send = send.reshape(blocks, chunk, 128)
     got = lax.all_to_all(send, ("gx", "gy"), split_axis=0, concat_axis=0, tiled=True)
@@ -710,7 +769,7 @@
         *far(mid, new, mids, news, free, displacement, displacement_prev, layer_labels),
         shear_table,
         viscosity_table,
-        *far(before, after, left, right),
+        *far(*beside_sides, *near_sides),
         scratch_shapes=[scratch(rows, depth)] * 4,
         tables=(8, 9),
         limit=24,

time: 53.7 us -> 48.4 us (0.901)
  starting transfers between devices: 18.2 us -> 14.8 us
  local copies, waits for them, and re-layouts: 1.77 us -> 0.11 us
  waiting for transfers between devices: 7.64 us -> 6.71 us
  Pallas kernels: 23.5 us -> 24.1 us
    all_to_all x1, starting transfers between devices: 9.02 us -> 4.66 us  [local(): lax.all_to_all(send, ('gx', 'gy'), split_axis=0, concat_axis=0, tiled=True)]
    unnamed x38, local copies, waits for them, and re-layouts: 1.77 us -> 0.11 us
    ppermute x4, starting transfers between devices: 9.14 us -> 10.2 us  [the longest x2 8.82 us: swap_pairs(): return (lax.ppermute(inner, axis, pairs(0)), outer)]
    ppermute x4, waiting for transfers between devices: 3.06 us -> 2.18 us  [the longest x2 2.17 us: swap_pairs(): return (lax.ppermute(inner, axis, pairs(0)), outer)]
    pallas_call x5, Pallas kernels: 16.2 us -> 16.7 us  [run(): pl.pallas_call(kernel, out_shape=out, in_specs=specs, out_specs=jax.tree....]
  transfers between devices with their start and end apart: 5 -> 5, of which waited for: 3 -> 2; matrix products, arithmetic and copies ran while one was open for 0% -> 0% of each run, Pallas kernels for 29% -> 33%
where the time goes in v5:
time: 48.4 us; the launch traced here: 48 us
  Pallas kernels  24.1 us (50%)
  starting transfers between devices  14.8 us (31%)
  waiting for transfers between devices  6.71 us (14%)
  between operations  1.59 us (3%)
  other arithmetic  0.69 us (1%)
    pallas_call x5, Pallas kernels, run(): pl.pallas_call(kernel, out_shape=out, in_specs=specs, out_specs=jax.tree....  16.7 us
    ppermute x2, starting transfers between devices, swap_pairs(): return (lax.ppermute(inner, axis, pairs(0)), outer)  8.82 us
    all_to_all x1, starting transfers between devices, local(): lax.all_to_all(send, ('gx', 'gy'), split_axis=0, concat_axis=0, tiled=True)  4.66 us
    all_to_all x1, waiting for transfers between devices, local(): lax.all_to_all(send, ('gx', 'gy'), split_axis=0, concat_axis=0, tiled=True)  4.53 us
    pallas_call x1, Pallas kernels, direct(): pl.pallas_call(functools.partial(land_and_step, room, chunk), out_shape=(...  3.01 us
    pallas_call x1, Pallas kernels, local(): pl.pallas_call(functools.partial(border_columns, inner), out_shape=(pltpu...  2.6 us
    ppermute x2, waiting for transfers between devices, swap_pairs(): return (lax.ppermute(inner, axis, pairs(0)), outer)  2.17 us
    pallas_call x1, Pallas kernels, local(): pl.pallas_call(functools.partial(address, grid, (rows, cols), room, chunk...  1.74 us
  transfers between devices with their start and end apart: 5, of which 2 were waited for; matrix products, arithmetic and copies ran while one was open for 0% of the time, Pallas kernels for 33%

profile of v5, /device:TPU:0, one launch (start us, length us, event | category | flops | bytes accessed | tf_op | source)
XLA Modules:
  0.0 48.0 jit_solution(6754659268721584371)
XLA Ops:
  0.6 2.6 %shard_map.155 = (f32[104,768]{1,0:T(8,128)S(1)}, f32[104,768]{1,0:T(8,128)S(1)}) custom-call(f32[24,16,768]{2,1,0:T(8,128)} %p_ref.7, f32[24,16,768]{2,1,0:T(8,128)} %q_ref.1, f32[24,16,768]{2,1,0:T(8,128)} %c_ref.7, f32[24,16,768]{2,1,0:T(8,128)} %n_ref.5, f32[24,16,768]{2,1,0:T(8,128)} %a_ref.5, f32[16,32,384]{2,1,0:T(8,128)} %d_ref.5, ...), custom_call_target="tpu_custom_call" | custom-call | tf_op jit(solution)/shard_map/pallas_call | solution.py:674
  3.2 0.7 %collective-permute-start.5 = (f32[104,768]{1,0:T(8,128)S(1)}, f32[104,768]{1,0:T(8,128)S(1)}, u32[]{:S(2)}, u32[]{:S(2)}) collective-permute-start(f32[104,768]{1,0:T(8,128)S(1)} %get-tuple-element.57), channel_id=1, source_target_pairs={{1,2},{2,1},{5,6},{6,5},{9,10},{10,9},{13,14},{14,13},{17,18},{18,... | collective-permute-start | bytes 958472 | tf_op jit(solution)/shard_map/ppermute | solution.py:615
  3.9 0.0 copy-start
  3.9 0.0 copy-start.1
  4.0 0.0 copy-start.2
  4.0 0.0 copy-start.3
  4.0 0.0 copy-start.6
  4.0 0.0 copy-start.9
  4.0 5.9 %collective-permute-start.4 = (f32[104,768]{1,0:T(8,128)S(1)}, f32[104,768]{1,0:T(8,128)S(1)}, u32[]{:S(2)}, u32[]{:S(2)}) collective-permute-start(f32[104,768]{1,0:T(8,128)S(1)} %get-tuple-element.54._), channel_id=1, source_target_pairs={{0,1},{1,0},{2,3},{3,2},{4,5},{5,4},{6,7},{7,6},{8,9},{9,8},{10,11... | collective-permute-start | bytes 958472 | tf_op jit(solution)/shard_map/ppermute | solution.py:616
  10.1 5.0 %shard_map.157 = (f32[24,16,768]{2,1,0:T(8,128)S(1)}, f32[16,32,384]{2,1,0:T(8,128)S(1)}) custom-call(f32[24,16,768]{2,1,0:T(8,128)S(1)} %copy-done, f32[24,16,768]{2,1,0:T(8,128)S(1)} %copy-done.9, f32[24,16,768]{2,1,0:T(8,128)S(1)} %copy-done.1, f32[24,16,768]{2,1,0:T(8,128)S(1)} %copy-done.2, f32[24,16,768]{2,1,0:T(8,128)S(1)} %copy-done.3, ...), custom_call_target="tpu_custom_call" | custom-call | flops 204554880 | bytes 10227744 | tf_op jit(solution)/shard_map/pallas_call | solution.py:644
  15.1 2.2 %collective-permute-done.4.beside_in = f32[104,768]{1,0:T(8,128)S(1)} collective-permute-done((f32[104,768]{1,0:T(8,128)S(1)}, f32[104,768]{1,0:T(8,128)S(1)}, u32[]{:S(2)}, u32[]{:S(2)}) %collective-permute-start.4) | collective-permute-done | bytes 319520 | tf_op jit(solution)/shard_map/ppermute | solution.py:616
  17.2 0.7 %shard_map.158 = (f32[120,768]{1,0:T(8,128)S(1)}, f32[120,768]{1,0:T(8,128)S(1)}) custom-call(f32[24,16,768]{2,1,0:T(8,128)S(1)} %copy-done, f32[24,16,768]{2,1,0:T(8,128)S(1)} %copy-done.1, f32[24,16,768]{2,1,0:T(8,128)S(1)} %get-tuple-element.55.mid_ref, f32[16,32,384]{2,1,0:T(8,128)S(1)} %copy-done.4, f32[16,32,384]{2,1,0:T(8,128)S(1)} %copy-done.5, ...), custom_call_target="tpu_custom_call" | custom-call | flops 161219200 | bytes 8060960 | tf_op jit(solution)/shard_map/pallas_call | solution.py:644
  18.0 0.7 %collective-permute-start.7 = (f32[120,768]{1,0:T(8,128)S(1)}, f32[120,768]{1,0:T(8,128)S(1)}, u32[]{:S(2)}, u32[]{:S(2)}) collective-permute-start(f32[120,768]{1,0:T(8,128)S(1)} %get-tuple-element.65), channel_id=1, source_target_pairs={{4,8},{8,4},{5,9},{9,5},{6,10},{10,6},{7,11},{11,7},{20,24},{24,20... | collective-permute-start | bytes 1105928 | tf_op jit(solution)/shard_map/ppermute | solution.py:615
  18.6 2.9 %collective-permute-start.6 = (f32[120,768]{1,0:T(8,128)S(1)}, f32[120,768]{1,0:T(8,128)S(1)}, u32[]{:S(2)}, u32[]{:S(2)}) collective-permute-start(f32[120,768]{1,0:T(8,128)S(1)} %get-tuple-element.58._), channel_id=1, source_target_pairs={{0,4},{4,0},{8,12},{12,8},{1,5},{5,1},{9,13},{13,9},{2,6},{6,2},{1... | collective-permute-start | bytes 1105928 | tf_op jit(solution)/shard_map/ppermute | solution.py:616
  21.5 1.7 %shard_map.159 = (bf16[640,288]{1,0:T(8,128)(2,1)S(1)}, bf16[640,48]{1,0:T(8,128)(2,1)S(1)}, f32[640,128]{1,0:T(8,128)S(1)}) custom-call(s32[8,12]{1,0:T(8,128)S(1)} %bitcast.14, s32[8,12]{1,0:T(8,128)S(1)} %bitcast.15, f32[120,768]{1,0:T(8,128)S(1)} %get-tuple-element.58._), custom_call_target="tpu_custom_call" | custom-call | flops 100000000 | bytes 10000000 | tf_op jit(solution)/shard_map/pallas_call | solution.py:726
  23.3 2.5 %shard_map.160 = (f32[24,16,768]{2,1,0:T(8,128)S(1)}, f32[24,16,768]{2,1,0:T(8,128)S(1)}, f32[640,128]{1,0:T(8,128)S(1)}) custom-call(f32[24,16,768]{2,1,0:T(8,128)S(1)} %copy-done, f32[24,16,768]{2,1,0:T(8,128)S(1)} %copy-done.1, f32[24,16,768]{2,1,0:T(8,128)S(1)} %copy-done.2, f32[24,16,768]{2,1,0:T(8,128)S(1)} %copy-done.3, ...), custom_call_target="tpu_custom_call" | custom-call | flops 205783040 | bytes 10289152 | tf_op jit(solution)/shard_map/pallas_call | solution.py:644
  25.8 0.0 copy-start.12
  25.9 1.8 %shard_map.161 = (f32[2,16,768]{2,1,0:T(8,128)}, f32[4,16,768]{2,1,0:T(8,128)}, f32[640,128]{1,0:T(8,128)}) custom-call(f32[24,16,768]{2,1,0:T(8,128)S(1)} %copy-done, f32[24,16,768]{2,1,0:T(8,128)S(1)} %copy-done.1, f32[24,16,768]{2,1,0:T(8,128)S(1)} %copy-done.2, f32[24,16,768]{2,1,0:T(8,128)S(1)} %copy-done.3, ...), custom_call_target="tpu_custom_call" | custom-call | flops 166952960 | bytes 8347648 | tf_op jit(solution)/shard_map/pallas_call | solution.py:644
  27.7 4.7 %all-to-all-start = ((f32[16,40,128]{2,1,0:T(8,128)}), f32[16,40,128]{2,1,0:T(8,128)S(1)}, u32[]{:S(2)}, u32[]{:S(2)}) async-start(f32[16,40,128]{2,1,0:T(8,128)} %bitcast.18), calls=%async_computation | async-start | bytes 655360 | tf_op jit(solution)/shard_map/all_to_all | solution.py:765
  32.3 6.8 %shard_map.162 = (f32[24,16,768]{2,1,0:T(8,128)}, f32[24,16,768]{2,1,0:T(8,128)}, f32[16,32,384]{2,1,0:T(8,128)S(1)}, f32[16,32,384]{2,1,0:T(8,128)S(1)}, f32[16,32,384]{2,1,0:T(8,128)S(1)}) custom-call(f32[24,16,768]{2,1,0:T(8,128)} %copy-done.10, f32[24,16,768]{2,1,0:T(8,128)} %copy-done.14, f32[2,16,768]{2,1,0:T(8,128)} %get-tuple-element.66.mids, ...), custom_call_target="tpu_custom_call" | custom-call | flops 237896320 | bytes 11894816 | tf_op jit(solution)/shard_map/pallas_call | solution.py:644
  39.1 4.5 %all-to-all-done = f32[16,40,128]{2,1,0:T(8,128)S(1)} async-done(((f32[16,40,128]{2,1,0:T(8,128)}), f32[16,40,128]{2,1,0:T(8,128)S(1)}, u32[]{:S(2)}, u32[]{:S(2)}) %all-to-all-start) | async-done | bytes 327712 | tf_op jit(solution)/shard_map/all_to_all | solution.py:765
  43.7 0.7 %slice_reduce_fusion = f32[]{:T(128)} fusion(f32[16,40,128]{2,1,0:T(8,128)S(1)} %all-to-all-done), kind=kLoop, calls=%fused_computation.4 | loop fusion | flops 15 | bytes 68 | tf_op jit(solution)/shard_map/reduce_max | solution.py:808
  45.0 3.0 %conditional.1 = ((f32[16,32,384]{2,1,0:T(8,128)}, f32[16,32,384]{2,1,0:T(8,128)}, f32[16,32,384]{2,1,0:T(8,128)})) conditional(s32[]{:T(128)} %convert_element_type.3, (f32[640,128]{1,0:T(8,128)S(1)}, f32[16,32,384]{2,1,0:T(8,128)S(1)}, f32[16,32,384]{2,1,0:T(8,128)S(1)}, f32[16,32,384]{2,1,0:T(8,128)S(1)}) %tuple.23, (f32[640,128]{1,0:T(8,128)S(1)}, ...), branch_computations={%region_1.0_spmd, %region_2.0_spmd} | conditional | flops 119603200 | bytes 10109148 | solution.py:807
  45.0 3.0 %branch_0_fun.1 = (f32[16,32,384]{2,1,0:T(8,128)}, f32[16,32,384]{2,1,0:T(8,128)}, f32[16,32,384]{2,1,0:T(8,128)}) custom-call(f32[640,128]{1,0:T(8,128)S(1)} %get-tuple-element.16.got_ref, f32[16,32,384]{2,1,0:T(8,128)S(1)} %get-tuple-element.17.free, f32[16,32,384]{2,1,0:T(8,128)S(1)} %get-tuple-element.18.after_free, ...), custom_call_target="tpu_custom_call" | custom-call | tf_op jit(solution)/shard_map/cond/branch_0_fun/pallas_call | solution.py:783
  (35 shorter events, 0.1 us)
Async XLA Ops:
  3.2 11.8 %collective-permute-start.5 = (f32[104,768]{1,0:T(8,128)S(1)}, f32[104,768]{1,0:T(8,128)S(1)}, u32[]{:S(2)}, u32[]{:S(2)}) collective-permute-start(f32[104,768]{1,0:T(8,128)S(1)} %get-tuple-element.57), channel_id=1, source_target_pairs={{1,2},{2,1},{5,6},{6,5},{9,10},{10,9},{13,14},{14,13},{17,18},{18,... | collective-permute-start | bytes 958472 | tf_op jit(solution)/shard_map/ppermute | solution.py:615
  3.9 6.0 %copy-start = (f32[24,16,768]{2,1,0:T(8,128)S(1)}, f32[24,16,768]{2,1,0:T(8,128)}, u32[]{:S(2)}) copy-start(f32[24,16,768]{2,1,0:T(8,128)} %p_ref.7) | copy-start | bytes 3538948
  3.9 6.0 %copy-start.1 = (f32[24,16,768]{2,1,0:T(8,128)S(1)}, f32[24,16,768]{2,1,0:T(8,128)}, u32[]{:S(2)}) copy-start(f32[24,16,768]{2,1,0:T(8,128)} %c_ref.7) | copy-start | bytes 3538948
  4.0 6.0 %copy-start.2 = (f32[24,16,768]{2,1,0:T(8,128)S(1)}, f32[24,16,768]{2,1,0:T(8,128)}, u32[]{:S(2)}) copy-start(f32[24,16,768]{2,1,0:T(8,128)} %n_ref.5) | copy-start | bytes 3538948
  4.0 6.0 %copy-start.3 = (f32[24,16,768]{2,1,0:T(8,128)S(1)}, f32[24,16,768]{2,1,0:T(8,128)}, u32[]{:S(2)}) copy-start(f32[24,16,768]{2,1,0:T(8,128)} %a_ref.5) | copy-start | bytes 3538948
  4.0 6.0 %copy-start.4 = (f32[16,32,384]{2,1,0:T(8,128)S(1)}, f32[16,32,384]{2,1,0:T(8,128)}, u32[]{:S(2)}) copy-start(f32[16,32,384]{2,1,0:T(8,128)} %d_ref.5) | copy-start | bytes 2359300
  4.0 6.0 %copy-start.5 = (f32[16,32,384]{2,1,0:T(8,128)S(1)}, f32[16,32,384]{2,1,0:T(8,128)}, u32[]{:S(2)}) copy-start(f32[16,32,384]{2,1,0:T(8,128)} %b_ref.5) | copy-start | bytes 2359300
  4.0 6.0 %copy-start.6 = (s32[16,32,384]{2,1,0:T(8,128)S(1)}, s32[16,32,384]{2,1,0:T(8,128)}, u32[]{:S(2)}) copy-start(s32[16,32,384]{2,1,0:T(8,128)} %l_ref.5) | copy-start | bytes 2359300
  4.0 6.0 %copy-start.9 = (f32[24,16,768]{2,1,0:T(8,128)S(1)}, f32[24,16,768]{2,1,0:T(8,128)}, u32[]{:S(2)}) copy-start(f32[24,16,768]{2,1,0:T(8,128)} %q_ref.1) | copy-start | bytes 3538948
  4.0 6.0 %copy-start.15 = (f32[4]{0:T(128)S(1)}, f32[4]{0:T(128)}, u32[]{:S(2)}) copy-start(f32[4]{0:T(128)} %shear.5) | copy-start | bytes 52
  4.0 6.0 %copy-start.16 = (f32[4]{0:T(128)S(1)}, f32[4]{0:T(128)}, u32[]{:S(2)}) copy-start(f32[4]{0:T(128)} %viscosity.5) | copy-start | bytes 52
  4.0 13.2 %collective-permute-start.4 = (f32[104,768]{1,0:T(8,128)S(1)}, f32[104,768]{1,0:T(8,128)S(1)}, u32[]{:S(2)}, u32[]{:S(2)}) collective-permute-start(f32[104,768]{1,0:T(8,128)S(1)} %get-tuple-element.54._), channel_id=1, source_target_pairs={{0,1},{1,0},{2,3},{3,2},{4,5},{5,4},{6,7},{7,6},{8,9},{9,8},{10,11... | collective-permute-start | bytes 958472 | tf_op jit(solution)/shard_map/ppermute | solution.py:616
  15.0 2.9 %copy-start.11 = (f32[16,32,384]{2,1,0:T(8,128)}, f32[16,32,384]{2,1,0:T(8,128)S(1)}, u32[]{:S(2)}) copy-start(f32[16,32,384]{2,1,0:T(8,128)S(1)} %get-tuple-element.56.free_ref) | copy-start | bytes 2359300
  15.0 10.8 %copy-start.7 = (f32[104,768]{1,0:T(8,128)}, f32[104,768]{1,0:T(8,128)S(1)}, u32[]{:S(2)}) copy-start(f32[104,768]{1,0:T(8,128)S(1)} %collective-permute-done.5.beside_out) | copy-start | bytes 958468
  17.2 8.6 %copy-start.8 = (f32[104,768]{1,0:T(8,128)}, f32[104,768]{1,0:T(8,128)S(1)}, u32[]{:S(2)}) copy-start(f32[104,768]{1,0:T(8,128)S(1)} %collective-permute-done.4.beside_in) | copy-start | bytes 958468
  17.2 4.3 %copy-start.17 = (s32[12,8]{0,1:T(8,128)S(1)}, s32[12,8]{0,1:T(8,128)}, u32[]{:S(2)}) copy-start(s32[12,8]{0,1:T(8,128)} %param.19) | copy-start | bytes 1156
  17.2 4.3 %copy-start.18 = (s32[12,8]{0,1:T(8,128)S(1)}, s32[12,8]{0,1:T(8,128)}, u32[]{:S(2)}) copy-start(s32[12,8]{0,1:T(8,128)} %param.20) | copy-start | bytes 1156
  18.0 7.8 %collective-permute-start.7 = (f32[120,768]{1,0:T(8,128)S(1)}, f32[120,768]{1,0:T(8,128)S(1)}, u32[]{:S(2)}, u32[]{:S(2)}) collective-permute-start(f32[120,768]{1,0:T(8,128)S(1)} %get-tuple-element.65), channel_id=1, source_target_pairs={{4,8},{8,4},{5,9},{9,5},{6,10},{10,6},{7,11},{11,7},{20,24},{24,20... | collective-permute-start | bytes 1105928 | tf_op jit(solution)/shard_map/ppermute | solution.py:615
  18.6 7.2 %collective-permute-start.6 = (f32[120,768]{1,0:T(8,128)S(1)}, f32[120,768]{1,0:T(8,128)S(1)}, u32[]{:S(2)}, u32[]{:S(2)}) collective-permute-start(f32[120,768]{1,0:T(8,128)S(1)} %get-tuple-element.58._), channel_id=1, source_target_pairs={{0,4},{4,0},{8,12},{12,8},{1,5},{5,1},{9,13},{13,9},{2,6},{6,2},{1... | collective-permute-start | bytes 1105928 | tf_op jit(solution)/shard_map/ppermute | solution.py:616
  25.8 1.9 %copy-start.10 = (f32[24,16,768]{2,1,0:T(8,128)}, f32[24,16,768]{2,1,0:T(8,128)S(1)}, u32[]{:S(2)}) copy-start(f32[24,16,768]{2,1,0:T(8,128)S(1)} %get-tuple-element.61.mid_ref) | copy-start | bytes 3538948
  25.8 1.9 %copy-start.14 = (f32[24,16,768]{2,1,0:T(8,128)}, f32[24,16,768]{2,1,0:T(8,128)S(1)}, u32[]{:S(2)}) copy-start(f32[24,16,768]{2,1,0:T(8,128)S(1)} %get-tuple-element.62.new_ref) | copy-start | bytes 3538948
  25.8 1.8 %copy-start.12 = (f32[120,768]{1,0:T(8,128)}, f32[120,768]{1,0:T(8,128)S(1)}, u32[]{:S(2)}) copy-start(f32[120,768]{1,0:T(8,128)S(1)} %collective-permute-done.7.near_out) | copy-start | bytes 1105924
  25.8 1.8 %copy-start.13 = (f32[120,768]{1,0:T(8,128)}, f32[120,768]{1,0:T(8,128)S(1)}, u32[]{:S(2)}) copy-start(f32[120,768]{1,0:T(8,128)S(1)} %collective-permute-done.6.near_in) | copy-start | bytes 1105924
  27.7 16.0 %all-to-all-start = ((f32[16,40,128]{2,1,0:T(8,128)}), f32[16,40,128]{2,1,0:T(8,128)S(1)}, u32[]{:S(2)}, u32[]{:S(2)}) async-start(f32[16,40,128]{2,1,0:T(8,128)} %bitcast.18), calls=%async_computation | async-start | bytes 655360 | tf_op jit(solution)/shard_map/all_to_all | solution.py:765
